TPU v7x, 32 devices: a whole 2x2x4 slice. The times are simulated.
32 devices in a mesh: fsdp: 8 (over z, x), tp: 4 (over y, core).
Axes of the slice: x: 2, y: 2, z: 4, core: 2. Of those that a mesh axis runs over, the one named last changes fastest.
Arguments:
- tokens: bfloat16 [4096, 2048], P(('fsdp', 'tp')), may hold values from -6 to 6
- seg_ids: int32 [8, 512], P('fsdp'), may hold values from 0 to 5, never falling along the last dimension, each value on 1 to 384 neighbouring positions
- pad_mask: int32 [8, 512], P('fsdp'), may hold values from 0 to 1, as said below
- expert_ids: int32 [4096, 8], P('fsdp'), may hold values from 0 to 15, all different within a row; in each aligned block of 512 rows (0 to 511, 512 to 1023, ...) at most 264 rows name the same one
- w_qkv: bfloat16 [3, 2048, 2048], P(None, 'fsdp', 'tp'), may hold values from -0.125 to 0.125
- w_out: bfloat16 [2048, 2048], P('tp', 'fsdp'), may hold values from -1 to 1
- w_router: bfloat16 [2048, 16], P(('fsdp', 'tp')), may hold values from -0.0625 to 0.0625
- norm_gains: bfloat16 [4, 2048], P(None, ('fsdp', 'tp')), may hold values from 0.25 to 1.75
- w_gate: bfloat16 [16, 2048, 1024], P('fsdp', None, 'tp'), may hold values from -0.125 to 0.125
- w_up: bfloat16 [16, 2048, 1024], P('fsdp', None, 'tp'), may hold values from -0.125 to 0.125
- w_down: bfloat16 [16, 1024, 2048], P('fsdp', 'tp'), may hold values from -4 to 4
- cotangent: bfloat16 [4096, 2048], P(('fsdp', 'tp')), may hold values from -6 to 6
Outputs:
- layer_out: bfloat16 [4096, 2048], P(('fsdp', 'tp'))
- input_grad: float32 [4096, 2048], P(('fsdp', 'tp'))
- grad_qkv: float32 [3, 2048, 2048], P(None, 'fsdp', 'tp')
- grad_out: float32 [2048, 2048], P('tp', 'fsdp')
- grad_router: float32 [2048, 16], P(('fsdp', 'tp'))
- grad_gains: float32 [4, 2048], P(None, ('fsdp', 'tp'))
- grad_gate: float32 [16, 2048, 1024], P('fsdp', None, 'tp')
- grad_up: float32 [16, 2048, 1024], P('fsdp', None, 'tp')
- grad_down: float32 [16, 1024, 2048], P('fsdp', 'tp')
Inputs may be any that keep to these rules, and one draw needn't show every extreme that they name: `expert_ids`: in the 512 rows of each sequence every row names 8 different experts, no expert is named by more than 264 rows, a bound that some block reaches. `seg_ids`: within a sequence the document numbers never fall. `pad_mask`: in each sequence the real tokens come first and padding tokens follow.
All inputs are finite; a program needn't handle non-finite values.
Results may differ from a plain program's by a relative error of at most 0.025.
Values may be sent and summed in bfloat16 or wider, within the bound.
No kernel may reach another device: no remote copies, remote signals or barrier semaphores. Data moves between devices by JAX's collectives and lax.ppermute only.
A program may use at most 384 MiB of HBM per device.

v0:
```python
import jax
import jax.numpy as jnp
from jax import lax
from jax.sharding import PartitionSpec as P

HD = 128


EPSILON = 1e-05
NEG_FILL = -1e30


def route_slots(expert_ids, n_experts, capacity):
    seq_len, top_count = expert_ids.shape
    experts = jnp.arange(n_experts, dtype=jnp.int32)
    counts = jnp.sum((expert_ids[:, :, None] == experts[None, None, :]).astype(jnp.int32), axis=1)
    earlier = jnp.cumsum(counts, axis=0) - counts
    slot_rank = jnp.take_along_axis(earlier, expert_ids, axis=1)
    flat_index = expert_ids * capacity + slot_rank
    token_index = jnp.broadcast_to(
        jnp.arange(seq_len, dtype=jnp.int32)[:, None], (seq_len, top_count)
    )
    source = jnp.full((n_experts * capacity,), seq_len, jnp.int32)
    source = source.at[flat_index.reshape(-1)].set(token_index.reshape(-1))
    return (flat_index, source)


def rope_tables(seq_len, head_size):
    half_size = head_size // 2
    inverse = 10000.0 ** (-2.0 * jnp.arange(half_size, dtype=jnp.float32) / head_size)
    angles = jnp.arange(seq_len, dtype=jnp.float32)[:, None] * inverse[None, :]
    return (jnp.cos(angles)[:, None, :], jnp.sin(angles)[:, None, :])


def rotate(values, cosine, sine):
    half_size = values.shape[-1] // 2
    first = values[..., :half_size]
    second = values[..., half_size:]
    return jnp.concatenate(
        [first * cosine - second * sine, second * cosine + first * sine], axis=-1
    )


def rotate_back(grads, cosine, sine):
    half_size = grads.shape[-1] // 2
    first = grads[..., :half_size]
    second = grads[..., half_size:]
    return jnp.concatenate(
        [first * cosine + second * sine, second * cosine - first * sine], axis=-1
    )


def allowed_mask(segment, padding, row_start, row_count):
    row_index = row_start + jnp.arange(row_count, dtype=jnp.int32)
    col_index = jnp.arange(segment.shape[0], dtype=jnp.int32)
    same_doc = segment[:, None] == segment[None, :]
    causal = col_index[None, :] <= row_index[:, None]
    usable = (padding[None, :] == 1) | (col_index[None, :] == row_index[:, None])
    return same_doc & causal & usable


def norm_forward(values, gain):
    scale = lax.rsqrt(jnp.mean(values * values, axis=-1, keepdims=True) + EPSILON)
    return (values * scale * gain, scale)


def norm_backward(values, scale, gain, grads):
    unit = values * scale
    gain_grad = jnp.sum(grads * unit, axis=0)
    scaled = grads * gain
    return (scale * (scaled - unit * jnp.mean(scaled * unit, axis=-1, keepdims=True)), gain_grad)


def gather_rows(values):
    return lax.all_gather(values, "tp", axis=0, tiled=True)


def scatter_rows(values):
    return lax.psum_scatter(
        values.astype(jnp.bfloat16), "tp", scatter_dimension=0, tiled=True
    ).astype(jnp.float32)


def tp_totals(first, second):
    return lax.psum((first, second), "tp")


def shards(
    tokens,
    seg_ids,
    pad_mask,
    expert_ids,
    w_qkv,
    w_out,
    w_router,
    norm_gains,
    w_gate,
    w_up,
    w_down,
    cotangent,
):
    tp_rank = lax.axis_index("tp")
    fsdp_count = lax.axis_size("fsdp")
    local_rows, width = tokens.shape
    seq_len = seg_ids.shape[1]
    exp_local = w_gate.shape[0]
    ff_local = w_gate.shape[2]
    n_experts = exp_local * fsdp_count
    top_count = expert_ids.shape[1]
    capacity = (seq_len * top_count * 33 + 32 * n_experts - 1) // (32 * n_experts)
    head_cols = w_qkv.shape[2]
    heads_local = head_cols // HD
    block_rows = min(512, seq_len)
    n_blocks = seq_len // block_rows
    score_scale = HD ** (-0.5)

    def send_experts(buffer):
        return lax.all_to_all(buffer, "fsdp", split_axis=0, concat_axis=1, tiled=True)

    def return_experts(buffer):
        back = lax.all_to_all(buffer, "fsdp", split_axis=1, concat_axis=0, tiled=True)
        return back.reshape(n_experts * capacity, back.shape[2])

    qkv_full, out_full = (
        lax.all_gather(w_qkv, "fsdp", axis=1, tiled=True),
        lax.all_gather(w_out, "fsdp", axis=1, tiled=True),
    )
    router_full, gains_full = (
        lax.all_gather(w_router, ("fsdp", "tp"), axis=0, tiled=True),
        lax.all_gather(norm_gains, ("fsdp", "tp"), axis=1, tiled=True),
    )
    gains_wide = gains_full.astype(jnp.float32)
    col_start = tp_rank * head_cols
    gain_query = lax.dynamic_slice_in_dim(gains_wide[2], col_start, head_cols)
    gain_key = lax.dynamic_slice_in_dim(gains_wide[3], col_start, head_cols)
    segment = seg_ids[0]
    padding = pad_mask[0]
    cosine, sine = rope_tables(seq_len, HD)
    x_own = tokens.astype(jnp.float32)
    normed1, scale1 = norm_forward(x_own, gains_wide[0])
    rows1 = gather_rows(normed1.astype(jnp.bfloat16))
    projected = jnp.einsum("sd,cdh->csh", rows1, qkv_full, preferred_element_type=jnp.float32)
    query_raw = projected[0]
    key_raw = projected[1]
    square_q, square_k = tp_totals(
        jnp.sum(query_raw * query_raw, axis=-1), jnp.sum(key_raw * key_raw, axis=-1)
    )
    scale_q = lax.rsqrt(square_q / width + EPSILON)[:, None]
    scale_k = lax.rsqrt(square_k / width + EPSILON)[:, None]
    unit_q = query_raw * scale_q
    unit_k = key_raw * scale_k
    queries = rotate((unit_q * gain_query).reshape(seq_len, heads_local, HD), cosine, sine).astype(
        jnp.bfloat16
    )
    keys = rotate((unit_k * gain_key).reshape(seq_len, heads_local, HD), cosine, sine).astype(
        jnp.bfloat16
    )
    values = projected[2].astype(jnp.bfloat16).reshape(seq_len, heads_local, HD)
    block_starts = jnp.arange(n_blocks, dtype=jnp.int32) * block_rows

    def block_scores(start):
        raw_scores = (
            jnp.einsum("qhd,khd->hqk", queries, keys, preferred_element_type=jnp.float32)
            * score_scale
        )
        allowed = allowed_mask(segment, padding, start, block_rows)
        return (queries, jnp.where(allowed[None], raw_scores, NEG_FILL), allowed)

    def attend(start):
        query_block, scores, allowed = block_scores(start)
        peak = jnp.max(scores, axis=-1, keepdims=True)
        powered = jnp.exp(scores - peak)
        total = jnp.sum(powered, axis=-1, keepdims=True)
        probs_low = (powered / total).astype(jnp.bfloat16)
        mixed_block = jnp.einsum(
            "hqk,khd->qhd", probs_low, values, preferred_element_type=jnp.float32
        )
        return (
            mixed_block.reshape(block_rows, head_cols).astype(jnp.bfloat16),
            (peak + jnp.log(total))[..., 0],
        )

    mixed_blocks, log_sums = lax.map(attend, block_starts)
    mixed = mixed_blocks.reshape(seq_len, head_cols)
    hidden = x_own + scatter_rows(jnp.dot(mixed, out_full, preferred_element_type=jnp.float32))
    normed2, scale2 = norm_forward(hidden, gains_wide[1])
    own_normed2 = normed2.astype(jnp.bfloat16)
    rows2 = gather_rows(own_normed2)
    logits = jnp.dot(rows2, router_full, preferred_element_type=jnp.float32)
    router_probs = jax.nn.softmax(logits, axis=-1)
    gates = jnp.take_along_axis(router_probs, expert_ids, axis=1)
    flat_index, source = route_slots(expert_ids, n_experts, capacity)
    padded_rows = jnp.concatenate([rows2, jnp.zeros((1, width), jnp.bfloat16)], axis=0)
    received = send_experts(padded_rows[source].reshape(n_experts, capacity, width))
    w_pair = jnp.concatenate([w_gate, w_up], axis=2)
    pair_pre = jnp.einsum("erd,edf->erf", received, w_pair, preferred_element_type=jnp.float32)
    gate_pre = pair_pre[..., :ff_local]
    up_pre = pair_pre[..., ff_local:]
    sigmoid_gate = jax.nn.sigmoid(gate_pre)
    silu_gate = gate_pre * sigmoid_gate
    active = (silu_gate * up_pre).astype(jnp.bfloat16)
    expert_part = jnp.einsum(
        "erf,efd->erd", active, w_down, preferred_element_type=jnp.float32
    ).astype(jnp.bfloat16)
    returned = return_experts(expert_part)
    combined = jnp.zeros((seq_len, returned.shape[1]), jnp.float32)
    for pick_rank in range(top_count):
        combined = combined + gates[:, pick_rank : pick_rank + 1] * returned[
            flat_index[:, pick_rank]
        ].astype(jnp.float32)
    layer_out = (hidden + scatter_rows(combined)).astype(jnp.bfloat16)
    grad_rows = gather_rows(cotangent)
    grad_cols = grad_rows.astype(jnp.float32)
    partial_dots = jnp.stack(
        [
            jnp.sum(returned[flat_index[:, pick_rank]].astype(jnp.float32) * grad_cols, axis=-1)
            for pick_rank in range(top_count)
        ],
        axis=1,
    )
    gate_dots = lax.psum(partial_dots, "tp")
    expert_range = jnp.arange(n_experts, dtype=jnp.int32)
    chosen = jnp.sum(
        gate_dots[:, :, None]
        * (expert_ids[:, :, None] == expert_range[None, None, :]).astype(jnp.float32),
        axis=1,
    )
    weighted = jnp.sum(gates * gate_dots, axis=-1, keepdims=True)
    logit_grad = (router_probs * (chosen - weighted)).astype(jnp.bfloat16)
    own_logit_grad = lax.dynamic_slice_in_dim(logit_grad, tp_rank * local_rows, local_rows, 0)
    slot_gates = (
        jnp.zeros((n_experts * capacity,), jnp.float32)
        .at[flat_index.reshape(-1)]
        .set(gates.reshape(-1))
    )
    padded_grads = jnp.concatenate([grad_rows, jnp.zeros((1, width), jnp.bfloat16)], axis=0)
    slot_grads = (padded_grads[source].astype(jnp.float32) * slot_gates[:, None]).astype(
        jnp.bfloat16
    )
    grad_received = send_experts(slot_grads.reshape(n_experts, capacity, width))
    active_grad = jnp.einsum(
        "erd,efd->erf", grad_received, w_down, preferred_element_type=jnp.float32
    )
    gate_grad = (
        active_grad * up_pre * sigmoid_gate * (1.0 + gate_pre * (1.0 - sigmoid_gate))
    ).astype(jnp.bfloat16)
    up_grad = (active_grad * silu_gate).astype(jnp.bfloat16)
    pair_grad = jnp.concatenate([gate_grad, up_grad], axis=2)
    grad_down = jnp.einsum(
        "erf,erd->efd", active, grad_received, preferred_element_type=jnp.float32
    )
    grad_pair = jnp.einsum("erd,erf->edf", received, pair_grad, preferred_element_type=jnp.float32)
    grad_gate = grad_pair[..., :ff_local]
    grad_up = grad_pair[..., ff_local:]
    input_part = jnp.einsum(
        "erf,edf->erd", pair_grad, w_pair, preferred_element_type=jnp.float32
    ).astype(jnp.bfloat16)
    sent_back = return_experts(input_part)
    token_grad = jnp.zeros((seq_len, sent_back.shape[1]), jnp.float32)
    for pick_rank in range(top_count):
        token_grad = token_grad + sent_back[flat_index[:, pick_rank]].astype(jnp.float32)
    normed2_grad = scatter_rows(token_grad) + jnp.dot(
        own_logit_grad, router_full.T, preferred_element_type=jnp.float32
    )
    hidden_norm_grad, gain2_grad = norm_backward(hidden, scale2, gains_wide[1], normed2_grad)
    hidden_grad = cotangent.astype(jnp.float32) + hidden_norm_grad
    router_grad = jnp.dot(own_normed2.T, own_logit_grad, preferred_element_type=jnp.float32)
    hidden_rows = gather_rows(hidden_grad.astype(jnp.bfloat16))
    grad_out_full = jnp.dot(mixed.T, hidden_rows, preferred_element_type=jnp.float32)
    mixed_grad = (
        jnp.dot(hidden_rows, out_full.T, preferred_element_type=jnp.float32)
        .astype(jnp.bfloat16)
        .reshape(seq_len, heads_local, HD)
    )

    def attend_back(carried, pieces):
        key_acc, value_acc = carried
        start, log_sum = pieces
        query_block, scores, allowed = block_scores(start)
        probs = jnp.where(allowed[None], jnp.exp(scores - log_sum[:, :, None]), 0.0)
        prob_grad = jnp.einsum(
            "qhd,khd->hqk", mixed_grad, values, preferred_element_type=jnp.float32
        )
        delta = jnp.sum(probs * prob_grad, axis=-1, keepdims=True)
        score_grad = (probs * (prob_grad - delta)).astype(jnp.bfloat16)
        query_block_grad = (
            jnp.einsum("hqk,khd->qhd", score_grad, keys, preferred_element_type=jnp.float32)
            * score_scale
        )
        key_acc = (
            key_acc
            + jnp.einsum(
                "hqk,qhd->khd", score_grad, query_block, preferred_element_type=jnp.float32
            )
            * score_scale
        )
        value_acc = value_acc + jnp.einsum(
            "hqk,qhd->khd",
            probs.astype(jnp.bfloat16),
            mixed_grad,
            preferred_element_type=jnp.float32,
        )
        return ((key_acc, value_acc), query_block_grad)

    zero_heads = jnp.zeros((seq_len, heads_local, HD), jnp.float32)
    (key_grad, value_grad), query_blocks = lax.scan(
        attend_back, (zero_heads, zero_heads), (block_starts, log_sums)
    )
    query_grad = query_blocks.reshape(seq_len, heads_local, HD)
    query_norm_grad = rotate_back(query_grad, cosine, sine).reshape(seq_len, head_cols)
    key_norm_grad = rotate_back(key_grad, cosine, sine).reshape(seq_len, head_cols)
    gain_query_grad = jnp.sum(query_norm_grad * unit_q, axis=0)
    gain_key_grad = jnp.sum(key_norm_grad * unit_k, axis=0)
    scaled_q = query_norm_grad * gain_query
    scaled_k = key_norm_grad * gain_key
    inner_q, inner_k = tp_totals(
        jnp.sum(scaled_q * unit_q, axis=-1), jnp.sum(scaled_k * unit_k, axis=-1)
    )
    query_raw_grad = scale_q * (scaled_q - unit_q * (inner_q / width)[:, None])
    key_raw_grad = scale_k * (scaled_k - unit_k * (inner_k / width)[:, None])
    qkv_grad = jnp.stack(
        [query_raw_grad, key_raw_grad, value_grad.reshape(seq_len, head_cols)]
    ).astype(jnp.bfloat16)
    grad_qkv_full = jnp.einsum("sd,csh->cdh", rows1, qkv_grad, preferred_element_type=jnp.float32)
    normed1_part = jnp.einsum("csh,cdh->sd", qkv_grad, qkv_full, preferred_element_type=jnp.float32)
    normed1_grad = scatter_rows(normed1_part)
    input_norm_grad, gain1_grad = norm_backward(x_own, scale1, gains_wide[0], normed1_grad)
    input_grad = hidden_grad + input_norm_grad
    zero_width = jnp.zeros((width,), jnp.float32)
    gains_grad = jnp.stack(
        [
            gain1_grad,
            gain2_grad,
            lax.dynamic_update_slice_in_dim(zero_width, gain_query_grad, col_start, 0),
            lax.dynamic_update_slice_in_dim(zero_width, gain_key_grad, col_start, 0),
        ]
    )
    grad_qkv, grad_out = (
        lax.psum_scatter(
            grad_qkv_full.astype(jnp.bfloat16), "fsdp", scatter_dimension=1, tiled=True
        ).astype(jnp.float32),
        lax.psum_scatter(
            grad_out_full.astype(jnp.bfloat16), "fsdp", scatter_dimension=1, tiled=True
        ).astype(jnp.float32),
    )
    grad_router, grad_gains = (
        lax.psum_scatter(router_grad, ("fsdp", "tp"), scatter_dimension=0, tiled=True),
        lax.psum_scatter(gains_grad, ("fsdp", "tp"), scatter_dimension=1, tiled=True),
    )
    return (
        layer_out,
        input_grad,
        grad_qkv,
        grad_out,
        grad_router,
        grad_gains,
        grad_gate,
        grad_up,
        grad_down,
    )


def solution(mesh):
    placed = (
        P(("fsdp", "tp"), None),
        P("fsdp", None),
        P("fsdp", None),
        P("fsdp", None),
        P(None, "fsdp", "tp"),
        P("tp", "fsdp"),
        P(("fsdp", "tp"), None),
        P(None, ("fsdp", "tp")),
        P("fsdp", None, "tp"),
        P("fsdp", None, "tp"),
        P("fsdp", "tp", None),
        P(("fsdp", "tp"), None),
    )
    return jax.shard_map(
        shards,
        mesh=mesh,
        in_specs=placed,
        out_specs=(
            P(("fsdp", "tp"), None),
            P(("fsdp", "tp"), None),
            P(None, "fsdp", "tp"),
            P("tp", "fsdp"),
            P(("fsdp", "tp"), None),
            P(None, ("fsdp", "tp")),
            P("fsdp", None, "tp"),
            P("fsdp", None, "tp"),
            P("fsdp", "tp", None),
        ),
        check_vma=False,
    )
```

profile of v0, /device:TPU:9, one launch (start us, length us, event | category | flops | bytes accessed | tf_op | source)
XLA Modules:
  0.0 3051.8 jit_solution(12842548354509482896)
XLA Ops:
  7.3 36.3 %all-gather = bf16[32,64,4]{1,2,0:T(4,128)(2,1)S(1)} all-gather(bf16[1,64,4]{1,2,0:T(4,128)(2,1)} %bitcast.232), channel_id=1, replica_groups=mesh['fsdp'=8,'tp'=4] {'fsdp','tp'}, dimensions={0}, use_global_device_ids=true | all-gather | bytes 16896 | tf_op jit(solution)/shard_map/all_gather | solution.py:130
  52.2 19.8 all-gather.9.cloned.1.call-done
  72.1 99.9 %all-gather.11.cloned.1.call-done = bf16[3,2048,512]{1,2,0:T(8,128)(2,1)} async-done(((bf16[3,256,512]{1,2,0:T(8,128)(2,1)}), bf16[3,2048,512]{1,2,0:T(8,128)(2,1)}) %all-gather.11.cloned.1.call-update) | async-done | bytes 6291472 | tf_op jit(solution)/shard_map/all_gather | solution.py:125
  200.8 22.5 all-gather.13.cloned.1.call-done
  228.0 31.7 %reduce-scatter.13.cloned.1.call-done = bf16[128,2048]{1,0:T(8,128)(2,1)} async-done(((bf16[512,2048]{1,0:T(8,128)(2,1)}), bf16[128,2048]{1,0:T(8,128)(2,1)}) %reduce-scatter.13.cloned.1.call-update) | async-done | bytes 524304 | tf_op jit(solution)/shard_map/reduce_scatter | solution.py:79
  265.4 26.7 gather_fusion.19
  312.3 35.0 %gather_fusion = bf16[4224,2048]{1,0:T(8,128)(2,1)} fusion(bf16[513,2048]{1,0:T(8,128)(2,1)} %concatenate.28, s32[5120]{0:T(1024)S(1)} %pad_clamp_fusion), kind=kCustom, calls=%fused_computation | custom fusion | bytes 34619904 | tf_op jit(solution)/shard_map/gather | solution.py:194
  357.8 367.7 %all-to-all-done = bf16[16,264,2048]{2,1,0:T(8,128)(2,1)} async-done(((bf16[16,264,2048]{2,1,0:T(8,128)(2,1)}), bf16[16,264,2048]{2,1,0:T(8,128)(2,1)}, u32[]{:S(2)}, u32[]{:S(2)}) %all-to-all-start) | async-done | bytes 17301536 | tf_op jit(solution)/shard_map/all_to_all | solution.py:118
  764.7 31.9 %copy.216 = bf16[2,2112,2048]{2,0,1:T(2,128)(2,1)} copy(bf16[2,2112,2048]{2,1,0:T(8,128)(2,1)} %convolution_convert_fusion) | data formatting | bytes 34603008 | tf_op jit(solution)/shard_map/convert_element_type | solution.py:204
  804.3 397.2 %all-gather.1 = bf16[32,64,16]{1,2,0:T(8,128)(2,1)S(1)} all-gather(bf16[1,64,16]{1,2,0:T(8,128)(2,1)S(1)} %bitcast.231), channel_id=1, replica_groups=mesh['fsdp'=8,'tp'=4] {'fsdp','tp'}, dimensions={0}, use_global_device_ids=true | all-gather | bytes 67584 | tf_op jit(solution)/shard_map/all_gather | solution.py:129
  1206.7 43.2 %gather_fusion.9 = bf16[4224,2048]{1,0:T(8,128)(2,1)} fusion(bf16[513,2048]{1,0:T(8,128)(2,1)} %concatenate.30, s32[5120]{0:T(1024)S(1)} %pad_clamp_fusion), kind=kCustom, calls=%fused_computation.9 | custom fusion | bytes 34619904 | tf_op jit(solution)/shard_map/gather | solution.py:237
  1252.2 33.0 %gather_fusion.18 = f32[4096]{0:T(1024)S(1)} fusion(f32[512,16]{0,1:T(8,128)S(1)} %fusion.56, s32[4096]{0:T(1024)S(1)} %copy-done.3), kind=kCustom, calls=%fused_computation.18 | custom fusion | bytes 65536 | tf_op jit(solution)/shard_map/jit(take_along_axis)/gather | solution.py:191
  1285.5 17.7 copy.217
  1454.4 377.6 %all_to_all.66 = bf16[16,264,2048]{2,1,0:T(8,128)(2,1)S(1)} all-to-all(bf16[16,264,2048]{2,1,0:T(8,128)(2,1)S(1)} %fusion), channel_id=1, replica_groups=mesh['fsdp'=8,'tp'=4] {'fsdp'}, dimensions={0} | all-to-all | bytes 34603008 | tf_op jit(solution)/shard_map/all_to_all | solution.py:118
  1871.2 28.8 copy.220
  1899.9 377.9 %all_to_all.67 = bf16[2,2112,2048]{2,0,1:T(2,128)(2,1)} all-to-all(bf16[2,2112,2048]{2,0,1:T(2,128)(2,1)S(1)} %copy.220), channel_id=1, replica_groups=mesh['fsdp'=8,'tp'=4] {'fsdp'}, dimensions={1} | all-to-all | bytes 34603008 | tf_op jit(solution)/shard_map/all_to_all | solution.py:121
  2277.8 17.7 copy.221
  2415.5 30.9 %reduce-scatter.17.cloned.1.call-done = bf16[128,2048]{1,0:T(8,128)(2,1)} async-done(((bf16[512,2048]{1,0:T(8,128)(2,1)}), bf16[128,2048]{1,0:T(8,128)(2,1)}) %reduce-scatter.17.cloned.1.call-update) | async-done | bytes 524304 | tf_op jit(solution)/shard_map/reduce_scatter | solution.py:79
  2451.5 23.1 all-gather.19.cloned.1.call-done
  2560.7 102.5 %reduce-scatter.25.cloned.1.call-done = f32[64,16]{1,0:T(8,128)} async-done(((f32[2048,16]{1,0:T(8,128)}), f32[64,16]{1,0:T(8,128)}) %reduce-scatter.25.cloned.1.call-update) | async-done | bytes 4112
  2700.4 52.6 %reduce-scatter.23.cloned.1.call-done = bf16[512,256]{1,0:T(8,128)(2,1)} async-done(((bf16[512,2048]{1,0:T(8,128)(2,1)}), bf16[512,256]{1,0:T(8,128)(2,1)}) %reduce-scatter.23.cloned.1.call-update) | async-done | bytes 262160 | tf_op jit(solution)/shard_map/reduce_scatter | solution.py:342
  2754.8 32.9 %reduce-scatter.15.cloned.1.call-done = bf16[128,2048]{1,0:T(8,128)(2,1)} async-done(((bf16[512,2048]{1,0:T(8,128)(2,1)}), bf16[128,2048]{1,0:T(8,128)(2,1)}) %reduce-scatter.15.cloned.1.call-update) | async-done | bytes 524304 | tf_op jit(solution)/shard_map/reduce_scatter | solution.py:79
  2791.4 110.1 %reduce-scatter.27.cloned.1.call-done = f32[64,4]{1,0:T(8,128)} async-done(((f32[2048,4]{1,0:T(8,128)}), f32[64,4]{1,0:T(8,128)}) %reduce-scatter.27.cloned.1.call-update) | async-done | bytes 1040
  2902.9 139.5 %reduce-scatter.21.cloned.1.call-done = bf16[3,256,512]{1,2,0:T(8,128)(2,1)} async-done(((bf16[3,2048,512]{1,2,0:T(8,128)(2,1)}), bf16[3,256,512]{1,2,0:T(8,128)(2,1)}) %reduce-scatter.21.cloned.1.call-update) | async-done | bytes 786448 | tf_op jit(solution)/shard_map/reduce_scatter | solution.py:339
  (315 shorter events, 580.3 us)
Async XLA Ops:
  7.2 747.6 %copy-start = (bf16[2,256,2048]{2,1,0:T(8,128)(2,1)S(1)}, bf16[2,256,2048]{2,1,0:T(8,128)(2,1)}, u32[]{:S(2)}) copy-start(bf16[2,256,2048]{2,1,0:T(8,128)(2,1)} %param.22) | copy-start | bytes 6291460
  7.2 64.9 %all-gather.9.cloned.1.call-start = ((), (), s32[]{:S(2)}) async-start(), calls=%async_computation.12 | async-start | bytes 2621440 | tf_op jit(solution)/shard_map/all_gather | solution.py:75
  43.7 217.4 %copy-start.36 = (f32[1,2048]{1,0:T(1,128)}, f32[1,2048]{1,0:T(1,128)S(1)}, u32[]{:S(2)}) copy-start(f32[1,2048]{1,0:T(1,128)S(1)} %get-tuple-element.168) | copy-start | bytes 24580
  44.9 133.3 %copy-start.62 = (f32[128]{0:T(128)}, f32[128]{0:T(128)S(1)}, u32[]{:S(2)}) copy-start(f32[128]{0:T(128)S(1)} %add_rsqrt_fusion.3) | copy-start | bytes 1540
  47.0 125.0 %all-gather.11.cloned.1.call-start = ((), (), s32[]{:S(2)}) async-start(), calls=%async_computation.13 | async-start | bytes 7077888 | tf_op jit(solution)/shard_map/all_gather | solution.py:125
  49.4 174.0 %all-gather.13.cloned.1.call-start = ((), (), s32[]{:S(2)}) async-start(), calls=%async_computation.14 | async-start | bytes 2359296 | tf_op jit(solution)/shard_map/all_gather | solution.py:126
  50.1 209.7 %reduce-scatter.13.cloned.1.call-start = ((), (), s32[]{:S(2)}) async-start(), calls=%async_computation.15 | async-start | bytes 2621440 | tf_op jit(solution)/shard_map/reduce_scatter | solution.py:79
  52.2 145.3 %copy-start.21 = (pred[512,512]{0,1:T(8,128)(4,1)}, pred[512,512]{0,1:T(8,128)(4,1)S(1)}, u32[]{:S(2)}) copy-start(pred[512,512]{0,1:T(8,128)(4,1)S(1)} %fusion.50) | copy-start | bytes 786436
  52.2 139.2 %copy-start.46 = (f32[1,512]{1,0:T(1,128)}, f32[1,512]{1,0:T(1,128)S(1)}, u32[]{:S(2)}) copy-start(f32[1,512]{1,0:T(1,128)S(1)} %get-tuple-element.197) | copy-start | bytes 6148
  52.2 140.6 %copy-start.48 = (f32[1,512]{1,0:T(1,128)}, f32[1,512]{1,0:T(1,128)S(1)}, u32[]{:S(2)}) copy-start(f32[1,512]{1,0:T(1,128)S(1)} %get-tuple-element.198) | copy-start | bytes 6148
  200.8 58.9 %copy-start.6 = (bf16[128,2048]{1,0:T(8,128)(2,1)S(1)}, bf16[128,2048]{1,0:T(8,128)(2,1)}, u32[]{:S(2)}) copy-start(bf16[128,2048]{1,0:T(8,128)(2,1)} %param.12) | copy-start | bytes 1572868
  227.7 81.3 %all-gather.15.cloned.1.call-start = ((), (), s32[]{:S(2)}) async-start(), calls=%async_computation.16 | async-start | bytes 2621440 | tf_op jit(solution)/shard_map/all_gather | solution.py:75
  347.2 378.3 %all-to-all-start = ((bf16[16,264,2048]{2,1,0:T(8,128)(2,1)}), bf16[16,264,2048]{2,1,0:T(8,128)(2,1)}, u32[]{:S(2)}, u32[]{:S(2)}) async-start(bf16[16,264,2048]{2,1,0:T(8,128)(2,1)} %bitcast.173), calls=%async_computation.1 | async-start | bytes 34603008 | tf_op jit(solution)/shard_map/all_to_all | solution.py:118
  796.6 488.9 %all-to-all-start.1 = ((bf16[2,2112,2048]{2,0,1:T(2,128)(2,1)}), bf16[2,2112,2048]{2,0,1:T(2,128)(2,1)}, u32[]{:S(2)}, u32[]{:S(2)}) async-start(bf16[2,2112,2048]{2,0,1:T(2,128)(2,1)} %copy.216), calls=%async_computation.2 | async-start | bytes 34603008 | tf_op jit(solution)/shard_map/all_to_all | solution.py:121
  803.6 399.9 %all-gather.17.cloned.1.call-start = ((), (), s32[]{:S(2)}) async-start(), calls=%async_computation.18 | async-start | bytes 2621440 | tf_op jit(solution)/shard_map/all_gather | solution.py:75
  804.2 1642.2 %reduce-scatter.17.cloned.1.call-start = ((), (), s32[]{:S(2)}) async-start(), calls=%async_computation.19 | async-start | bytes 2621440 | tf_op jit(solution)/shard_map/reduce_scatter | solution.py:79
  1201.7 48.2 %copy-start.28 = (bf16[2048,16]{0,1:T(8,128)(2,1)}, bf16[2048,16]{0,1:T(8,128)(2,1)S(1)}, u32[]{:S(2)}) copy-start(bf16[2048,16]{0,1:T(8,128)(2,1)S(1)} %reshape.657) | copy-start | bytes 196612
  2414.7 59.9 %all-gather.19.cloned.1.call-start = ((), (), s32[]{:S(2)}) async-start(), calls=%async_computation.20 | async-start | bytes 2621440 | tf_op jit(solution)/shard_map/all_gather | solution.py:75
  2451.4 98.2 %reduce-scatter.19.cloned.1.call-start = ((), (), s32[]{:S(2)}) async-start(), calls=%async_computation.21 | async-start | bytes 2621440 | tf_op jit(solution)/shard_map/reduce_scatter | solution.py:79
  2516.8 146.4 %reduce-scatter.25.cloned.1.call-start = ((), (), s32[]{:S(2)}) async-start(), calls=%async_computation.24 | async-start | bytes 1081344
  2519.2 233.8 %reduce-scatter.23.cloned.1.call-start = ((), (), s32[]{:S(2)}) async-start(), calls=%async_computation.23 | async-start | bytes 2359296 | tf_op jit(solution)/shard_map/reduce_scatter | solution.py:342
  2523.6 264.1 %reduce-scatter.15.cloned.1.call-start = ((), (), s32[]{:S(2)}) async-start(), calls=%async_computation.17 | async-start | bytes 2621440 | tf_op jit(solution)/shard_map/reduce_scatter | solution.py:79
  2533.3 368.2 %reduce-scatter.27.cloned.1.call-start = ((), (), s32[]{:S(2)}) async-start(), calls=%async_computation.25 | async-start | bytes 1081344
  2552.5 489.9 %reduce-scatter.21.cloned.1.call-start = ((), (), s32[]{:S(2)}) async-start(), calls=%async_computation.22 | async-start | bytes 7077888 | tf_op jit(solution)/shard_map/reduce_scatter | solution.py:339
  (59 other events, 842.6 us)
Sparse Core Ops, SparseCore 0:
  47.1 24.8 all-gather.8
  74.7 97.2 all-gather.10
  174.0 49.2 all-gather.12
  227.9 31.8 reduce-scatter.12
  263.3 23.0 all-gather.14
  805.8 24.0 all-gather.16
  2414.8 31.5 reduce-scatter.16
  2451.5 23.0 all-gather.18
  2516.9 32.6 reduce-scatter.18
  2552.4 110.7 reduce-scatter.24
  2666.7 86.2 reduce-scatter.22
  2755.4 32.3 reduce-scatter.14
  2790.7 110.7 reduce-scatter.26
  2904.9 137.3 reduce-scatter.20
where the time goes:
time: 3060 us; the launch traced here: 3050 us
  blocking collectives  1210 us (40%)
  waiting for transfers between devices  1050 us (34%)
  local copies, waits for them, and re-layouts  541 us (18%)
  matrix products  136 us (4%)
  other arithmetic  85.2 us (3%)
    all_gather x1, blocking collectives, shards(): lax.all_gather(w_router, ('fsdp', 'tp'), axis=0, tiled=True)  397 us
    all_to_all x1, blocking collectives, return_experts(): lax.all_to_all(buffer, 'fsdp', split_axis=1, concat_axis=0, tiled=True)  378 us
    all_to_all x1, blocking collectives, send_experts(): lax.all_to_all(buffer, 'fsdp', split_axis=0, concat_axis=1, tiled=True)  378 us
    all_to_all x1, waiting for transfers between devices, send_experts(): lax.all_to_all(buffer, 'fsdp', split_axis=0, concat_axis=1, tiled=True)  368 us
    unnamed x16, waiting for transfers between devices  214 us
    reduce_scatter x1, waiting for transfers between devices, shards(): lax.psum_scatter(grad_qkv_full.astype(jnp.bfloat16), 'fsdp', scatter_dime...  139 us
    reduce_scatter x4, waiting for transfers between devices, scatter_rows(): lax.psum_scatter(values.astype(jnp.bfloat16), 'tp', scatter_dimension=0,...  112 us
    gather x8, local copies, waits for them, and re-layouts, shards(): returned[flat_index[:, pick_rank]].astype(jnp.float32)  108 us
  transfers between devices with their start and end apart: 16, of which 13 were waited for; matrix products, arithmetic and copies ran while one was open for 8% of the time, Pallas kernels for 0%

commit v1 on v0

--- a/solution.py
+++ b/solution.py
@@ -360,6 +360,233 @@
     )
 
 
+def gather_all(values, axis=0):
+    return lax.all_gather(values, ("fsdp", "tp"), axis=axis, tiled=True)
+
+
+def scatter_all(values):
+    return lax.psum_scatter(values, ("fsdp", "tp"), scatter_dimension=0, tiled=True)
+
+
+def dense_shards(
+    tokens,
+    seg_ids,
+    pad_mask,
+    expert_ids,
+    w_qkv,
+    w_out,
+    w_router,
+    norm_gains,
+    w_gate,
+    w_up,
+    w_down,
+    cotangent,
+):
+    fsdp_rank = lax.axis_index("fsdp")
+    tp_rank = lax.axis_index("tp")
+    fsdp_count = lax.axis_size("fsdp")
+    tp_count = lax.axis_size("tp")
+    local_rows, width = tokens.shape
+    seq_len = seg_ids.shape[1]
+    exp_local, _, ff_local = w_gate.shape
+    n_experts = exp_local * fsdp_count
+    head_cols = w_qkv.shape[2]
+    heads_local = head_cols // HD
+    score_scale = HD ** (-0.5)
+    own_start = tp_rank * local_rows
+
+    def own_rows(values):
+        return lax.dynamic_slice_in_dim(values, own_start, local_rows, 0)
+
+    rows_x = gather_rows(tokens).astype(jnp.float32)
+    qkv_full = lax.all_gather(w_qkv, "fsdp", axis=1, tiled=True)
+    out_full = lax.all_gather(w_out, "fsdp", axis=1, tiled=True)
+    small_full = gather_all(jnp.concatenate([w_router, norm_gains.T], axis=1))
+    router_full = small_full[:, :n_experts]
+    gains_wide = small_full[:, n_experts:].T.astype(jnp.float32)
+    all_y = gather_all(cotangent)
+    col_start = tp_rank * head_cols
+    gain_query = lax.dynamic_slice_in_dim(gains_wide[2], col_start, head_cols)
+    gain_key = lax.dynamic_slice_in_dim(gains_wide[3], col_start, head_cols)
+    cosine, sine = rope_tables(seq_len, HD)
+    x_own = tokens.astype(jnp.float32)
+    normed1, scale1 = norm_forward(rows_x, gains_wide[0])
+    rows1 = normed1.astype(jnp.bfloat16)
+    projected = jnp.einsum("sd,cdh->csh", rows1, qkv_full, preferred_element_type=jnp.float32)
+    query_raw = projected[0]
+    key_raw = projected[1]
+    square_q, square_k = tp_totals(
+        jnp.sum(query_raw * query_raw, axis=-1), jnp.sum(key_raw * key_raw, axis=-1)
+    )
+    scale_q = lax.rsqrt(square_q / width + EPSILON)[:, None]
+    scale_k = lax.rsqrt(square_k / width + EPSILON)[:, None]
+    unit_q = query_raw * scale_q
+    unit_k = key_raw * scale_k
+    queries = rotate((unit_q * gain_query).reshape(seq_len, heads_local, HD), cosine, sine).astype(
+        jnp.bfloat16
+    )
+    keys = rotate((unit_k * gain_key).reshape(seq_len, heads_local, HD), cosine, sine).astype(
+        jnp.bfloat16
+    )
+    values = projected[2].astype(jnp.bfloat16).reshape(seq_len, heads_local, HD)
+    raw_scores = (
+        jnp.einsum("qhd,khd->hqk", queries, keys, preferred_element_type=jnp.float32) * score_scale
+    )
+    allowed = allowed_mask(seg_ids[0], pad_mask[0], 0, seq_len)
+    scores = jnp.where(allowed[None], raw_scores, NEG_FILL)
+    powered = jnp.exp(scores - jnp.max(scores, axis=-1, keepdims=True))
+    probs = powered / jnp.sum(powered, axis=-1, keepdims=True)
+    probs_low = probs.astype(jnp.bfloat16)
+    mixed = (
+        jnp.einsum("hqk,khd->qhd", probs_low, values, preferred_element_type=jnp.float32)
+        .reshape(seq_len, head_cols)
+        .astype(jnp.bfloat16)
+    )
+    hidden = x_own + scatter_rows(jnp.dot(mixed, out_full, preferred_element_type=jnp.float32))
+    normed2, scale2 = norm_forward(hidden, gains_wide[1])
+    own_normed2 = normed2.astype(jnp.bfloat16)
+    all_n2 = gather_all(own_normed2)
+
+    logits = jnp.dot(own_normed2, router_full, preferred_element_type=jnp.float32)
+    router_probs = jax.nn.softmax(logits, axis=-1)
+    own_ids = own_rows(expert_ids)
+    expert_range = jnp.arange(n_experts, dtype=jnp.int32)
+    named = (own_ids[:, :, None] == expert_range[None, None, :]).any(axis=1)
+    own_gates = jnp.where(named, router_probs, 0.0)
+    all_gates = gather_all(own_gates)
+    local_gates = lax.dynamic_slice_in_dim(all_gates, fsdp_rank * exp_local, exp_local, 1)
+
+    gate_pre = jnp.einsum("td,edf->tef", all_n2, w_gate, preferred_element_type=jnp.float32)
+    up_pre = jnp.einsum("td,edf->tef", all_n2, w_up, preferred_element_type=jnp.float32)
+    y_down = jnp.einsum("td,efd->tef", all_y, w_down, preferred_element_type=jnp.float32)
+    sigmoid_gate = jax.nn.sigmoid(gate_pre)
+    silu_gate = gate_pre * sigmoid_gate
+    active = silu_gate * up_pre
+    part_dots = jnp.sum(active * y_down, axis=-1)
+    gated_active = (active * local_gates[:, :, None]).astype(jnp.bfloat16)
+    active_grad = y_down * local_gates[:, :, None]
+    gate_grad = (
+        active_grad * up_pre * sigmoid_gate * (1.0 + gate_pre * (1.0 - sigmoid_gate))
+    ).astype(jnp.bfloat16)
+    up_grad = (active_grad * silu_gate).astype(jnp.bfloat16)
+    token_grad = (
+        jnp.einsum("tef,edf->td", gate_grad, w_gate, preferred_element_type=jnp.float32)
+        + jnp.einsum("tef,edf->td", up_grad, w_up, preferred_element_type=jnp.float32)
+    ).astype(jnp.bfloat16)
+    combined = jnp.einsum(
+        "tef,efd->td", gated_active, w_down, preferred_element_type=jnp.float32
+    ).astype(jnp.bfloat16)
+
+    all_dots = lax.all_gather(lax.psum(part_dots.T, "tp"), "fsdp", axis=0, tiled=True)
+    own_dots = lax.dynamic_slice_in_dim(
+        all_dots, (fsdp_rank * tp_count + tp_rank) * local_rows, local_rows, 1
+    ).T
+    chosen = jnp.where(named, own_dots, 0.0)
+    weighted = jnp.sum(own_gates * chosen, axis=-1, keepdims=True)
+    own_logit_grad = (router_probs * (chosen - weighted)).astype(jnp.bfloat16)
+
+    normed2_grad = scatter_all(token_grad).astype(jnp.float32) + jnp.dot(
+        own_logit_grad, router_full.T, preferred_element_type=jnp.float32
+    )
+    hidden_norm_grad, gain2_grad = norm_backward(hidden, scale2, gains_wide[1], normed2_grad)
+    hidden_grad = cotangent.astype(jnp.float32) + hidden_norm_grad
+    hidden_rows = gather_rows(hidden_grad.astype(jnp.bfloat16))
+
+    layer_out = (hidden + scatter_all(combined).astype(jnp.float32)).astype(jnp.bfloat16)
+    grad_down = jnp.einsum("tef,td->efd", gated_active, all_y, preferred_element_type=jnp.float32)
+    grad_gate = jnp.einsum("td,tef->edf", all_n2, gate_grad, preferred_element_type=jnp.float32)
+    grad_up = jnp.einsum("td,tef->edf", all_n2, up_grad, preferred_element_type=jnp.float32)
+    all_logit_grad = gather_all(own_logit_grad)
+    router_rows = w_router.shape[0]
+    router_cols = lax.dynamic_slice_in_dim(
+        all_n2, (fsdp_rank * tp_count + tp_rank) * router_rows, router_rows, 1
+    )
+    grad_router = jnp.einsum(
+        "td,te->de", router_cols, all_logit_grad, preferred_element_type=jnp.float32
+    )
+
+    grad_out_full = jnp.dot(mixed.T, hidden_rows, preferred_element_type=jnp.float32)
+    mixed_grad = (
+        jnp.dot(hidden_rows, out_full.T, preferred_element_type=jnp.float32)
+        .astype(jnp.bfloat16)
+        .reshape(seq_len, heads_local, HD)
+    )
+    prob_grad = jnp.einsum("qhd,khd->hqk", mixed_grad, values, preferred_element_type=jnp.float32)
+    delta = jnp.sum(probs * prob_grad, axis=-1, keepdims=True)
+    score_grad = (probs * (prob_grad - delta)).astype(jnp.bfloat16)
+    query_grad = (
+        jnp.einsum("hqk,khd->qhd", score_grad, keys, preferred_element_type=jnp.float32)
+        * score_scale
+    )
+    key_grad = (
+        jnp.einsum("hqk,qhd->khd", score_grad, queries, preferred_element_type=jnp.float32)
+        * score_scale
+    )
+    value_grad = jnp.einsum(
+        "hqk,qhd->khd", probs_low, mixed_grad, preferred_element_type=jnp.float32
+    )
+    query_norm_grad = rotate_back(query_grad, cosine, sine).reshape(seq_len, head_cols)
+    key_norm_grad = rotate_back(key_grad, cosine, sine).reshape(seq_len, head_cols)
+    gain_query_grad = jnp.sum(query_norm_grad * unit_q, axis=0)
+    gain_key_grad = jnp.sum(key_norm_grad * unit_k, axis=0)
+    scaled_q = query_norm_grad * gain_query
+    scaled_k = key_norm_grad * gain_key
+    inner_q, inner_k = tp_totals(
+        jnp.sum(scaled_q * unit_q, axis=-1), jnp.sum(scaled_k * unit_k, axis=-1)
+    )
+    query_raw_grad = scale_q * (scaled_q - unit_q * (inner_q / width)[:, None])
+    key_raw_grad = scale_k * (scaled_k - unit_k * (inner_k / width)[:, None])
+    qkv_grad = jnp.stack(
+        [query_raw_grad, key_raw_grad, value_grad.reshape(seq_len, head_cols)]
+    ).astype(jnp.bfloat16)
+    grad_qkv_full = jnp.einsum("sd,csh->cdh", rows1, qkv_grad, preferred_element_type=jnp.float32)
+    normed1_part = jnp.einsum("csh,cdh->sd", qkv_grad, qkv_full, preferred_element_type=jnp.float32)
+    normed1_grad = scatter_rows(normed1_part)
+    gain1_grad = jnp.sum(normed1_part * (rows_x * scale1), axis=0)
+    input_norm_grad, _ = norm_backward(x_own, own_rows(scale1), gains_wide[0], normed1_grad)
+    input_grad = hidden_grad + input_norm_grad
+    zero_width = jnp.zeros((width,), jnp.float32)
+    gains_grad = jnp.stack(
+        [
+            gain1_grad,
+            gain2_grad,
+            lax.dynamic_update_slice_in_dim(zero_width, gain_query_grad, col_start, 0),
+            lax.dynamic_update_slice_in_dim(zero_width, gain_key_grad, col_start, 0),
+        ]
+    )
+    grad_qkv = lax.psum_scatter(
+        grad_qkv_full.astype(jnp.bfloat16), "fsdp", scatter_dimension=1, tiled=True
+    ).astype(jnp.float32)
+    grad_out = lax.psum_scatter(
+        grad_out_full.astype(jnp.bfloat16), "fsdp", scatter_dimension=1, tiled=True
+    ).astype(jnp.float32)
+    gain_cols = norm_gains.shape[1]
+    grad_gains = lax.dynamic_slice_in_dim(
+        lax.psum(gains_grad, ("fsdp", "tp")),
+        (fsdp_rank * tp_count + tp_rank) * gain_cols,
+        gain_cols,
+        1,
+    )
+    return (
+        layer_out,
+        input_grad,
+        grad_qkv,
+        grad_out,
+        grad_router,
+        grad_gains,
+        grad_gate,
+        grad_up,
+        grad_down,
+    )
+
+
+def pick_shards(*arguments):
+    n_experts = arguments[8].shape[0] * lax.axis_size("fsdp")
+    top_count = arguments[3].shape[1]
+    body = dense_shards if n_experts <= 2 * top_count else shards
+    return body(*arguments)
+
+
 def solution(mesh):
     placed = (
         P(("fsdp", "tp"), None),
@@ -376,7 +603,7 @@
         P(("fsdp", "tp"), None),
     )
     return jax.shard_map(
-        shards,
+        pick_shards,
         mesh=mesh,
         in_specs=placed,
         out_specs=(

time: 3060 us -> 1270 us (0.42)
  blocking collectives: 1210 us -> 215 us
  local copies, waits for them, and re-layouts: 541 us -> 34.3 us
  waiting for transfers between devices: 1050 us -> 729 us
  matrix products: 136 us -> 204 us
    all_to_all x2 -> x0, blocking collectives: 755 us -> none  [the longest x1 378 us: return_experts(): lax.all_to_all(buffer, 'fsdp', split_axis=1, concat_axis=0, tiled=True)]
    all_to_all x2 -> x0, waiting for transfers between devices: 368 us -> none  [the longest x1 368 us: send_experts(): lax.all_to_all(buffer, 'fsdp', split_axis=0, concat_axis=1, tiled=True)]
    gather x26 -> x0, local copies, waits for them, and re-layouts: 354 us -> none  [the longest x8 108 us: shards(): returned[flat_index[:, pick_rank]].astype(jnp.float32)]
    all_gather x2 -> x4, blocking collectives: 433 us -> 142 us  [the longest x3 119 us: gather_all(): return lax.all_gather(values, ('fsdp', 'tp'), axis=axis, tiled=True)]
    unnamed x16 -> x12, waiting for transfers between devices: 214 us -> 2.03 us
    reduce_scatter x2 -> x4, waiting for transfers between devices: 192 us -> 378 us  [the longest x2 261 us: scatter_all(): lax.psum_scatter(values, ('fsdp', 'tp'), scatter_dimension=0, tiled=True)]
    all_gather x2 -> x4, waiting for transfers between devices: 122 us -> 295 us  [the longest x2 197 us: gather_all(): return lax.all_gather(values, ('fsdp', 'tp'), axis=axis, tiled=True)]
    reduce_scatter x4 -> x2, waiting for transfers between devices: 112 us -> 32 us  [scatter_rows(): lax.psum_scatter(values.astype(jnp.bfloat16), 'tp', scatter_dimension=0,...]
  transfers between devices with their start and end apart: 16 -> 12, of which waited for: 13 -> 9; matrix products, arithmetic and copies ran while one was open for 8% -> 15% of each run, Pallas kernels for 0% -> 0%
where the time goes in v1:
time: 1270 us; the launch traced here: 1260 us
  waiting for transfers between devices  729 us (57%)
  blocking collectives  215 us (17%)
  matrix products  204 us (16%)
  other arithmetic  62.4 us (5%)
  local copies, waits for them, and re-layouts  34.3 us (3%)
  between operations  15 us (1%)
    reduce_scatter x2, waiting for transfers between devices, scatter_all(): lax.psum_scatter(values, ('fsdp', 'tp'), scatter_dimension=0, tiled=True)  261 us
    all_gather x2, waiting for transfers between devices, gather_all(): return lax.all_gather(values, ('fsdp', 'tp'), axis=axis, tiled=True)  197 us
    all_gather x3, blocking collectives, gather_all(): return lax.all_gather(values, ('fsdp', 'tp'), axis=axis, tiled=True)  119 us
    reduce_scatter x1, waiting for transfers between devices, dense_shards(): lax.psum_scatter(grad_qkv_full.astype(jnp.bfloat16), 'fsdp', scatter_dime...  117 us
    all_gather x1, waiting for transfers between devices, dense_shards(): qkv_full = lax.all_gather(w_qkv, 'fsdp', axis=1, tiled=True)  81.1 us
    psum x1, blocking collectives, dense_shards(): lax.psum(gains_grad, ('fsdp', 'tp'))  51.6 us
    reduce_scatter x2, waiting for transfers between devices, scatter_rows(): lax.psum_scatter(values.astype(jnp.bfloat16), 'tp', scatter_dimension=0,...  32 us
    dot_general x1, matrix products, dense_shards(): jnp.einsum('td,efd->tef', all_y, w_down, preferred_element_type=jnp.float32)  26.7 us
  transfers between devices with their start and end apart: 12, of which 9 were waited for; matrix products, arithmetic and copies ran while one was open for 15% of the time, Pallas kernels for 0%

profile of v1, /device:TPU:9, one launch (start us, length us, event | category | flops | bytes accessed | tf_op | source)
XLA Modules:
  0.0 1261.3 jit_solution(9005046093666208533)
XLA Ops:
  12.5 36.7 %all-gather = bf16[32,64,20]{1,2,0:T(8,128)(2,1)S(1)} all-gather(bf16[1,64,20]{1,2,0:T(8,128)(2,1)S(1)} %maximum_bitcast_fusion), channel_id=1, replica_groups=mesh['fsdp'=8,'tp'=4] {'fsdp','tp'}, dimensions={0}, use_global_device_ids=true | all-gather | bytes 84480 | tf_op jit(solution)/shard_map/all_gather | solution.py:364
  53.6 81.1 %all-gather.11.cloned.1.call-done = bf16[3,2048,512]{1,2,0:T(8,128)(2,1)} async-done(((bf16[3,256,512]{1,2,0:T(8,128)(2,1)}), bf16[3,2048,512]{1,2,0:T(8,128)(2,1)}) %all-gather.11.cloned.1.call-update) | async-done | bytes 6291472 | tf_op jit(solution)/shard_map/all_gather | solution.py:402
  169.0 17.0 %all-gather.13.cloned.1.call-done = bf16[512,2048]{1,0:T(8,128)(2,1)} async-done(((bf16[512,256]{1,0:T(8,128)(2,1)}), bf16[512,2048]{1,0:T(8,128)(2,1)}) %all-gather.13.cloned.1.call-update) | async-done | bytes 2097168 | tf_op jit(solution)/shard_map/all_gather | solution.py:403
  190.2 32.0 %reduce-scatter.7.cloned.1.call-done = bf16[128,2048]{1,0:T(8,128)(2,1)} async-done(((bf16[512,2048]{1,0:T(8,128)(2,1)}), bf16[128,2048]{1,0:T(8,128)(2,1)}) %reduce-scatter.7.cloned.1.call-update) | async-done | bytes 524304 | tf_op jit(solution)/shard_map/reduce_scatter | solution.py:79
  229.1 111.1 %all-gather.15.cloned.1.call-done = bf16[4096,2048]{1,0:T(8,128)(2,1)} async-done(((bf16[128,2048]{1,0:T(8,128)(2,1)}), bf16[4096,2048]{1,0:T(8,128)(2,1)}) %all-gather.15.cloned.1.call-update) | async-done | bytes 16777232 | tf_op jit(solution)/shard_map/all_gather | solution.py:364
  340.1 15.3 %fusion.10 = f32[4096,2,256]{0,2,1:T(8,128)} fusion(bf16[2,2048,256]{2,1,0:T(8,128)(2,1)} %param.21, bf16[4096,2048]{1,0:T(8,128)(2,1)} %all-gather.15.cloned.1.call-done), kind=kOutput, calls=%fused_computation.12 | convolution fusion | flops 8589934592 | bytes 27262976 | tf_op jit(solution)/shard_map/td,edf->tef/dot_general | solution.py:460
  355.4 14.7 %fusion.12 = f32[4096,2,256]{0,2,1:T(8,128)} fusion(bf16[2,2048,256]{2,1,0:T(8,128)(2,1)S(1)} %copy-done.31, bf16[4096,2048]{1,0:T(8,128)(2,1)} %all-gather.15.cloned.1.call-done), kind=kOutput, calls=%fused_computation.14 | convolution fusion | flops 8589934592 | bytes 27262976 | tf_op jit(solution)/shard_map/td,edf->tef/dot_general | solution.py:459
  370.1 86.2 %all-gather.17.cloned.1.call-done = bf16[4096,2048]{1,0:T(8,128)(2,1)} async-done(((bf16[128,2048]{1,0:T(8,128)(2,1)}), bf16[4096,2048]{1,0:T(8,128)(2,1)}) %all-gather.17.cloned.1.call-update) | async-done | bytes 16777232 | tf_op jit(solution)/shard_map/all_gather | solution.py:364
  456.4 26.7 %multiply_reduce_fusion = (f32[4096,2]{0,1:T(2,128)S(1)}, f32[4096,2,256]{0,2,1:T(8,128)}) fusion(f32[4096,2,256]{0,2,1:T(8,128)} %fusion.10, f32[4096,2,256]{0,2,1:T(8,128)} %fusion.12, bf16[2,256,2048]{2,1,0:T(8,128)(2,1)S(1)} %copy-done, bf16[4096,2048]{1,0:T(8,128)(2,1)} %all-gather.17.cloned.1.call-done), kind=kOutput, calls=%fused_computation.16 | convolution fusion | flops 8604606464 | bytes 44072960 | tf_op jit(solution)/shard_map/td,efd->tef/dot_general | solution.py:461
  493.3 22.9 %all-gather.1 = f32[8,2,4096]{2,1,0:T(2,128)S(1)} all-gather(f32[1,2,4096]{2,1,0:T(2,128)S(1)} %bitcast.142), channel_id=1, replica_groups=mesh['fsdp'=8,'tp'=4] {'fsdp'}, dimensions={0}, use_global_device_ids=true | all-gather | bytes 294912 | tf_op jit(solution)/shard_map/all_gather | solution.py:480
  517.7 43.1 %all_gather.35 = f32[4096,16]{0,1:T(8,128)S(1)} all-gather(f32[128,16]{0,1:T(8,128)S(1)} %get-tuple-element.60), channel_id=1, replica_groups=mesh['fsdp'=8,'tp'=4] {'fsdp','tp'}, dimensions={0}, use_global_device_ids=true | all-gather | bytes 270336 | tf_op jit(solution)/shard_map/all_gather | solution.py:364
  560.8 21.9 %multiply_convert_fusion = (bf16[4096,2,256]{0,2,1:T(8,128)(2,1)}, bf16[4096,2,256]{0,2,1:T(8,128)(2,1)S(1)}, bf16[4096,2,256]{0,2,1:T(8,128)(2,1)}) fusion(f32[4096,2,256]{0,2,1:T(8,128)} %get-tuple-element.91, f32[4096,2]{0,1:T(2,128)S(1)} %constant_dynamic-slice_fusion.1, f32[4096,2,256]{0,2,1:T(8,128)} %fusion.12, f32[4096,2,256]{0,2,1:T(8,128)} %fusion.10), kind=kLoop, calls=%fused_computation.17 | loop fusion | flops 35651584 | bytes 37781504 | tf_op jit(solution)/shard_map/convert_element_type | solution.py:471
  582.7 15.3 %fusion.71 = f32[4096,2048,1]{1,0,2:T(8,128)} fusion(bf16[4096,2,256]{0,2,1:T(8,128)(2,1)S(1)} %get-tuple-element.62, bf16[2,2048,256]{2,1,0:T(8,128)(2,1)S(1)} %copy-done.32), kind=kOutput, calls=%fused_computation.153 | convolution fusion | flops 8589934592 | bytes 39845888 | tf_op jit(solution)/shard_map/tef,edf->td/dot_general | solution.py:473
  598.0 22.8 %fusion.1 = bf16[4096,2048]{1,0:T(8,128)(2,1)} fusion(f32[4096,2048,1]{1,0,2:T(8,128)} %fusion.71, bf16[4096,2,256]{0,2,1:T(8,128)(2,1)} %get-tuple-element.61, bf16[2,2048,256]{2,1,0:T(8,128)(2,1)} %param.21), kind=kOutput, calls=%fused_computation.2 | convolution fusion | flops 8606711808 | bytes 56623104 | tf_op jit(solution)/shard_map/tef,edf->td/dot_general | solution.py:474
  621.7 186.8 %reduce-scatter.11.cloned.1.call-done = bf16[128,2048]{1,0:T(8,128)(2,1)} async-done(((bf16[4096,2048]{1,0:T(8,128)(2,1)}), bf16[128,2048]{1,0:T(8,128)(2,1)}) %reduce-scatter.11.cloned.1.call-update) | async-done | bytes 524304 | tf_op jit(solution)/shard_map/reduce_scatter | solution.py:368
  813.9 21.8 %all-gather.19.cloned.1.call-done = bf16[512,2048]{1,0:T(8,128)(2,1)} async-done(((bf16[128,2048]{1,0:T(8,128)(2,1)}), bf16[512,2048]{1,0:T(8,128)(2,1)}) %all-gather.19.cloned.1.call-update) | async-done | bytes 2097168 | tf_op jit(solution)/shard_map/all_gather | solution.py:75
  879.6 14.7 %bitcast_convert_fusion = bf16[4096,2048]{1,0:T(8,128)(2,1)} fusion(bf16[4096,2,256]{0,2,1:T(8,128)(2,1)} %get-tuple-element.63, bf16[2,256,2048]{2,1,0:T(8,128)(2,1)S(1)} %copy-done), kind=kOutput, calls=%fused_computation.3 | convolution fusion | flops 8598323200 | bytes 23068672 | tf_op jit(solution)/shard_map/tef,efd->td/dot_general | solution.py:476
  903.4 15.0 %fusion.20 = f32[2,2048,256]{1,2,0:T(8,128)} fusion(bf16[4096,2,256]{0,2,1:T(8,128)(2,1)} %copy-done.9, bf16[4096,2048]{1,0:T(8,128)(2,1)} %all-gather.15.cloned.1.call-done), kind=kOutput, calls=%fused_computation.35 | convolution fusion | flops 8589934592 | bytes 25165824 | tf_op jit(solution)/shard_map/td,tef->edf/dot_general | solution.py:497
  923.8 15.2 %fusion.23 = f32[2,2048,256]{1,2,0:T(8,128)} fusion(bf16[4096,2,256]{0,2,1:T(8,128)(2,1)} %get-tuple-element.61, bf16[4096,2048]{1,0:T(8,128)(2,1)} %all-gather.15.cloned.1.call-done), kind=kOutput, calls=%fused_computation.36 | convolution fusion | flops 8589934592 | bytes 25165824 | tf_op jit(solution)/shard_map/td,tef->edf/dot_general | solution.py:498
  944.4 39.1 %all_gather.39 = bf16[4096,16]{0,1:T(8,128)(2,1)S(1)} all-gather(bf16[128,16]{0,1:T(8,128)(2,1)S(1)} %multiply_convert_fusion.7), channel_id=1, replica_groups=mesh['fsdp'=8,'tp'=4] {'fsdp','tp'}, dimensions={0}, use_global_device_ids=true | all-gather | bytes 135168 | tf_op jit(solution)/shard_map/all_gather | solution.py:364
  985.7 15.2 %fusion.2 = f32[2,256,2048]{2,1,0:T(8,128)} fusion(bf16[4096,2,256]{0,2,1:T(8,128)(2,1)} %get-tuple-element.63, bf16[4096,2048]{1,0:T(8,128)(2,1)} %all-gather.17.cloned.1.call-done), kind=kOutput, calls=%fused_computation.4 | convolution fusion | flops 8589934592 | bytes 25165824 | tf_op jit(solution)/shard_map/tef,td->efd/dot_general | solution.py:496
  1001.7 51.6 %psum.47 = f32[4,2048]{1,0:T(4,128)S(1)} all-reduce(f32[4,2048]{1,0:T(4,128)S(1)} %pad_maximum_fusion.7), channel_id=1, replica_groups=mesh['fsdp'=8,'tp'=4] {'fsdp','tp'}, use_global_device_ids=true, to_apply=%region_31.32 | all-reduce | flops 8192 | bytes 65536 | tf_op jit(solution)/shard_map/psum | solution.py:565
  1057.2 74.2 %reduce-scatter.9.cloned.1.call-done = bf16[128,2048]{1,0:T(8,128)(2,1)} async-done(((bf16[4096,2048]{1,0:T(8,128)(2,1)}), bf16[128,2048]{1,0:T(8,128)(2,1)}) %reduce-scatter.9.cloned.1.call-update) | async-done | bytes 524304 | tf_op jit(solution)/shard_map/reduce_scatter | solution.py:368
  1135.0 116.6 %reduce-scatter.15.cloned.1.call-done = bf16[3,256,512]{1,2,0:T(8,128)(2,1)} async-done(((bf16[3,2048,512]{1,2,0:T(8,128)(2,1)}), bf16[3,256,512]{1,2,0:T(8,128)(2,1)}) %reduce-scatter.15.cloned.1.call-update) | async-done | bytes 786448 | tf_op jit(solution)/shard_map/reduce_scatter | solution.py:557
  (180 shorter events, 149.3 us)
Async XLA Ops:
  7.2 449.2 %copy-start = (bf16[2,256,2048]{2,1,0:T(8,128)(2,1)S(1)}, bf16[2,256,2048]{2,1,0:T(8,128)(2,1)}, u32[]{:S(2)}) copy-start(bf16[2,256,2048]{2,1,0:T(8,128)(2,1)} %param.22) | copy-start | bytes 6291460
  7.2 43.3 %copy-start.25 = (s32[1,512]{1,0:T(1,128)S(1)}, s32[1,512]{1,0:T(1,128)}, u32[]{:S(2)}) copy-start(s32[1,512]{1,0:T(1,128)} %param.13) | copy-start | bytes 6148
  7.2 44.3 %all-gather.9.cloned.1.call-start = ((), (), s32[]{:S(2)}) async-start(), calls=%async_computation.6 | async-start | bytes 2621440 | tf_op jit(solution)/shard_map/all_gather | solution.py:75
  7.9 126.7 %all-gather.11.cloned.1.call-start = ((), (), s32[]{:S(2)}) async-start(), calls=%async_computation.7 | async-start | bytes 7077888 | tf_op jit(solution)/shard_map/all_gather | solution.py:402
  10.3 175.7 %all-gather.13.cloned.1.call-start = ((), (), s32[]{:S(2)}) async-start(), calls=%async_computation.8 | async-start | bytes 2359296 | tf_op jit(solution)/shard_map/all_gather | solution.py:403
  11.0 211.2 %reduce-scatter.7.cloned.1.call-start = ((), (), s32[]{:S(2)}) async-start(), calls=%async_computation.9 | async-start | bytes 2621440 | tf_op jit(solution)/shard_map/reduce_scatter | solution.py:79
  49.5 91.5 %copy-start.23 = (f32[1,2048]{1,0:T(1,128)}, f32[1,2048]{1,0:T(1,128)S(1)}, u32[]{:S(2)}) copy-start(f32[1,2048]{1,0:T(1,128)S(1)} %get-tuple-element.85) | copy-start | bytes 24580
  50.5 108.1 %copy-start.10 = (f32[512,64]{1,0:T(8,128)}, f32[512,64]{1,0:T(8,128)S(1)}, u32[]{:S(2)}) copy-start(f32[512,64]{1,0:T(8,128)S(1)} %get-tuple-element.87) | copy-start | bytes 393220
  53.5 87.5 %copy-start.28 = (f32[512]{0:T(512)}, f32[512]{0:T(512)S(1)}, u32[]{:S(2)}) copy-start(f32[512]{0:T(512)S(1)} %add_rsqrt_fusion.2) | copy-start | bytes 6148
  168.9 54.6 %copy-start.33 = (bf16[4,128,512]{2,1,0:T(8,128)(2,1)}, bf16[4,128,512]{2,1,0:T(8,128)(2,1)S(1)}, u32[]{:S(2)}) copy-start(bf16[4,128,512]{2,1,0:T(8,128)(2,1)S(1)} %convolution_convert_fusion.4) | copy-start | bytes 1572868
  168.9 53.3 %copy-start.1 = (bf16[128,2048]{1,0:T(8,128)(2,1)S(1)}, bf16[128,2048]{1,0:T(8,128)(2,1)}, u32[]{:S(2)}) copy-start(bf16[128,2048]{1,0:T(8,128)(2,1)} %param.12) | copy-start | bytes 1572868
  190.2 150.0 %all-gather.15.cloned.1.call-start = ((), (), s32[]{:S(2)}) async-start(), calls=%async_computation.10 | async-start | bytes 17301504 | tf_op jit(solution)/shard_map/all_gather | solution.py:364
  225.6 230.8 %all-gather.17.cloned.1.call-start = ((), (), s32[]{:S(2)}) async-start(), calls=%async_computation.12 | async-start | bytes 17301504 | tf_op jit(solution)/shard_map/all_gather | solution.py:364
  226.2 582.3 %reduce-scatter.11.cloned.1.call-start = ((), (), s32[]{:S(2)}) async-start(), calls=%async_computation.13 | async-start | bytes 17301504 | tf_op jit(solution)/shard_map/reduce_scatter | solution.py:368
  228.5 287.9 %copy-start.30 = (f32[128]{0:T(128)}, f32[128]{0:T(128)S(1)}, u32[]{:S(2)}) copy-start(f32[128]{0:T(128)S(1)} %get-tuple-element.92) | copy-start | bytes 1540
  516.4 66.3 %copy-start.22 = (f32[16,4096]{1,0:T(8,128)}, f32[16,4096]{1,0:T(8,128)S(1)}, u32[]{:S(2)}) copy-start(f32[16,4096]{1,0:T(8,128)S(1)} %reshape.375) | copy-start | bytes 786436
  560.8 21.9 %copy-start.32 = (bf16[2,2048,256]{2,1,0:T(8,128)(2,1)S(1)}, bf16[2,2048,256]{2,1,0:T(8,128)(2,1)}, u32[]{:S(2)}) copy-start(bf16[2,2048,256]{2,1,0:T(8,128)(2,1)} %param.20) | copy-start | bytes 6291460
  620.8 187.6 %copy-start.4 = (bf16[128,2048]{1,0:T(8,128)(2,1)S(1)}, bf16[128,2048]{1,0:T(8,128)(2,1)}, u32[]{:S(2)}) copy-start(bf16[128,2048]{1,0:T(8,128)(2,1)} %reduce-scatter.7.cloned.1.call-done) | copy-start | bytes 1572868
  620.8 214.8 %all-gather.19.cloned.1.call-start = ((), (), s32[]{:S(2)}) async-start(), calls=%async_computation.14 | async-start | bytes 2621440 | tf_op jit(solution)/shard_map/all_gather | solution.py:75
  813.4 240.6 %reduce-scatter.17.cloned.1.call-start = ((), (), s32[]{:S(2)}) async-start(), calls=%async_computation.17 | async-start | bytes 2359296 | tf_op jit(solution)/shard_map/reduce_scatter | solution.py:560
  840.0 215.8 %reduce-scatter.13.cloned.1.call-start = ((), (), s32[]{:S(2)}) async-start(), calls=%async_computation.15 | async-start | bytes 2621440 | tf_op jit(solution)/shard_map/reduce_scatter | solution.py:79
  879.4 252.0 %reduce-scatter.9.cloned.1.call-start = ((), (), s32[]{:S(2)}) async-start(), calls=%async_computation.11 | async-start | bytes 17301504 | tf_op jit(solution)/shard_map/reduce_scatter | solution.py:368
  894.3 357.3 %reduce-scatter.15.cloned.1.call-start = ((), (), s32[]{:S(2)}) async-start(), calls=%async_computation.16 | async-start | bytes 7077888 | tf_op jit(solution)/shard_map/reduce_scatter | solution.py:557
  1000.9 130.5 %copy-start.27 = (f32[128]{0:T(128)S(1)}, f32[128]{0:T(128)}, u32[]{:S(2)}) copy-start(f32[128]{0:T(128)} %copy-done.26) | copy-start | bytes 1540
  (26 other events, 118.9 us)
Sparse Core Ops, SparseCore 0:
  9.6 25.0 all-gather.8
  37.3 97.2 all-gather.10
  136.7 49.2 all-gather.12
  190.3 31.8 reduce-scatter.6
  225.9 114.1 all-gather.14
  343.3 113.0 all-gather.16
  621.0 187.4 reduce-scatter.10
  813.5 22.0 all-gather.18
  840.1 65.9 reduce-scatter.16
  908.6 32.4 reduce-scatter.12
  943.4 187.9 reduce-scatter.8
  1134.9 116.7 reduce-scatter.14

commit v2 on v1

--- a/solution.py
+++ b/solution.py
@@ -1,6 +1,11 @@
+import functools
+import itertools
+
 import jax
 import jax.numpy as jnp
 from jax import lax
+from jax.experimental import pallas as pl
+from jax.experimental.pallas import tpu as pltpu
 from jax.sharding import PartitionSpec as P
 
 HD = 128
@@ -360,12 +365,188 @@
     )
 
 
-def gather_all(values, axis=0):
-    return lax.all_gather(values, ("fsdp", "tp"), axis=axis, tiled=True)
-
-
-def scatter_all(values):
-    return lax.psum_scatter(values, ("fsdp", "tp"), scatter_dimension=0, tiled=True)
+GRID = (4, 2, 2, 2)
+LANES = 128
+CONTRACT_LAST = (((1,), (1,)), ((), ()))
+
+
+def permutation(target):
+    def place(z, x, y, c):
+        return ((z * GRID[1] + x) * GRID[2] + y) * GRID[3] + c
+
+    return [
+        (place(*at), place(*target(*at))) for at in itertools.product(*(range(n) for n in GRID))
+    ]
+
+
+SWAP_CORE = permutation(lambda z, x, y, c: (z, x, y, 1 - c))
+SWAP_X = permutation(lambda z, x, y, c: (z, 1 - x, y, c))
+SWAP_Y = permutation(lambda z, x, y, c: (z, x, 1 - y, c))
+SWAP_FIRST = permutation(lambda z, x, y, c: (z, 1 - x, y, c) if c == 0 else (z, x, 1 - y, c))
+SWAP_SECOND = permutation(lambda z, x, y, c: (z, x, 1 - y, c) if c == 0 else (z, 1 - x, y, c))
+SWAP_Z = [permutation(lambda z, x, y, c, b=b: (z ^ b, x, y, c)) for b in (1, 2)]
+
+
+def shift_z(steps):
+    return permutation(lambda z, x, y, c: ((z + steps) % GRID[0], x, y, c))
+
+
+def send(values, pairs):
+    return lax.ppermute(values, ("fsdp", "tp"), pairs)
+
+
+def add_low(*terms):
+    return sum(term.astype(jnp.float32) for term in terms).astype(jnp.bfloat16)
+
+
+def gather_rounds(own):
+    rounds = []
+    column = own
+    for step in range(GRID[0]):
+        if step:
+            column = send(column, shift_z(1))
+        half = jnp.concatenate([column, send(column, SWAP_FIRST)], axis=0)
+        plane = jnp.concatenate([half, send(half, SWAP_SECOND)], axis=0)
+        rounds.append((plane, send(plane, SWAP_CORE)))
+    return rounds
+
+
+def scatter_rounds(rounds):
+    total = None
+    for step, (plane, other) in enumerate(rounds):
+        rows = plane.shape[0] // 4
+        back = send(other, SWAP_CORE)
+        second = send(add_low(plane[2 * rows :], back[2 * rows :]), SWAP_SECOND)
+        first = send(
+            add_low(plane[rows : 2 * rows], back[rows : 2 * rows], second[rows:]), SWAP_FIRST
+        )
+        mine = [plane[:rows], back[:rows], second[:rows], first]
+        if step:
+            mine = [send(add_low(*mine), shift_z(-step))]
+        mine = sum(term.astype(jnp.float32) for term in mine)
+        total = mine if total is None else total + mine
+    return total
+
+
+def scatter_small(rounds):
+    plane = jnp.stack([pair[0] for pair in rounds])
+    other = jnp.stack([pair[1] for pair in rounds])
+    rows = plane.shape[-1] // 4
+    plane = plane + send(other, SWAP_CORE)
+    half = plane[..., : 2 * rows] + send(plane[..., 2 * rows :], SWAP_SECOND)
+    mine = half[..., :rows] + send(half[..., rows:], SWAP_FIRST)
+    return mine[0] + sum(send(mine[step], shift_z(-step)) for step in range(1, GRID[0]))
+
+
+def butterfly_sum(values):
+    for pairs in (SWAP_CORE, SWAP_Y, SWAP_X, *SWAP_Z):
+        values = values + send(values, pairs)
+    return values
+
+
+def tp_gather(own):
+    is_core1 = lax.axis_index("tp") % 2 == 1
+    is_y1 = lax.axis_index("tp") >= 2
+    far = send(own, SWAP_Y)
+    mine = jnp.stack([jnp.where(is_y1, far, own), jnp.where(is_y1, own, far)])
+    theirs = send(mine, SWAP_CORE)
+    both = jnp.stack(
+        [jnp.where(is_core1, theirs, mine), jnp.where(is_core1, mine, theirs)], axis=1
+    )
+    return both.reshape(4 * own.shape[0], *own.shape[1:])
+
+
+def tp_scatter(values):
+    core = lax.axis_index("tp") % 2
+    side = lax.axis_index("tp") // 2
+    rows = values.shape[0] // 4
+    blocks = values.astype(jnp.bfloat16).reshape(2, 2, rows, values.shape[1])
+    theirs = lax.dynamic_index_in_dim(blocks, 1 - core, 1, keepdims=False)
+    mine = lax.dynamic_index_in_dim(blocks, core, 1, keepdims=False)
+    back = send(theirs, SWAP_CORE)
+
+    def at(pair, which):
+        return lax.dynamic_index_in_dim(pair, which, 0, keepdims=False)
+
+    far = send(add_low(at(mine, 1 - side), at(back, 1 - side)), SWAP_Y)
+    return sum(term.astype(jnp.float32) for term in (at(mine, side), at(back, side), far))
+
+
+def expert_kernel(
+    rows_ref,
+    grads_ref,
+    router_ref,
+    place_ref,
+    gate_ref,
+    up_ref,
+    down_ref,
+    route_ref,
+    active_ref,
+    hidden_ref,
+    dots_ref,
+    *,
+    n_experts,
+):
+    exp_local, width, units = gate_ref.shape
+    rows = rows_ref[...]
+    grads = grads_ref[:, :width]
+    named = grads_ref[:, width:].astype(jnp.float32)
+    lane = lax.broadcasted_iota(jnp.int32, (1, LANES), 1)
+    logits = jnp.dot(rows, router_ref[...], preferred_element_type=jnp.float32)
+    logits = jnp.where(lane < n_experts, logits, NEG_FILL)
+    powered = jnp.exp(logits - jnp.max(logits, axis=-1, keepdims=True))
+    gates = powered / jnp.sum(powered, axis=-1, keepdims=True) * named
+    route = None
+    dots = jnp.zeros(logits.shape, jnp.float32)
+    for expert in range(exp_local):
+        place = place_ref[expert : expert + 1, :]
+        gate = jnp.sum(gates * place, axis=-1, keepdims=True)
+        gate_pre = jnp.dot(rows, gate_ref[expert], preferred_element_type=jnp.float32)
+        up_pre = jnp.dot(rows, up_ref[expert], preferred_element_type=jnp.float32)
+        y_down = lax.dot_general(
+            grads, down_ref[expert], CONTRACT_LAST, preferred_element_type=jnp.float32
+        )
+        sigmoid = 1.0 / (1.0 + jnp.exp(-gate_pre))
+        silu = gate_pre * sigmoid
+        active = silu * up_pre
+        dots = dots + jnp.sum(active * y_down, axis=-1, keepdims=True) * place
+        active_ref[:, expert * units : (expert + 1) * units] = (active * gate).astype(jnp.bfloat16)
+        active_grad = y_down * gate
+        gate_grad = (active_grad * up_pre * sigmoid * (1.0 + gate_pre * (1.0 - sigmoid))).astype(
+            jnp.bfloat16
+        )
+        up_grad = (active_grad * silu).astype(jnp.bfloat16)
+        hidden_ref[:, expert * units : (expert + 1) * units] = gate_grad
+        hidden_ref[:, (exp_local + expert) * units : (exp_local + expert + 1) * units] = up_grad
+        part = lax.dot_general(
+            gate_grad, gate_ref[expert], CONTRACT_LAST, preferred_element_type=jnp.float32
+        ) + lax.dot_general(
+            up_grad, up_ref[expert], CONTRACT_LAST, preferred_element_type=jnp.float32
+        )
+        route = part if route is None else route + part
+    route_ref[...] = route.astype(jnp.bfloat16)
+    dots_ref[...] = jnp.transpose(dots)[:n_experts]
+
+
+def expert_rows(rows, grads, router, place, w_gate, w_up, w_down, n_experts):
+    count, width = rows.shape
+    exp_local, _, units = w_gate.shape
+    flops = 2 * count * width * units * exp_local * 5
+    moved = 2 * (3 * rows.size + 3 * w_gate.size + 3 * count * exp_local * units)
+    return pl.pallas_call(
+        functools.partial(expert_kernel, n_experts=n_experts),
+        out_shape=[
+            jax.ShapeDtypeStruct((count, width), jnp.bfloat16),
+            jax.ShapeDtypeStruct((count, exp_local * units), jnp.bfloat16),
+            jax.ShapeDtypeStruct((count, 2 * exp_local * units), jnp.bfloat16),
+            jax.ShapeDtypeStruct((n_experts, count), jnp.float32),
+        ],
+        cost_estimate=pl.CostEstimate(
+            flops=flops, bytes_accessed=moved, transcendentals=count * units * exp_local
+        ),
+        compiler_params=pltpu.CompilerParams(vmem_limit_bytes=40 * 1024 * 1024),
+        name="expert_rows",
+    )(rows, grads, router, place, w_gate, w_up, w_down)
 
 
 def dense_shards(
@@ -394,17 +575,29 @@
     heads_local = head_cols // HD
     score_scale = HD ** (-0.5)
     own_start = tp_rank * local_rows
+    small_cols = norm_gains.shape[1]
+    small_start = (fsdp_rank * tp_count + tp_rank) * small_cols
 
     def own_rows(values):
         return lax.dynamic_slice_in_dim(values, own_start, local_rows, 0)
 
-    rows_x = gather_rows(tokens).astype(jnp.float32)
+    rows_x = tp_gather(tokens).astype(jnp.float32)
     qkv_full = lax.all_gather(w_qkv, "fsdp", axis=1, tiled=True)
     out_full = lax.all_gather(w_out, "fsdp", axis=1, tiled=True)
-    small_full = gather_all(jnp.concatenate([w_router, norm_gains.T], axis=1))
-    router_full = small_full[:, :n_experts]
-    gains_wide = small_full[:, n_experts:].T.astype(jnp.float32)
-    all_y = gather_all(cotangent)
+    small_own = jnp.concatenate([w_router.T, norm_gains], axis=0)
+    small_full = butterfly_sum(
+        lax.dynamic_update_slice_in_dim(
+            jnp.zeros((n_experts + 4, width), jnp.bfloat16), small_own, small_start, 1
+        )
+    )
+    router_full = small_full[:n_experts].T
+    gains_wide = small_full[n_experts:].astype(jnp.float32)
+    own_ids = own_rows(expert_ids)
+    expert_range = jnp.arange(n_experts, dtype=jnp.int32)
+    named = (own_ids[:, :, None] == expert_range[None, None, :]).any(axis=1)
+    named_wide = jnp.pad(named.astype(jnp.bfloat16), ((0, 0), (0, LANES - n_experts)))
+    grad_rounds = gather_rounds(jnp.concatenate([cotangent, named_wide], axis=1))
+
     col_start = tp_rank * head_cols
     gain_query = lax.dynamic_slice_in_dim(gains_wide[2], col_start, head_cols)
     gain_key = lax.dynamic_slice_in_dim(gains_wide[3], col_start, head_cols)
@@ -442,68 +635,68 @@
         .reshape(seq_len, head_cols)
         .astype(jnp.bfloat16)
     )
-    hidden = x_own + scatter_rows(jnp.dot(mixed, out_full, preferred_element_type=jnp.float32))
+    hidden = x_own + tp_scatter(jnp.dot(mixed, out_full, preferred_element_type=jnp.float32))
     normed2, scale2 = norm_forward(hidden, gains_wide[1])
     own_normed2 = normed2.astype(jnp.bfloat16)
-    all_n2 = gather_all(own_normed2)
+    row_rounds = gather_rounds(own_normed2)
+
+    router_wide = jnp.pad(router_full, ((0, 0), (0, LANES - n_experts)))
+    place = (
+        jnp.arange(LANES)[None, :] == fsdp_rank * exp_local + jnp.arange(exp_local)[:, None]
+    ).astype(jnp.float32)
+    results = [
+        [
+            expert_rows(rows, grads, router_wide, place, w_gate, w_up, w_down, n_experts)
+            for rows, grads in zip(row_pair, grad_pair)
+        ]
+        for row_pair, grad_pair in zip(row_rounds, grad_rounds)
+    ]
+    token_grad = scatter_rounds([(mine[0], other[0]) for mine, other in results])
+    own_dots = scatter_small([(mine[3], other[3]) for mine, other in results]).T
 
     logits = jnp.dot(own_normed2, router_full, preferred_element_type=jnp.float32)
     router_probs = jax.nn.softmax(logits, axis=-1)
-    own_ids = own_rows(expert_ids)
-    expert_range = jnp.arange(n_experts, dtype=jnp.int32)
-    named = (own_ids[:, :, None] == expert_range[None, None, :]).any(axis=1)
     own_gates = jnp.where(named, router_probs, 0.0)
-    all_gates = gather_all(own_gates)
-    local_gates = lax.dynamic_slice_in_dim(all_gates, fsdp_rank * exp_local, exp_local, 1)
-
-    gate_pre = jnp.einsum("td,edf->tef", all_n2, w_gate, preferred_element_type=jnp.float32)
-    up_pre = jnp.einsum("td,edf->tef", all_n2, w_up, preferred_element_type=jnp.float32)
-    y_down = jnp.einsum("td,efd->tef", all_y, w_down, preferred_element_type=jnp.float32)
-    sigmoid_gate = jax.nn.sigmoid(gate_pre)
-    silu_gate = gate_pre * sigmoid_gate
-    active = silu_gate * up_pre
-    part_dots = jnp.sum(active * y_down, axis=-1)
-    gated_active = (active * local_gates[:, :, None]).astype(jnp.bfloat16)
-    active_grad = y_down * local_gates[:, :, None]
-    gate_grad = (
-        active_grad * up_pre * sigmoid_gate * (1.0 + gate_pre * (1.0 - sigmoid_gate))
-    ).astype(jnp.bfloat16)
-    up_grad = (active_grad * silu_gate).astype(jnp.bfloat16)
-    token_grad = (
-        jnp.einsum("tef,edf->td", gate_grad, w_gate, preferred_element_type=jnp.float32)
-        + jnp.einsum("tef,edf->td", up_grad, w_up, preferred_element_type=jnp.float32)
-    ).astype(jnp.bfloat16)
-    combined = jnp.einsum(
-        "tef,efd->td", gated_active, w_down, preferred_element_type=jnp.float32
-    ).astype(jnp.bfloat16)
-
-    all_dots = lax.all_gather(lax.psum(part_dots.T, "tp"), "fsdp", axis=0, tiled=True)
-    own_dots = lax.dynamic_slice_in_dim(
-        all_dots, (fsdp_rank * tp_count + tp_rank) * local_rows, local_rows, 1
-    ).T
     chosen = jnp.where(named, own_dots, 0.0)
     weighted = jnp.sum(own_gates * chosen, axis=-1, keepdims=True)
     own_logit_grad = (router_probs * (chosen - weighted)).astype(jnp.bfloat16)
 
-    normed2_grad = scatter_all(token_grad).astype(jnp.float32) + jnp.dot(
+    normed2_grad = token_grad + jnp.dot(
         own_logit_grad, router_full.T, preferred_element_type=jnp.float32
     )
     hidden_norm_grad, gain2_grad = norm_backward(hidden, scale2, gains_wide[1], normed2_grad)
     hidden_grad = cotangent.astype(jnp.float32) + hidden_norm_grad
-    hidden_rows = gather_rows(hidden_grad.astype(jnp.bfloat16))
-
-    layer_out = (hidden + scatter_all(combined).astype(jnp.float32)).astype(jnp.bfloat16)
-    grad_down = jnp.einsum("tef,td->efd", gated_active, all_y, preferred_element_type=jnp.float32)
-    grad_gate = jnp.einsum("td,tef->edf", all_n2, gate_grad, preferred_element_type=jnp.float32)
-    grad_up = jnp.einsum("td,tef->edf", all_n2, up_grad, preferred_element_type=jnp.float32)
-    all_logit_grad = gather_all(own_logit_grad)
-    router_rows = w_router.shape[0]
-    router_cols = lax.dynamic_slice_in_dim(
-        all_n2, (fsdp_rank * tp_count + tp_rank) * router_rows, router_rows, 1
-    )
-    grad_router = jnp.einsum(
-        "td,te->de", router_cols, all_logit_grad, preferred_element_type=jnp.float32
-    )
+    hidden_rows = tp_gather(hidden_grad.astype(jnp.bfloat16))
+
+    actives, _ = lax.optimization_barrier(([[half[1] for half in pair] for pair in results], hidden_grad))
+    down_rows = w_down.reshape(exp_local * ff_local, width)
+    combined = scatter_rounds(
+        [
+            [
+                jnp.dot(active, down_rows, preferred_element_type=jnp.float32).astype(jnp.bfloat16)
+                for active in pair
+            ]
+            for pair in actives
+        ]
+    )
+    layer_out = (hidden + combined).astype(jnp.bfloat16)
+
+    all_n2 = jnp.concatenate([half for pair in row_rounds for half in pair], axis=0)
+    all_y = jnp.concatenate([half[:, :width] for pair in grad_rounds for half in pair], axis=0)
+    all_active = jnp.concatenate([half[1] for pair in results for half in pair], axis=0)
+    all_hidden = jnp.concatenate([half[2] for pair in results for half in pair], axis=0)
+
+    def pair_dots(left, right):
+        return lax.dot_general(
+            left, right, (((0,), (0,)), ((), ())), preferred_element_type=jnp.float32
+        )
+
+    def hidden_piece(index):
+        return all_hidden[:, index * ff_local : (index + 1) * ff_local]
+
+    grad_down = pair_dots(all_active, all_y).reshape(exp_local, ff_local, width)
+    grad_gate = jnp.stack([pair_dots(all_n2, hidden_piece(e)) for e in range(exp_local)])
+    grad_up = jnp.stack([pair_dots(all_n2, hidden_piece(exp_local + e)) for e in range(exp_local)])
 
     grad_out_full = jnp.dot(mixed.T, hidden_rows, preferred_element_type=jnp.float32)
     mixed_grad = (
@@ -541,7 +734,7 @@
     ).astype(jnp.bfloat16)
     grad_qkv_full = jnp.einsum("sd,csh->cdh", rows1, qkv_grad, preferred_element_type=jnp.float32)
     normed1_part = jnp.einsum("csh,cdh->sd", qkv_grad, qkv_full, preferred_element_type=jnp.float32)
-    normed1_grad = scatter_rows(normed1_part)
+    normed1_grad = tp_scatter(normed1_part)
     gain1_grad = jnp.sum(normed1_part * (rows_x * scale1), axis=0)
     input_norm_grad, _ = norm_backward(x_own, own_rows(scale1), gains_wide[0], normed1_grad)
     input_grad = hidden_grad + input_norm_grad
@@ -554,19 +747,21 @@
             lax.dynamic_update_slice_in_dim(zero_width, gain_key_grad, col_start, 0),
         ]
     )
+    router_part = pair_dots(own_logit_grad, own_normed2)
+    small_grad = lax.dynamic_slice_in_dim(
+        butterfly_sum(jnp.concatenate([router_part, gains_grad], axis=0)),
+        small_start,
+        small_cols,
+        1,
+    )
+    grad_router = small_grad[:n_experts].T
+    grad_gains = small_grad[n_experts:]
     grad_qkv = lax.psum_scatter(
         grad_qkv_full.astype(jnp.bfloat16), "fsdp", scatter_dimension=1, tiled=True
     ).astype(jnp.float32)
     grad_out = lax.psum_scatter(
         grad_out_full.astype(jnp.bfloat16), "fsdp", scatter_dimension=1, tiled=True
     ).astype(jnp.float32)
-    gain_cols = norm_gains.shape[1]
-    grad_gains = lax.dynamic_slice_in_dim(
-        lax.psum(gains_grad, ("fsdp", "tp")),
-        (fsdp_rank * tp_count + tp_rank) * gain_cols,
-        gain_cols,
-        1,
-    )
     return (
         layer_out,
         input_grad,
@@ -581,9 +776,11 @@
 
 
 def pick_shards(*arguments):
-    n_experts = arguments[8].shape[0] * lax.axis_size("fsdp")
+    fsdp_count, tp_count = lax.axis_size("fsdp"), lax.axis_size("tp")
+    n_experts = arguments[8].shape[0] * fsdp_count
     top_count = arguments[3].shape[1]
-    body = dense_shards if n_experts <= 2 * top_count else shards
+    fits = (fsdp_count, tp_count) == (GRID[0] * GRID[1], GRID[2] * GRID[3])
+    body = dense_shards if fits and n_experts <= 2 * top_count else shards
     return body(*arguments)
 
 

time: 1270 us -> 867 us (0.68)
  waiting for transfers between devices: 729 us -> 359 us
  blocking collectives: 215 us -> 22.1 us
  starting transfers between devices: 1.32 us -> 91.6 us
  matrix products: 204 us -> 114 us
  Pallas kernels: 0 us -> 78.2 us
  local copies, waits for them, and re-layouts: 34.3 us -> 95.7 us
  other arithmetic: 62.4 us -> 80.2 us
    ppermute x0 -> x84, waiting for transfers between devices: none -> 359 us  [send(): return lax.ppermute(values, ('fsdp', 'tp'), pairs)]
    reduce_scatter x4 -> x0, waiting for transfers between devices: 293 us -> none  [the longest x2 261 us: scatter_all(): lax.psum_scatter(values, ('fsdp', 'tp'), scatter_dimension=0, tiled=True)]
    all_gather x4 -> x0, waiting for transfers between devices: 219 us -> none  [the longest x2 197 us: gather_all(): return lax.all_gather(values, ('fsdp', 'tp'), axis=axis, tiled=True)]
    all_gather x4 -> x0, blocking collectives: 142 us -> none  [the longest x3 119 us: gather_all(): return lax.all_gather(values, ('fsdp', 'tp'), axis=axis, tiled=True)]
    reduce_scatter x1, waiting for transfers between devices: 117 us -> 0.01 us  [dense_shards(): lax.psum_scatter(grad_qkv_full.astype(jnp.bfloat16), 'fsdp', scatter_dime...]
    ppermute x0 -> x84, starting transfers between devices: none -> 91.5 us  [send(): return lax.ppermute(values, ('fsdp', 'tp'), pairs)]
    dot_general x10 -> x14, matrix products: 157 us -> 71.5 us  [the longest x6 53 us: pair_dots(): lax.dot_general(left, right, (((0,), (0,)), ((), ())), preferred_element_...]
    all_gather x1, waiting for transfers between devices: 81.1 us -> 0.01 us  [dense_shards(): qkv_full = lax.all_gather(w_qkv, 'fsdp', axis=1, tiled=True)]
  transfers between devices with their start and end apart: 12 -> 88, of which waited for: 9 -> 33; matrix products, arithmetic and copies ran while one was open for 15% -> 31% of each run, Pallas kernels for 0% -> 9%
where the time goes in v2:
time: 867 us; the launch traced here: 857 us
  waiting for transfers between devices  359 us (41%)
  matrix products  114 us (13%)
  local copies, waits for them, and re-layouts  95.7 us (11%)
  starting transfers between devices  91.6 us (11%)
  other arithmetic  80.2 us (9%)
  Pallas kernels  78.2 us (9%)
  blocking collectives  22.1 us (3%)
  between operations  16 us (2%)
    ppermute x84, waiting for transfers between devices, send(): return lax.ppermute(values, ('fsdp', 'tp'), pairs)  359 us
    ppermute x84, starting transfers between devices, send(): return lax.ppermute(values, ('fsdp', 'tp'), pairs)  91.5 us
    pallas_call x8, Pallas kernels, expert_rows(): pl.pallas_call(functools.partial(expert_kernel, n_experts=n_experts), out...  78.2 us
    unnamed x265, local copies, waits for them, and re-layouts  69.6 us
    dot_general x6, matrix products, pair_dots(): lax.dot_general(left, right, (((0,), (0,)), ((), ())), preferred_element_...  53 us
    convert_element_type x24, other arithmetic, add_low(): sum((term.astype(jnp.float32) for term in terms)).astype(jnp.bfloat16)  27.4 us
    psum x2, blocking collectives, tp_totals(): return lax.psum((first, second), 'tp')  22.1 us
    dot_general x8, matrix products, dense_shards(): jnp.dot(active, down_rows, preferred_element_type=jnp.float32)  18.4 us
  transfers between devices with their start and end apart: 88, of which 33 were waited for; matrix products, arithmetic and copies ran while one was open for 31% of the time, Pallas kernels for 9%

profile of v2, /device:TPU:9, one launch (start us, length us, event | category | flops | bytes accessed | tf_op | source)
XLA Modules:
  0.0 857.2 jit_solution(1717138282976794026)
XLA Ops:
  18.5 23.8 %collective-permute-done.3 = bf16[20,2048]{0,1:T(8,128)(2,1)S(1)} collective-permute-done((bf16[20,2048]{0,1:T(8,128)(2,1)S(1)}, bf16[20,2048]{0,1:T(8,128)(2,1)S(1)}, u32[]{:S(2)}, u32[]{:S(2)}) %collective-permute-start.3) | collective-permute-done | bytes 81952 | tf_op jit(solution)/shard_map/ppermute | solution.py:395
  44.7 10.4 %collective-permute-done.4 = bf16[20,2048]{0,1:T(8,128)(2,1)} collective-permute-done((bf16[20,2048]{0,1:T(8,128)(2,1)S(1)}, bf16[20,2048]{0,1:T(8,128)(2,1)}, u32[]{:S(2)}, u32[]{:S(2)}) %collective-permute-start.4) | collective-permute-done | bytes 81952 | tf_op jit(solution)/shard_map/ppermute | solution.py:395
  56.8 28.6 %collective-permute-done.5 = bf16[20,2048]{0,1:T(8,128)(2,1)S(1)} collective-permute-done((bf16[20,2048]{0,1:T(8,128)(2,1)S(1)}, bf16[20,2048]{0,1:T(8,128)(2,1)S(1)}, u32[]{:S(2)}, u32[]{:S(2)}) %collective-permute-start.5) | collective-permute-done | bytes 81952 | tf_op jit(solution)/shard_map/ppermute | solution.py:395
  87.8 50.7 %collective-permute-done.6 = bf16[20,2048]{0,1:T(8,128)(2,1)} collective-permute-done((bf16[20,2048]{0,1:T(8,128)(2,1)S(1)}, bf16[20,2048]{0,1:T(8,128)(2,1)}, u32[]{:S(2)}, u32[]{:S(2)}) %collective-permute-start.6) | collective-permute-done | bytes 81952 | tf_op jit(solution)/shard_map/ppermute | solution.py:395
  147.5 11.0 %collective-permute-done.19 = bf16[128,2176]{1,0:T(8,128)(2,1)S(1)} collective-permute-done((bf16[128,2176]{1,0:T(8,128)(2,1)S(1)}, bf16[128,2176]{1,0:T(8,128)(2,1)S(1)}, u32[]{:S(2)}, u32[]{:S(2)}) %collective-permute-start.19) | collective-permute-done | bytes 557088 | tf_op jit(solution)/shard_map/ppermute | solution.py:395
  215.6 16.6 %all-reduce.3 = (f32[512]{0:T(512)}, f32[512]{0:T(512)}) all-reduce(f32[512]{0:T(512)} %get-tuple-element.141, f32[512]{0:T(512)S(1)} %get-tuple-element.140), channel_id=1, replica_groups=mesh['fsdp'=8,'tp'=4] {'tp'}, use_global_device_ids=true, to_apply=%region_4.5 | all-reduce | flops 1024 | bytes 8192 | tf_op jit(solution)/shard_map/psum | solution.py:90
  261.6 9.7 %collective-permute-done.8 = bf16[128,2048]{1,0:T(8,128)(2,1)S(1)} collective-permute-done((bf16[128,2048]{1,0:T(8,128)(2,1)S(1)}, bf16[128,2048]{1,0:T(8,128)(2,1)S(1)}, u32[]{:S(2)}, u32[]{:S(2)}) %collective-permute-start.8) | collective-permute-done | bytes 524320 | tf_op jit(solution)/shard_map/ppermute | solution.py:395
  305.5 14.1 %collective-permute-done.23 = bf16[128,2048]{1,0:T(8,128)(2,1)S(1)} collective-permute-done((bf16[128,2048]{1,0:T(8,128)(2,1)S(1)}, bf16[128,2048]{1,0:T(8,128)(2,1)S(1)}, u32[]{:S(2)}, u32[]{:S(2)}) %collective-permute-start.23) | collective-permute-done | bytes 524320 | tf_op jit(solution)/shard_map/ppermute | solution.py:395
  358.4 10.8 %expert_rows.9 = (bf16[512,2048]{1,0:T(8,128)(2,1)}, bf16[512,512]{1,0:T(8,128)(2,1)S(1)}, bf16[512,1024]{1,0:T(8,128)(2,1)S(1)}, f32[16,512]{1,0:T(8,128)S(1)}) custom-call(bf16[512,2048]{1,0:T(8,128)(2,1)S(1)} %collective-permute-done.13.rows_ref, bf16[512,2176]{1,0:T(8,128)(2,1)} %collective-permute-done.14.grads_ref, ...), custom_call_target="tpu_custom_call" | custom-call | flops 5368709120 | bytes 14155776 | tf_op jit(solution)/shard_map/expert_rows/pallas_call | solution.py:536
  370.5 9.7 %expert_rows.10 = (bf16[512,2048]{1,0:T(8,128)(2,1)S(1)}, bf16[512,512]{1,0:T(8,128)(2,1)S(1)}, bf16[512,1024]{1,0:T(8,128)(2,1)S(1)}, f32[16,512]{1,0:T(8,128)S(1)}) custom-call(bf16[512,2048]{1,0:T(8,128)(2,1)} %get-tuple-element.179.rows_ref, bf16[512,2176]{1,0:T(8,128)(2,1)} %constant_dynamic-update-slice_fusion.3.grads_ref, ...), custom_call_target="tpu_custom_call" | custom-call | flops 5368709120 | bytes 14155776 | tf_op jit(solution)/shard_map/expert_rows/pallas_call | solution.py:536
  390.2 9.5 %expert_rows.11 = (bf16[512,2048]{1,0:T(8,128)(2,1)S(1)}, bf16[512,512]{1,0:T(8,128)(2,1)S(1)}, bf16[512,1024]{1,0:T(8,128)(2,1)S(1)}, f32[16,512]{1,0:T(8,128)S(1)}) custom-call(bf16[512,2048]{1,0:T(8,128)(2,1)S(1)} %collective-permute-done.21.rows_ref, bf16[512,2176]{1,0:T(8,128)(2,1)} %collective-permute-done.22.grads_ref, ...), custom_call_target="tpu_custom_call" | custom-call | flops 5368709120 | bytes 14155776 | tf_op jit(solution)/shard_map/expert_rows/pallas_call | solution.py:536
  402.7 9.7 %expert_rows.12 = (bf16[512,2048]{1,0:T(8,128)(2,1)S(1)}, bf16[512,512]{1,0:T(8,128)(2,1)S(1)}, bf16[512,1024]{1,0:T(8,128)(2,1)S(1)}, f32[16,512]{1,0:T(8,128)S(1)}) custom-call(bf16[512,2048]{1,0:T(8,128)(2,1)} %get-tuple-element.177.rows_ref, bf16[512,2176]{1,0:T(8,128)(2,1)} %copy-done.50, bf16[2048,128]{1,0:T(8,128)(2,1)S(1)} %copy-done.15, ...), custom_call_target="tpu_custom_call" | custom-call | flops 5368709120 | bytes 14155776 | tf_op jit(solution)/shard_map/expert_rows/pallas_call | solution.py:536
  429.3 10.5 %expert_rows.13 = (bf16[512,2048]{1,0:T(8,128)(2,1)}, bf16[512,512]{1,0:T(8,128)(2,1)S(1)}, bf16[512,1024]{1,0:T(8,128)(2,1)S(1)}, f32[16,512]{1,0:T(8,128)S(1)}) custom-call(bf16[512,2048]{1,0:T(8,128)(2,1)S(1)} %collective-permute-done.29.rows_ref, bf16[512,2176]{1,0:T(8,128)(2,1)} %copy-done.76, bf16[2048,128]{1,0:T(8,128)(2,1)S(1)} %copy-done.16, ...), custom_call_target="tpu_custom_call" | custom-call | flops 5368709120 | bytes 14155776 | tf_op jit(solution)/shard_map/expert_rows/pallas_call | solution.py:536
  439.9 9.9 %expert_rows.14 = (bf16[512,2048]{1,0:T(8,128)(2,1)S(1)}, bf16[512,512]{1,0:T(8,128)(2,1)S(1)}, bf16[512,1024]{1,0:T(8,128)(2,1)S(1)}, f32[16,512]{1,0:T(8,128)S(1)}) custom-call(bf16[512,2048]{1,0:T(8,128)(2,1)} %get-tuple-element.175.rows_ref, bf16[512,2176]{1,0:T(8,128)(2,1)} %constant_dynamic-update-slice_fusion.15.grads_ref, ...), custom_call_target="tpu_custom_call" | custom-call | flops 5368709120 | bytes 14155776 | tf_op jit(solution)/shard_map/expert_rows/pallas_call | solution.py:536
  479.2 15.2 %fusion.64 = f32[512,2048]{1,0:T(8,128)} fusion(bf16[4096,512]{1,0:T(8,128)(2,1)} %constant_dynamic-update-slice_fusion.42, bf16[4096,2048]{1,0:T(8,128)(2,1)} %slice_dynamic-update-slice_fusion), kind=kOutput, calls=%fused_computation.277 | convolution fusion | flops 8589934592 | bytes 25165824 | tf_op jit(solution)/shard_map/dot_general | solution.py:690
  542.1 9.7 %collective-permute-done.49 = bf16[128,2048]{1,0:T(8,128)(2,1)S(1)} collective-permute-done((bf16[128,2048]{1,0:T(8,128)(2,1)S(1)}, bf16[128,2048]{1,0:T(8,128)(2,1)S(1)}, u32[]{:S(2)}, u32[]{:S(2)}) %collective-permute-start.49) | collective-permute-done | bytes 524320 | tf_op jit(solution)/shard_map/ppermute | solution.py:395
  551.8 11.2 %collective-permute-done.53 = bf16[128,2048]{1,0:T(8,128)(2,1)S(1)} collective-permute-done((bf16[128,2048]{1,0:T(8,128)(2,1)S(1)}, bf16[128,2048]{1,0:T(8,128)(2,1)S(1)}, u32[]{:S(2)}, u32[]{:S(2)}) %collective-permute-start.53) | collective-permute-done | bytes 524320 | tf_op jit(solution)/shard_map/ppermute | solution.py:395
  567.5 9.8 %convolution_bitcast_fusion = f32[1,2048,256]{2,1,0:T(8,128)} fusion(bf16[4096,2048]{1,0:T(8,128)(2,1)} %constant_dynamic-update-slice_fusion.18, bf16[4096,1024]{1,0:T(8,128)(2,1)S(1)} %bitcast.233), kind=kOutput, calls=%fused_computation.25 | convolution fusion | flops 4294967296 | bytes 20971520 | tf_op jit(solution)/shard_map/dot_general | solution.py:690
  582.6 9.9 %convolution_bitcast_fusion.1 = f32[1,2048,256]{2,1,0:T(8,128)} fusion(bf16[4096,2048]{1,0:T(8,128)(2,1)} %constant_dynamic-update-slice_fusion.18, bf16[4096,1024]{1,0:T(8,128)(2,1)S(1)} %bitcast.233), kind=kOutput, calls=%fused_computation.26 | convolution fusion | flops 4294967296 | bytes 20971520 | tf_op jit(solution)/shard_map/dot_general | solution.py:690
  705.7 18.2 %collective-permute-done.83 = f32[20,2048]{1,0:T(8,128)S(1)} collective-permute-done((f32[20,2048]{1,0:T(8,128)S(1)}, f32[20,2048]{1,0:T(8,128)S(1)}, u32[]{:S(2)}, u32[]{:S(2)}) %collective-permute-start.83) | collective-permute-done | bytes 163872 | tf_op jit(solution)/shard_map/ppermute | solution.py:395
  732.0 9.4 %collective-permute-done.64 = bf16[256,2048]{1,0:T(8,128)(2,1)S(1)} collective-permute-done((bf16[256,2048]{1,0:T(8,128)(2,1)S(1)}, bf16[256,2048]{1,0:T(8,128)(2,1)S(1)}, u32[]{:S(2)}, u32[]{:S(2)}) %collective-permute-start.64) | collective-permute-done | bytes 1048608 | tf_op jit(solution)/shard_map/ppermute | solution.py:395
  742.8 37.3 %collective-permute-done.61 = bf16[256,2048]{1,0:T(8,128)(2,1)S(1)} collective-permute-done((bf16[256,2048]{1,0:T(8,128)(2,1)S(1)}, bf16[256,2048]{1,0:T(8,128)(2,1)S(1)}, u32[]{:S(2)}, u32[]{:S(2)}) %collective-permute-start.61) | collective-permute-done | bytes 1048608 | tf_op jit(solution)/shard_map/ppermute | solution.py:395
  788.8 32.0 %collective-permute-done.74 = bf16[128,2048]{1,0:T(8,128)(2,1)S(1)} collective-permute-done((bf16[128,2048]{1,0:T(8,128)(2,1)S(1)}, bf16[128,2048]{1,0:T(8,128)(2,1)S(1)}, u32[]{:S(2)}, u32[]{:S(2)}) %collective-permute-start.74) | collective-permute-done | bytes 524320 | tf_op jit(solution)/shard_map/ppermute | solution.py:395
  820.8 19.6 %collective-permute-done.70 = bf16[128,2048]{1,0:T(8,128)(2,1)S(1)} collective-permute-done((bf16[128,2048]{1,0:T(8,128)(2,1)S(1)}, bf16[128,2048]{1,0:T(8,128)(2,1)S(1)}, u32[]{:S(2)}, u32[]{:S(2)}) %collective-permute-start.70) | collective-permute-done | bytes 524320 | tf_op jit(solution)/shard_map/ppermute | solution.py:395
  (597 shorter events, 444.0 us)
Async XLA Ops:
  7.2 193.7 %all-gather.3.cloned.1.call-start = ((), (), s32[]{:S(2)}) async-start(), calls=%async_computation.2 | async-start | bytes 7077888 | tf_op jit(solution)/shard_map/all_gather | solution.py:585
  9.7 236.3 %all-gather.5.cloned.1.call-start = ((), (), s32[]{:S(2)}) async-start(), calls=%async_computation.3 | async-start | bytes 2359296 | tf_op jit(solution)/shard_map/all_gather | solution.py:586
  10.8 135.0 %collective-permute-start.11 = (bf16[128,2176]{1,0:T(8,128)(2,1)}, bf16[128,2176]{1,0:T(8,128)(2,1)S(1)}, u32[]{:S(2)}, u32[]{:S(2)}) collective-permute-start(bf16[128,2176]{1,0:T(8,128)(2,1)} %pad_maximum_fusion.20), channel_id=1, source_target_pairs={{0,4},{1,3},{2,6},{3,1},{4,0},{5,7},{6,2},{7,5},{8,12},{9,11},{10,... | collective-permute-start | bytes 1671176 | tf_op jit(solution)/shard_map/ppermute | solution.py:395
  12.1 132.6 %collective-permute-start.18 = (bf16[128,2176]{1,0:T(8,128)(2,1)}, bf16[128,2176]{1,0:T(8,128)(2,1)S(1)}, u32[]{:S(2)}, u32[]{:S(2)}) collective-permute-start(bf16[128,2176]{1,0:T(8,128)(2,1)} %pad_maximum_fusion.20), channel_id=1, source_target_pairs={{0,8},{1,9},{2,10},{3,11},{4,12},{5,13},{6,14},{7,15},{8,16},{9,17... | collective-permute-start | bytes 1671176 | tf_op jit(solution)/shard_map/ppermute | solution.py:395
  13.3 129.6 %collective-permute-start = (bf16[128,2048]{1,0:T(8,128)(2,1)S(1)}, bf16[128,2048]{1,0:T(8,128)(2,1)}, u32[]{:S(2)}, u32[]{:S(2)}) collective-permute-start(bf16[128,2048]{1,0:T(8,128)(2,1)S(1)} %copy-done.41), channel_id=1, source_target_pairs={{0,2},{1,3},{2,0},{3,1},{4,6},{5,7},{6,4},{7,5},{8,10},{9,11},{10,... | collective-permute-start | bytes 1572872 | tf_op jit(solution)/shard_map/ppermute | solution.py:395
  16.4 829.5 %reduce-scatter.5.cloned.1.call-start = ((), (), s32[]{:S(2)}) async-start(), calls=%async_computation.5 | async-start | bytes 2359296 | tf_op jit(solution)/shard_map/reduce_scatter | solution.py:762
  85.6 53.0 %collective-permute-start.6 = (bf16[20,2048]{0,1:T(8,128)(2,1)S(1)}, bf16[20,2048]{0,1:T(8,128)(2,1)}, u32[]{:S(2)}, u32[]{:S(2)}) collective-permute-start(bf16[20,2048]{0,1:T(8,128)(2,1)S(1)} %add.390), channel_id=1, source_target_pairs={{0,16},{1,17},{2,18},{3,19},{4,20},{5,21},{6,22},{7,23},{8,24},{9,... | collective-permute-start | bytes 245768 | tf_op jit(solution)/shard_map/ppermute | solution.py:395
  169.7 85.1 %collective-permute-start.14 = (bf16[512,2176]{1,0:T(8,128)(2,1)S(1)}, bf16[512,2176]{1,0:T(8,128)(2,1)}, u32[]{:S(2)}, u32[]{:S(2)}) collective-permute-start(bf16[512,2176]{1,0:T(8,128)(2,1)S(1)} %pad_maximum_fusion.2.grads_ref), channel_id=1, source_target_pairs={{0,1},{1,0},{2,3},{3,2},{4,5},{5,4},{6,7},{7,6},{8,9},{9,8},{10,11... | collective-permute-start | bytes 6684680 | tf_op jit(solution)/shard_map/ppermute | solution.py:395
  180.0 70.2 %collective-permute-start.28 = (bf16[256,2176]{1,0:T(8,128)(2,1)}, bf16[256,2176]{1,0:T(8,128)(2,1)}, u32[]{:S(2)}, u32[]{:S(2)}) collective-permute-start(bf16[256,2176]{1,0:T(8,128)(2,1)} %pad_maximum_fusion.8), channel_id=1, source_target_pairs={{0,2},{1,5},{2,0},{3,7},{4,6},{5,1},{6,4},{7,3},{8,10},{9,13},{10,... | collective-permute-start | bytes 3342344 | tf_op jit(solution)/shard_map/ppermute | solution.py:395
  187.9 84.9 %collective-permute-start.22 = (bf16[512,2176]{1,0:T(8,128)(2,1)}, bf16[512,2176]{1,0:T(8,128)(2,1)}, u32[]{:S(2)}, u32[]{:S(2)}) collective-permute-start(bf16[512,2176]{1,0:T(8,128)(2,1)} %constant_dynamic-update-slice_fusion.3.grads_ref), channel_id=1, source_target_pairs={{0,1},{1,0},{2,3},{3,2},{4,5},{5,4},{6,7},{7,6},{8,9},{9,8},{10,11... | collective-permute-start | bytes 6684680 | tf_op jit(solution)/shard_map/ppermute | solution.py:395
  197.9 53.9 %collective-permute-start.36 = (bf16[256,2176]{1,0:T(8,128)(2,1)}, bf16[256,2176]{1,0:T(8,128)(2,1)}, u32[]{:S(2)}, u32[]{:S(2)}) collective-permute-start(bf16[256,2176]{1,0:T(8,128)(2,1)} %pad_maximum_fusion.9), channel_id=1, source_target_pairs={{0,2},{1,5},{2,0},{3,7},{4,6},{5,1},{6,4},{7,3},{8,10},{9,13},{10,... | collective-permute-start | bytes 3342344 | tf_op jit(solution)/shard_map/ppermute | solution.py:395
  254.8 48.3 %collective-permute-start.38 = (bf16[512,2176]{1,0:T(8,128)(2,1)}, bf16[512,2176]{1,0:T(8,128)(2,1)S(1)}, u32[]{:S(2)}, u32[]{:S(2)}) collective-permute-start(bf16[512,2176]{1,0:T(8,128)(2,1)} %constant_dynamic-update-slice_fusion.15.grads_ref), channel_id=1, source_target_pairs={{0,1},{1,0},{2,3},{3,2},{4,5},{5,4},{6,7},{7,6},{8,9},{9,8},{10,11... | collective-permute-start | bytes 6684680 | tf_op jit(solution)/shard_map/ppermute | solution.py:395
  330.4 56.7 %collective-permute-start.25 = (bf16[256,2048]{1,0:T(8,128)(2,1)}, bf16[256,2048]{1,0:T(8,128)(2,1)}, u32[]{:S(2)}, u32[]{:S(2)}) collective-permute-start(bf16[256,2048]{1,0:T(8,128)(2,1)} %pad_maximum_fusion.13), channel_id=1, source_target_pairs={{0,2},{1,5},{2,0},{3,7},{4,6},{5,1},{6,4},{7,3},{8,10},{9,13},{10,... | collective-permute-start | bytes 3145736 | tf_op jit(solution)/shard_map/ppermute | solution.py:395
  357.4 67.7 %collective-permute-start.33 = (bf16[256,2048]{1,0:T(8,128)(2,1)}, bf16[256,2048]{1,0:T(8,128)(2,1)}, u32[]{:S(2)}, u32[]{:S(2)}) collective-permute-start(bf16[256,2048]{1,0:T(8,128)(2,1)} %pad_maximum_fusion.14), channel_id=1, source_target_pairs={{0,2},{1,5},{2,0},{3,7},{4,6},{5,1},{6,4},{7,3},{8,10},{9,13},{10,... | collective-permute-start | bytes 3145736 | tf_op jit(solution)/shard_map/ppermute | solution.py:395
  417.6 124.5 %collective-permute-start.41 = (bf16[128,2048]{1,0:T(8,128)(2,1)}, bf16[128,2048]{1,0:T(8,128)(2,1)S(1)}, u32[]{:S(2)}, u32[]{:S(2)}) collective-permute-start(bf16[128,2048]{1,0:T(8,128)(2,1)} %add_convert_fusion.22), channel_id=1, source_target_pairs={{0,4},{1,3},{2,6},{3,1},{4,0},{5,7},{6,2},{7,5},{8,12},{9,11},{10,... | collective-permute-start | bytes 1572872 | tf_op jit(solution)/shard_map/ppermute | solution.py:395
  461.3 80.8 %collective-permute-start.45 = (bf16[128,2048]{1,0:T(8,128)(2,1)S(1)}, bf16[128,2048]{1,0:T(8,128)(2,1)S(1)}, u32[]{:S(2)}, u32[]{:S(2)}) collective-permute-start(bf16[128,2048]{1,0:T(8,128)(2,1)S(1)} %add_convert_fusion.20), channel_id=1, source_target_pairs={{0,24},{1,25},{2,26},{3,27},{4,28},{5,29},{6,30},{7,31},{8,0},{9,1... | collective-permute-start | bytes 1572872 | tf_op jit(solution)/shard_map/ppermute | solution.py:395
  603.2 244.5 %reduce-scatter.3.cloned.1.call-start = ((), (), s32[]{:S(2)}) async-start(), calls=%async_computation.4 | async-start | bytes 7077888 | tf_op jit(solution)/shard_map/reduce_scatter | solution.py:759
  680.0 46.8 %collective-permute-start.77 = (bf16[2,128,2048]{2,1,0:T(8,128)(2,1)S(1)}, bf16[2,128,2048]{2,1,0:T(8,128)(2,1)S(1)}, u32[]{:S(2)}, u32[]{:S(2)}) collective-permute-start(bf16[2,128,2048]{2,1,0:T(8,128)(2,1)S(1)} %dynamic-slice_bitcast_fusion), channel_id=1, source_target_pairs={{0,1},{1,0},{2,3},{3,2},{4,5},{5,4},{6,7},{7,6},{8,9},{9,8},{10,11... | collective-permute-start | bytes 3145736 | tf_op jit(solution)/shard_map/ppermute | solution.py:395
  723.9 56.3 %collective-permute-start.61 = (bf16[256,2048]{1,0:T(8,128)(2,1)S(1)}, bf16[256,2048]{1,0:T(8,128)(2,1)S(1)}, u32[]{:S(2)}, u32[]{:S(2)}) collective-permute-start(bf16[256,2048]{1,0:T(8,128)(2,1)S(1)} %add_convert_fusion.3), channel_id=1, source_target_pairs={{0,2},{1,5},{2,0},{3,7},{4,6},{5,1},{6,4},{7,3},{8,10},{9,13},{10,... | collective-permute-start | bytes 3145736 | tf_op jit(solution)/shard_map/ppermute | solution.py:395
  726.9 53.6 %collective-permute-start.78 = (bf16[128,2048]{1,0:T(8,128)(2,1)S(1)}, bf16[128,2048]{1,0:T(8,128)(2,1)S(1)}, u32[]{:S(2)}, u32[]{:S(2)}) collective-permute-start(bf16[128,2048]{1,0:T(8,128)(2,1)S(1)} %fusion.24), channel_id=1, source_target_pairs={{0,2},{1,3},{2,0},{3,1},{4,6},{5,7},{6,4},{7,5},{8,10},{9,11},{10,... | collective-permute-start | bytes 1572872 | tf_op jit(solution)/shard_map/ppermute | solution.py:395
  729.1 51.9 %collective-permute-start.73 = (bf16[128,2048]{1,0:T(8,128)(2,1)S(1)}, bf16[128,2048]{1,0:T(8,128)(2,1)S(1)}, u32[]{:S(2)}, u32[]{:S(2)}) collective-permute-start(bf16[128,2048]{1,0:T(8,128)(2,1)S(1)} %add_convert_fusion.10), channel_id=1, source_target_pairs={{0,4},{1,3},{2,6},{3,1},{4,0},{5,7},{6,2},{7,5},{8,12},{9,11},{10,... | collective-permute-start | bytes 1572872 | tf_op jit(solution)/shard_map/ppermute | solution.py:395
  731.1 51.3 %collective-permute-start.69 = (bf16[128,2048]{1,0:T(8,128)(2,1)S(1)}, bf16[128,2048]{1,0:T(8,128)(2,1)S(1)}, u32[]{:S(2)}, u32[]{:S(2)}) collective-permute-start(bf16[128,2048]{1,0:T(8,128)(2,1)S(1)} %add_convert_fusion.12), channel_id=1, source_target_pairs={{0,4},{1,3},{2,6},{3,1},{4,0},{5,7},{6,2},{7,5},{8,12},{9,11},{10,... | collective-permute-start | bytes 1572872 | tf_op jit(solution)/shard_map/ppermute | solution.py:395
  783.9 56.4 %collective-permute-start.70 = (bf16[128,2048]{1,0:T(8,128)(2,1)S(1)}, bf16[128,2048]{1,0:T(8,128)(2,1)S(1)}, u32[]{:S(2)}, u32[]{:S(2)}) collective-permute-start(bf16[128,2048]{1,0:T(8,128)(2,1)S(1)} %add_convert_fusion.11), channel_id=1, source_target_pairs={{0,16},{1,17},{2,18},{3,19},{4,20},{5,21},{6,22},{7,23},{8,24},{9,... | collective-permute-start | bytes 1572872 | tf_op jit(solution)/shard_map/ppermute | solution.py:395
  785.4 59.0 %collective-permute-start.66 = (bf16[128,2048]{1,0:T(8,128)(2,1)S(1)}, bf16[128,2048]{1,0:T(8,128)(2,1)S(1)}, u32[]{:S(2)}, u32[]{:S(2)}) collective-permute-start(bf16[128,2048]{1,0:T(8,128)(2,1)S(1)} %add_convert_fusion.13), channel_id=1, source_target_pairs={{0,24},{1,25},{2,26},{3,27},{4,28},{5,29},{6,30},{7,31},{8,0},{9,1... | collective-permute-start | bytes 1572872 | tf_op jit(solution)/shard_map/ppermute | solution.py:395
  (175 other events, 3172.5 us)
Sparse Core Ops, SparseCore 0:
  10.7 134.4 all-gather.2
  147.2 73.6 all-gather.4
  603.3 66.3 reduce-scatter.4
  673.2 166.0 reduce-scatter.2

commit v3 on v0

--- a/solution.py
+++ b/solution.py
@@ -1,6 +1,12 @@
+import functools
+import itertools
+
 import jax
 import jax.numpy as jnp
 from jax import lax
+from jax.experimental import pallas as pl
+from jax.experimental.pallas import tpu as pltpu
+from jax.sharding import Mesh
 from jax.sharding import PartitionSpec as P
 
 HD = 128
@@ -360,35 +366,702 @@
     )
 
 
+GRID = (4, 2, 2, 2)
+FINE = ("z", "x", "y", "core")
+LANES = 128
+CONTRACT_LAST = (((1,), (1,)), ((), ()))
+
+
+def permutation(target):
+    def place(z, x, y, c):
+        return ((z * GRID[1] + x) * GRID[2] + y) * GRID[3] + c
+
+    return [
+        (place(*at), place(*target(*at))) for at in itertools.product(*(range(n) for n in GRID))
+    ]
+
+
+SWAP_CORE = permutation(lambda z, x, y, c: (z, x, y, 1 - c))
+SWAP_X = permutation(lambda z, x, y, c: (z, 1 - x, y, c))
+SWAP_Y = permutation(lambda z, x, y, c: (z, x, 1 - y, c))
+SWAP_BOTH = permutation(lambda z, x, y, c: (z, x, 1 - y, 1 - c))
+SWAP_FIRST = permutation(lambda z, x, y, c: (z, 1 - x, y, c) if c == 0 else (z, x, 1 - y, c))
+SWAP_SECOND = permutation(lambda z, x, y, c: (z, x, 1 - y, c) if c == 0 else (z, 1 - x, y, c))
+
+
+def shift_z(steps):
+    return permutation(lambda z, x, y, c: ((z + steps) % GRID[0], x, y, c))
+
+
+def send(values, pairs):
+    return lax.ppermute(values, FINE, pairs)
+
+
+def add_low(*terms):
+    return sum(term.astype(jnp.float32) for term in terms).astype(jnp.bfloat16)
+
+
+def side_totals(first, second):
+    return lax.psum((first, second), FINE[2:])
+
+
+def fence(*values):
+    return lax.optimization_barrier(values)
+
+
+def wide_sum(*terms):
+    return sum(term.astype(jnp.float32) for term in terms)
+
+
+def pair_dots(left, right):
+    return lax.dot_general(left, right, (((0,), (0,)), ((), ())), preferred_element_type=jnp.float32)
+
+
+def side_pair(own, far):
+    is_far = lax.axis_index("y") == 1
+    return jnp.stack([jnp.where(is_far, far, own), jnp.where(is_far, own, far)])
+
+
+def four_rows(mine, theirs):
+    is_second = lax.axis_index("core") == 1
+    both = jnp.stack(
+        [jnp.where(is_second, theirs, mine), jnp.where(is_second, mine, theirs)], axis=1
+    )
+    return both.reshape(4 * mine.shape[1], *mine.shape[2:])
+
+
+def core_split(values):
+    core = lax.axis_index("core")
+    blocks = values.astype(jnp.bfloat16).reshape(2, 2, values.shape[0] // 4, values.shape[1])
+    return (
+        lax.dynamic_index_in_dim(blocks, 1 - core, 1, keepdims=False),
+        lax.dynamic_index_in_dim(blocks, core, 1, keepdims=False),
+    )
+
+
+def side_split(mine, back):
+    side = lax.axis_index("y")
+
+    def at(pair, which):
+        return lax.dynamic_index_in_dim(pair, which, 0, keepdims=False)
+
+    away = add_low(at(mine, 1 - side), at(back, 1 - side))
+    return (away, wide_sum(at(mine, side), at(back, side)))
+
+
+def expert_kernel(blocks_ref, near_ref, far_ref, *refs, n_experts):
+    grad_block_refs, (router_ref, place_ref), own, other = refs[:4], refs[4:6], refs[6:9], refs[9:12]
+    outputs, (gates_ref, dots_sum_ref, route_ref) = refs[-10:-3], refs[-3:]
+    near_route_ref, far_route_ref, active_ref, hidden_ref, dots_ref, grads_ref, rows_ref = outputs
+    _, width, units = own[0].shape
+    exp_local = place_ref.shape[0]
+    half = near_ref.shape[0]
+    step = pl.program_id(0)
+
+    @pl.when(step == 0)
+    def _():
+        rows_ref[:half] = near_ref[...]
+        rows_ref[half:] = far_ref[...]
+        quarter = half // 2
+        for at, ref in enumerate(grad_block_refs):
+            grads_ref[at * quarter : (at + 1) * quarter] = ref[:, :width]
+        named = jnp.concatenate([ref[:, width:] for ref in grad_block_refs], axis=0)
+        lane = lax.broadcasted_iota(jnp.int32, (1, LANES), 1)
+        logits = jnp.dot(rows_ref[...], router_ref[...], preferred_element_type=jnp.float32)
+        logits = jnp.where(lane < n_experts, logits, NEG_FILL)
+        powered = jnp.exp(logits - jnp.max(logits, axis=-1, keepdims=True))
+        total = jnp.sum(powered, axis=-1, keepdims=True)
+        gates_ref[...] = powered / total * named.astype(jnp.float32)
+        dots_sum_ref[...] = jnp.zeros_like(dots_sum_ref)
+        route_ref[...] = jnp.zeros_like(route_ref)
+
+    def expert(place, gate_ref, up_ref, down_ref):
+        rows = rows_ref[...]
+        gate = jnp.sum(gates_ref[...] * place, axis=-1, keepdims=True)
+        gate_pre = jnp.dot(rows, gate_ref[0], preferred_element_type=jnp.float32)
+        up_pre = jnp.dot(rows, up_ref[0], preferred_element_type=jnp.float32)
+        y_down = lax.dot_general(
+            grads_ref[...], down_ref[0], CONTRACT_LAST, preferred_element_type=jnp.float32
+        )
+        sigmoid = 1.0 / (1.0 + jnp.exp(-gate_pre))
+        silu = gate_pre * sigmoid
+        active = silu * up_pre
+        dots_sum_ref[...] += jnp.sum(active * y_down, axis=-1, keepdims=True) * place
+        active_ref[...] = (active * gate).astype(jnp.bfloat16)
+        active_grad = y_down * gate
+        gate_grad = (active_grad * up_pre * sigmoid * (1.0 + gate_pre * (1.0 - sigmoid))).astype(
+            jnp.bfloat16
+        )
+        up_grad = (active_grad * silu).astype(jnp.bfloat16)
+        hidden_ref[:, :units] = gate_grad
+        hidden_ref[:, units:] = up_grad
+        route_ref[...] += lax.dot_general(
+            gate_grad, gate_ref[0], CONTRACT_LAST, preferred_element_type=jnp.float32
+        ) + lax.dot_general(
+            up_grad, up_ref[0], CONTRACT_LAST, preferred_element_type=jnp.float32
+        )
+
+    place = place_ref[pl.ds(step % exp_local, 1), :]
+
+    @pl.when(step < exp_local)
+    def _():
+        expert(place, *own)
+
+    @pl.when(step >= exp_local)
+    def _():
+        expert(place, *other)
+
+    @pl.when(step == 2 * exp_local - 1)
+    def _():
+        near_route_ref[...] = route_ref[:half].astype(jnp.bfloat16)
+        far_route_ref[...] = route_ref[half:].astype(jnp.bfloat16)
+        dots_ref[...] = jnp.transpose(dots_sum_ref[...])[:n_experts]
+
+
+def expert_rows(at, before, blocks, near, far, all_grads, router, place, own, other, n_experts):
+    half, width = near.shape
+    count = 2 * half
+    exp_local, _, units = own[0].shape
+    wide = all_grads.shape[1]
+
+    def whole(array):
+        return pl.BlockSpec(
+            array.shape, lambda step, blocks: (0,) * array.ndim, pipeline_mode=pl.Buffered(1)
+        )
+
+    def picked(row):
+        return pl.BlockSpec(
+            (count // 4, wide), lambda step, blocks: (blocks[row], 0), pipeline_mode=pl.Buffered(1)
+        )
+
+    def own_expert(array):
+        return pl.BlockSpec(
+            (1, *array.shape[1:]), lambda step, blocks: (jnp.minimum(step, exp_local - 1), 0, 0)
+        )
+
+    def other_expert(array):
+        return pl.BlockSpec(
+            (1, *array.shape[1:]), lambda step, blocks: (jnp.maximum(step - exp_local, 0), 0, 0)
+        )
+
+    def first_block(shape):
+        return pl.BlockSpec(shape, lambda step, blocks: (0, 0))
+
+    def step_block(columns):
+        return pl.BlockSpec((count, columns), lambda step, blocks: (at, step))
+
+    def round_block(columns):
+        return pl.BlockSpec((count, columns), lambda step, blocks: (at, 0))
+
+    def rounds(columns):
+        return jax.ShapeDtypeStruct((GRID[0] * count, columns), jnp.bfloat16)
+
+    inputs = (blocks, near, far, *(all_grads for _ in range(4)), router, place, *own, *other, *before)
+    order = (2, 3, 5, 6)
+    route = jax.ShapeDtypeStruct((half, width), jnp.bfloat16)
+    return pl.pallas_call(
+        functools.partial(expert_kernel, n_experts=n_experts),
+        out_shape=[
+            route,
+            route,
+            rounds(2 * exp_local * units),
+            rounds(4 * exp_local * units),
+            jax.ShapeDtypeStruct((n_experts, count), jnp.float32),
+            rounds(width),
+            rounds(width),
+        ],
+        grid_spec=pltpu.PrefetchScalarGridSpec(
+            num_scalar_prefetch=1,
+            grid=(2 * exp_local,),
+            in_specs=[
+                whole(near),
+                whole(far),
+                *(picked(row) for row in range(4)),
+                whole(router),
+                whole(place),
+                *(own_expert(array) for array in own),
+                *(other_expert(array) for array in other),
+                *(pl.BlockSpec(memory_space=pl.ANY) for _ in before),
+            ],
+            out_specs=[
+                first_block((half, width)),
+                first_block((half, width)),
+                step_block(units),
+                step_block(2 * units),
+                first_block((n_experts, count)),
+                round_block(width),
+                round_block(width),
+            ],
+            scratch_shapes=[
+                pltpu.VMEM((count, LANES), jnp.float32),
+                pltpu.VMEM((count, LANES), jnp.float32),
+                pltpu.VMEM((count, width), jnp.float32),
+            ],
+        ),
+        input_output_aliases={
+            len(inputs) - len(before) + index: order[index] for index in range(len(before))
+        },
+        cost_estimate=pl.CostEstimate(flops=1024, bytes_accessed=1024, transcendentals=0),
+        compiler_params=pltpu.CompilerParams(
+            dimension_semantics=("arbitrary",), vmem_limit_bytes=46 * 1024 * 1024
+        ),
+        name="expert_rows",
+    )(*inputs)
+
+
+def dense_shards(
+    tokens,
+    seg_ids,
+    pad_mask,
+    expert_ids,
+    w_qkv,
+    w_out,
+    w_router,
+    norm_gains,
+    w_gate,
+    w_up,
+    w_down,
+    cotangent,
+):
+    z, x, y, core = (lax.axis_index(name) for name in FINE)
+    fsdp_rank = z * GRID[1] + x
+    tp_rank = y * GRID[3] + core
+    local_rows, width = tokens.shape
+    seq_len = seg_ids.shape[1]
+    exp_local, _, ff_local = w_gate.shape
+    n_experts = w_router.shape[1]
+    head_cols = w_qkv.shape[2]
+    heads_local = head_cols // HD
+    score_scale = HD ** (-0.5)
+    own_start = tp_rank * local_rows
+    small_cols = norm_gains.shape[1]
+    fsdp = FINE[:2]
+
+    def own_rows(values):
+        return lax.dynamic_slice_in_dim(values, own_start, local_rows, 0)
+
+    tp_swaps = (SWAP_CORE, SWAP_Y, SWAP_BOTH)
+    z_shifts = [shift_z(steps) for steps in range(1, GRID[0])]
+    small_own = jnp.pad(
+        jnp.concatenate([w_router, norm_gains.T], axis=1), ((0, 0), (0, LANES - n_experts - 4))
+    )
+    small = lax.dynamic_update_slice_in_dim(
+        jnp.zeros((w_qkv.shape[1], LANES), jnp.bfloat16), small_own, tp_rank * small_cols, 0
+    )
+    smalls, tokens_own = fence([send(small, swap) for swap in tp_swaps], tokens)
+    small = small + smalls[0] + smalls[1] + smalls[2]
+    weights_own = jnp.concatenate(
+        [w_qkv.transpose(1, 0, 2).reshape(w_qkv.shape[1], -1), w_out.T, small], axis=1
+    )
+    weights_full = lax.all_gather(weights_own, fsdp, axis=0, tiled=True)
+    names = jnp.arange(n_experts, dtype=jnp.int32)
+    own_ids = own_rows(expert_ids)
+    named = (own_ids[:, :, None] == names[None, None, :]).any(axis=1)
+    named_wide = jnp.pad(named.astype(jnp.bfloat16), ((0, 0), (0, LANES - n_experts)))
+    grads_own = jnp.concatenate([cotangent, named_wide], axis=1)
+    far = send(tokens_own, SWAP_Y)
+    mine = side_pair(tokens, far)
+    theirs = send(mine, SWAP_CORE)
+    rows_x = four_rows(mine, theirs).astype(jnp.float32)
+    scale1 = lax.rsqrt(jnp.mean(rows_x * rows_x, axis=-1, keepdims=True) + EPSILON)
+    own_weights = (w_gate, w_up, w_down)
+    grads_own, weights_own, weights_full, scale1, rows_x = fence(
+        grads_own, own_weights, weights_full, scale1, rows_x
+    )
+    all_grads_abs = lax.all_gather(grads_own, FINE[:3], axis=0, tiled=True)
+    other_weights = tuple(send(weight, SWAP_CORE) for weight in weights_own)
+    qkv_full = weights_full[:, : 3 * head_cols]
+    out_full = weights_full[:, 3 * head_cols : 4 * head_cols]
+    router_wide = weights_full[:, 4 * head_cols :]
+    router_full = router_wide[:, :n_experts]
+    gains_wide = router_wide[:, n_experts : n_experts + 4].T.astype(jnp.float32)
+
+    cosine, sine = rope_tables(seq_len, HD)
+    allowed = allowed_mask(seg_ids[0], pad_mask[0], 0, seq_len)
+    x_own = tokens.astype(jnp.float32)
+    col_start = tp_rank * head_cols
+    gain_query = lax.dynamic_slice_in_dim(gains_wide[2], col_start, head_cols)
+    gain_key = lax.dynamic_slice_in_dim(gains_wide[3], col_start, head_cols)
+    rows1 = (rows_x * scale1 * gains_wide[0]).astype(jnp.bfloat16)
+    projected = jnp.dot(rows1, qkv_full, preferred_element_type=jnp.float32)
+    query_raw = projected[:, :head_cols]
+    key_raw = projected[:, head_cols : 2 * head_cols]
+    values = projected[:, 2 * head_cols :].astype(jnp.bfloat16).reshape(seq_len, heads_local, HD)
+    squares = side_totals(
+        jnp.sum(query_raw * query_raw, axis=-1), jnp.sum(key_raw * key_raw, axis=-1)
+    )
+    scale_q = lax.rsqrt(squares[0] / width + EPSILON)[:, None]
+    scale_k = lax.rsqrt(squares[1] / width + EPSILON)[:, None]
+    unit_q = query_raw * scale_q
+    unit_k = key_raw * scale_k
+    queries = rotate((unit_q * gain_query).reshape(seq_len, heads_local, HD), cosine, sine).astype(
+        jnp.bfloat16
+    )
+    keys = rotate((unit_k * gain_key).reshape(seq_len, heads_local, HD), cosine, sine).astype(
+        jnp.bfloat16
+    )
+    raw_scores = (
+        jnp.einsum("qhd,khd->hqk", queries, keys, preferred_element_type=jnp.float32) * score_scale
+    )
+    scores = jnp.where(allowed[None], raw_scores, NEG_FILL)
+    powered = jnp.exp(scores - jnp.max(scores, axis=-1, keepdims=True))
+    probs = powered / jnp.sum(powered, axis=-1, keepdims=True)
+    probs_low = probs.astype(jnp.bfloat16)
+    mixed = (
+        jnp.einsum("hqk,khd->qhd", probs_low, values, preferred_element_type=jnp.float32)
+        .reshape(seq_len, head_cols)
+        .astype(jnp.bfloat16)
+    )
+    away, mine = core_split(
+        lax.dot_general(mixed, out_full, CONTRACT_LAST, preferred_element_type=jnp.float32)
+    )
+    away, kept = side_split(mine, send(away, SWAP_CORE))
+    far, kept = fence(send(away, SWAP_Y), kept)
+    hidden = x_own + kept + far
+    normed2, scale2 = norm_forward(hidden, gains_wide[1])
+    own_normed2 = normed2.astype(jnp.bfloat16)
+
+    place = (
+        jnp.arange(LANES)[None, :] == fsdp_rank * exp_local + jnp.arange(exp_local)[:, None]
+    ).astype(jnp.float32)
+    rows, rows_near, rows_far = [own_normed2], [], []
+    results, seconds, firsts, homes = [], [], [], []
+
+    def hop(column):
+        return send(column, z_shifts[0])
+
+    def experts(at):
+        plane = (z - at) % GRID[0] * (GRID[1] * GRID[2])
+        beside = jnp.where(core == 0, (1 - x) * GRID[2] + y, x * GRID[2] + 1 - y)
+        across = jnp.where(core == 0, x * GRID[2] + 1 - y, (1 - x) * GRID[2] + y)
+        opposite = (1 - x) * GRID[2] + 1 - y
+        blocks = plane + jnp.stack([x * GRID[2] + y, beside, across, opposite])
+        before = [results[at - 1][index] for index in (2, 3, 5, 6)] if at else []
+        return expert_rows(
+            at,
+            before,
+            blocks.astype(jnp.int32),
+            rows_near[at],
+            rows_far[at],
+            all_grads_abs,
+            router_wide,
+            place,
+            own_weights,
+            other_weights,
+            n_experts,
+        )
+
+    def near_of(at, arrived):
+        return jnp.concatenate([rows[at], arrived], axis=0)
+
+    def first_part(near, second):
+        half = near.shape[0] // 2
+        return add_low(near[half:], second[half:])
+
+    def mine_part(near, second, first):
+        half = near.shape[0] // 2
+        return wide_sum(near[:half], second[:half], first)
+
+    def route_first(at):
+        return send(first_part(results[at][0], seconds[at]), SWAP_FIRST)
+
+    def route_home(at):
+        mine = mine_part(results[at][0], seconds[at], firsts[at])
+        return send(mine.astype(jnp.bfloat16), z_shifts[GRID[0] - 1 - at])
+
+    hopped, arrived = fence(hop(rows[0]), send(rows[0], SWAP_FIRST))
+    rows.append(hopped)
+    rows_near.append(near_of(0, arrived))
+    hopped, arrived, second = fence(
+        hop(rows[1]), send(rows[1], SWAP_FIRST), send(rows_near[0], SWAP_SECOND)
+    )
+    rows.append(hopped)
+    rows_near.append(near_of(1, arrived))
+    rows_far.append(second)
+    hopped, arrived, second, result = fence(
+        hop(rows[2]), send(rows[2], SWAP_FIRST), send(rows_near[1], SWAP_SECOND), experts(0)
+    )
+    rows.append(hopped)
+    rows_near.append(near_of(2, arrived))
+    rows_far.append(second)
+    results.append(result)
+    arrived, second, back, result = fence(
+        send(rows[3], SWAP_FIRST),
+        send(rows_near[2], SWAP_SECOND),
+        send(results[0][1], SWAP_SECOND),
+        experts(1),
+    )
+    rows_near.append(near_of(3, arrived))
+    rows_far.append(second)
+    seconds.append(back)
+    results.append(result)
+    second, back, first, result = fence(
+        send(rows_near[3], SWAP_SECOND),
+        send(results[1][1], SWAP_SECOND),
+        route_first(0),
+        experts(2),
+    )
+    rows_far.append(second)
+    seconds.append(back)
+    firsts.append(first)
+    results.append(result)
+    back, first, result = fence(
+        send(results[2][1], SWAP_SECOND), route_first(1), experts(3)
+    )
+    seconds.append(back)
+    firsts.append(first)
+    results.append(result)
+    homes.append(mine_part(results[0][0], seconds[0], firsts[0]))
+
+    dots = jnp.stack([result[4] for result in results])
+    part = dots.shape[-1] // 4
+    all_active, all_hidden, all_grads, all_rows = (results[-1][index] for index in (2, 3, 5, 6))
+    down_rows = jnp.concatenate(
+        [weights[2].reshape(-1, width) for weights in (own_weights, other_weights)]
+    )
+    back, first, home, dots_back, dots, all_active, down_rows, all_hidden = fence(
+        send(results[3][1], SWAP_SECOND),
+        route_first(2),
+        route_home(1),
+        send(dots[..., 2 * part :], SWAP_SECOND),
+        dots,
+        all_active,
+        down_rows,
+        all_hidden,
+    )
+    seconds.append(back)
+    firsts.append(first)
+    homes.append(home)
+    dots = dots[..., : 2 * part] + dots_back
+    units = exp_local * ff_local
+    pair_count = 2 * exp_local
+
+    def piece(at):
+        return all_hidden[:, at * ff_local : (at + 1) * ff_local]
+
+    first, home, dots_back, dots, output, all_hidden = fence(
+        route_first(3),
+        route_home(2),
+        send(dots[..., part:], SWAP_FIRST),
+        dots,
+        jnp.dot(all_active, down_rows, preferred_element_type=jnp.float32).astype(jnp.bfloat16),
+        all_hidden,
+    )
+    half = output.shape[0] // (2 * GRID[0])
+    outputs = [
+        (output[2 * at * half : (2 * at + 1) * half], output[(2 * at + 1) * half : 2 * (at + 1) * half])
+        for at in range(GRID[0])
+    ]
+    firsts.append(first)
+    homes.append(home)
+    dots = dots[..., :part] + dots_back
+    home, dots_back, dots, outputs, all_hidden, others = fence(
+        route_home(3),
+        [send(dots[at], shift_z(-at)) for at in range(1, GRID[0])],
+        dots[0],
+        outputs,
+        all_hidden,
+        [pair_dots(all_rows, piece(pair_count))],
+    )
+    homes.append(home)
+    token_grad = wide_sum(*homes)
+    own_dots = (dots + dots_back[0] + dots_back[1] + dots_back[2]).T
+
+    logits = jnp.dot(own_normed2, router_full, preferred_element_type=jnp.float32)
+    router_probs = jax.nn.softmax(logits, axis=-1)
+    own_gates = jnp.where(named, router_probs, 0.0)
+    chosen = jnp.where(named, own_dots, 0.0)
+    weighted = jnp.sum(own_gates * chosen, axis=-1, keepdims=True)
+    own_logit_grad = (router_probs * (chosen - weighted)).astype(jnp.bfloat16)
+    normed2_grad = token_grad + jnp.dot(
+        own_logit_grad, router_full.T, preferred_element_type=jnp.float32
+    )
+    hidden_norm_grad, gain2_grad = norm_backward(hidden, scale2, gains_wide[1], normed2_grad)
+    hidden_grad = cotangent.astype(jnp.float32) + hidden_norm_grad
+    hidden_low = hidden_grad.astype(jnp.bfloat16)
+    far, hidden_low, outputs, all_hidden, more = fence(
+        send(hidden_low, SWAP_Y),
+        hidden_low,
+        outputs,
+        all_hidden,
+        [pair_dots(all_rows, piece(pair_count + 1))],
+    )
+    others = [*others, *more]
+    mine = side_pair(hidden_low, far)
+    theirs, mine, outputs, all_hidden = fence(send(mine, SWAP_CORE), mine, outputs, all_hidden)
+    hidden_rows = four_rows(mine, theirs)
+    mixed_grad = jnp.dot(hidden_rows, out_full, preferred_element_type=jnp.float32).astype(
+        jnp.bfloat16
+    )
+    mixed_grad, grad_out_full = fence(
+        mixed_grad, pair_dots(hidden_rows, mixed).astype(jnp.bfloat16)
+    )
+    grad_out = (
+        lax.psum_scatter(grad_out_full, fsdp, scatter_dimension=0, tiled=True)
+        .astype(jnp.float32)
+        .T
+    )
+    mixed_grad = mixed_grad.reshape(seq_len, heads_local, HD)
+    prob_grad = jnp.einsum("qhd,khd->hqk", mixed_grad, values, preferred_element_type=jnp.float32)
+    delta = jnp.sum(probs * prob_grad, axis=-1, keepdims=True)
+    score_grad = (probs * (prob_grad - delta)).astype(jnp.bfloat16)
+    value_grad = jnp.einsum(
+        "hqk,qhd->khd", probs_low, mixed_grad, preferred_element_type=jnp.float32
+    )
+    query_grad = (
+        jnp.einsum("hqk,khd->qhd", score_grad, keys, preferred_element_type=jnp.float32)
+        * score_scale
+    )
+    key_grad = (
+        jnp.einsum("hqk,qhd->khd", score_grad, queries, preferred_element_type=jnp.float32)
+        * score_scale
+    )
+    query_norm_grad = rotate_back(query_grad, cosine, sine).reshape(seq_len, head_cols)
+    key_norm_grad = rotate_back(key_grad, cosine, sine).reshape(seq_len, head_cols)
+    gain_query_grad = jnp.sum(query_norm_grad * unit_q, axis=0)
+    gain_key_grad = jnp.sum(key_norm_grad * unit_k, axis=0)
+    scaled_q = query_norm_grad * gain_query
+    scaled_k = key_norm_grad * gain_key
+    inners = side_totals(jnp.sum(scaled_q * unit_q, axis=-1), jnp.sum(scaled_k * unit_k, axis=-1))
+    query_raw_grad = scale_q * (scaled_q - unit_q * (inners[0] / width)[:, None])
+    key_raw_grad = scale_k * (scaled_k - unit_k * (inners[1] / width)[:, None])
+    qkv_grad = jnp.concatenate(
+        [query_raw_grad, key_raw_grad, value_grad.reshape(seq_len, head_cols)], axis=1
+    ).astype(jnp.bfloat16)
+    normed1_part = lax.dot_general(
+        qkv_grad, qkv_full, CONTRACT_LAST, preferred_element_type=jnp.float32
+    )
+    gain1_grad = jnp.sum(normed1_part * (rows_x * scale1), axis=0)
+    away, mine = core_split(normed1_part)
+    zero_width = jnp.zeros((width,), jnp.float32)
+    gains_grad = jnp.stack(
+        [
+            gain1_grad,
+            gain2_grad,
+            lax.dynamic_update_slice_in_dim(zero_width, gain_query_grad, col_start, 0),
+            lax.dynamic_update_slice_in_dim(zero_width, gain_key_grad, col_start, 0),
+        ]
+    )
+    small = jnp.concatenate([pair_dots(own_normed2, own_logit_grad), gains_grad.T], axis=1)
+    small = jnp.pad(small, ((0, 0), (0, LANES - n_experts - 4)))
+    grad_full = jnp.concatenate([pair_dots(rows1, qkv_grad), small], axis=1).astype(jnp.bfloat16)
+    grad_own = lax.psum_scatter(grad_full, fsdp, scatter_dimension=0, tiled=True)
+    grad_qkv = (
+        grad_own[:, : 3 * head_cols].astype(jnp.float32).reshape(-1, 3, head_cols).transpose(1, 0, 2)
+    )
+    small = grad_own[:, 3 * head_cols :]
+    away, mine, outputs, all_hidden, all_active, _ = fence(
+        away, mine, outputs, all_hidden, all_active, grad_full
+    )
+    back, mine, output_seconds, others, more, other_down, all_hidden = fence(
+        send(away, SWAP_CORE),
+        mine,
+        [send(pair[1], SWAP_SECOND) for pair in outputs],
+        [send(other, SWAP_CORE) for other in others],
+        [pair_dots(all_rows, piece(pair_count + at)) for at in range(2, pair_count)],
+        pair_dots(all_active[:, units:], all_grads),
+        all_hidden,
+    )
+    away, kept = side_split(mine, back)
+    output_firsts = [
+        send(first_part(pair[0], second), SWAP_FIRST)
+        for pair, second in zip(outputs, output_seconds)
+    ]
+    far, kept, output_firsts, more, other_down, grad_pair, all_hidden = fence(
+        send(away, SWAP_Y),
+        kept,
+        output_firsts,
+        [send(other, SWAP_CORE) for other in more],
+        send(other_down, SWAP_CORE),
+        [pair_dots(all_rows, piece(at)) + other for at, other in enumerate(others)],
+        all_hidden,
+    )
+    output_mine = [
+        mine_part(pair[0], second, first)
+        for pair, second, first in zip(outputs, output_seconds, output_firsts)
+    ]
+    output_homes = [
+        send(output_mine[at].astype(jnp.bfloat16), shift_z(-at)) for at in range(1, GRID[0])
+    ]
+    normed1_grad = kept + far
+    input_norm_grad, _ = norm_backward(x_own, own_rows(scale1), gains_wide[0], normed1_grad)
+    input_grad = hidden_grad + input_norm_grad
+    grad_pair = [
+        *grad_pair,
+        *(pair_dots(all_rows, piece(2 + at)) + other for at, other in enumerate(more)),
+    ]
+    grad_down = (pair_dots(all_active[:, :units], all_grads) + other_down).reshape(
+        exp_local, ff_local, width
+    )
+    layer_out = (hidden + wide_sum(output_mine[0], *output_homes)).astype(jnp.bfloat16)
+    grad_gate = jnp.stack(grad_pair[0::2])
+    grad_up = jnp.stack(grad_pair[1::2])
+    small = lax.dynamic_slice_in_dim(
+        wide_sum(small, *(send(small, swap) for swap in tp_swaps)),
+        tp_rank * small_cols,
+        small_cols,
+        0,
+    )
+    grad_router = small[:, :n_experts]
+    grad_gains = small[:, n_experts : n_experts + 4].T
+    return (
+        layer_out,
+        input_grad,
+        grad_qkv,
+        grad_out,
+        grad_router,
+        grad_gains,
+        grad_gate,
+        grad_up,
+        grad_down,
+    )
+
+
 def solution(mesh):
-    placed = (
-        P(("fsdp", "tp"), None),
-        P("fsdp", None),
-        P("fsdp", None),
-        P("fsdp", None),
-        P(None, "fsdp", "tp"),
-        P("tp", "fsdp"),
-        P(("fsdp", "tp"), None),
-        P(None, ("fsdp", "tp")),
-        P("fsdp", None, "tp"),
-        P("fsdp", None, "tp"),
-        P("fsdp", "tp", None),
-        P(("fsdp", "tp"), None),
-    )
+    fast = tuple(mesh.shape.values()) == (GRID[0] * GRID[1], GRID[2] * GRID[3])
+    fine = Mesh(mesh.devices.reshape(GRID), FINE) if fast else None
+
+    def layer(*arguments):
+        n_experts = arguments[8].shape[0]
+        top_count = arguments[3].shape[1]
+        if fast and n_experts <= 2 * top_count:
+            return placed_shards(dense_shards, fine, FINE[:2], FINE[2:])(*arguments)
+        return placed_shards(shards, mesh, ("fsdp",), ("tp",))(*arguments)
+
+    return layer
+
+
+def placed_shards(body, mesh, fsdp, tp):
+    rows = P((*fsdp, *tp), None)
+    experts = P(fsdp, None, tp)
+    columns = P(None, (*fsdp, *tp))
     return jax.shard_map(
-        shards,
+        body,
         mesh=mesh,
-        in_specs=placed,
+        in_specs=(
+            rows,
+            P(fsdp, None),
+            P(fsdp, None),
+            P(fsdp, None),
+            P(None, fsdp, tp),
+            P(tp, fsdp),
+            rows,
+            columns,
+            experts,
+            experts,
+            P(fsdp, tp, None),
+            rows,
+        ),
         out_specs=(
-            P(("fsdp", "tp"), None),
-            P(("fsdp", "tp"), None),
-            P(None, "fsdp", "tp"),
-            P("tp", "fsdp"),
-            P(("fsdp", "tp"), None),
-            P(None, ("fsdp", "tp")),
-            P("fsdp", None, "tp"),
-            P("fsdp", None, "tp"),
-            P("fsdp", "tp", None),
+            rows,
+            rows,
+            P(None, fsdp, tp),
+            P(tp, fsdp),
+            rows,
+            columns,
+            experts,
+            experts,
+            P(fsdp, tp, None),
         ),
         check_vma=False,
     )

time: 3060 us -> 761 us (0.25)
  blocking collectives: 1210 us -> 12 us
  waiting for transfers between devices: 1050 us -> 323 us
  local copies, waits for them, and re-layouts: 541 us -> 47.2 us
  Pallas kernels: 0 us -> 116 us
  starting transfers between devices: 13.8 us -> 62.3 us
    all_to_all x2 -> x0, blocking collectives: 755 us -> none  [the longest x1 378 us: return_experts(): lax.all_to_all(buffer, 'fsdp', split_axis=1, concat_axis=0, tiled=True)]
    all_gather x2 -> x0, blocking collectives: 433 us -> none  [the longest x1 397 us: shards(): lax.all_gather(w_router, ('fsdp', 'tp'), axis=0, tiled=True)]
    all_to_all x2 -> x0, waiting for transfers between devices: 368 us -> none  [the longest x1 368 us: send_experts(): lax.all_to_all(buffer, 'fsdp', split_axis=0, concat_axis=1, tiled=True)]
    gather x26 -> x0, local copies, waits for them, and re-layouts: 354 us -> none  [the longest x8 108 us: shards(): returned[flat_index[:, pick_rank]].astype(jnp.float32)]
    reduce_scatter x6 -> x2, waiting for transfers between devices: 304 us -> 40 us  [the longest x1 40 us: dense_shards(): lax.psum_scatter(grad_full, fsdp, scatter_dimension=0, tiled=True)]
    unnamed x16 -> x4, waiting for transfers between devices: 214 us -> 0.07 us
    ppermute x0 -> x60, waiting for transfers between devices: none -> 174 us  [send(): return lax.ppermute(values, FINE, pairs)]
    pallas_call x0 -> x4, Pallas kernels: none -> 116 us  [expert_rows(): pl.pallas_call(functools.partial(expert_kernel, n_experts=n_experts), out...]
  transfers between devices with their start and end apart: 16 -> 64, of which waited for: 13 -> 22; matrix products, arithmetic and copies ran while one was open for 8% -> 28% of each run, Pallas kernels for 0% -> 15%
where the time goes in v3:
time: 761 us; the launch traced here: 753 us
  waiting for transfers between devices  323 us (42%)
  matrix products  117 us (15%)
  Pallas kernels  116 us (15%)
  starting transfers between devices  62.3 us (8%)
  other arithmetic  60.5 us (8%)
  local copies, waits for them, and re-layouts  47.2 us (6%)
  between operations  15.6 us (2%)
  blocking collectives  12 us (2%)
    ppermute x60, waiting for transfers between devices, send(): return lax.ppermute(values, FINE, pairs)  174 us
    pallas_call x4, Pallas kernels, expert_rows(): pl.pallas_call(functools.partial(expert_kernel, n_experts=n_experts), out...  116 us
    all_gather x1, waiting for transfers between devices, dense_shards(): weights_full = lax.all_gather(weights_own, fsdp, axis=0, tiled=True)  109 us
    dot_general x13, matrix products, pair_dots(): lax.dot_general(left, right, (((0,), (0,)), ((), ())), preferred_element_...  68.4 us
    ppermute x60, starting transfers between devices, send(): return lax.ppermute(values, FINE, pairs)  61.9 us
    reduce_scatter x1, waiting for transfers between devices, dense_shards(): lax.psum_scatter(grad_full, fsdp, scatter_dimension=0, tiled=True)  40 us
    unnamed x194, local copies, waits for them, and re-layouts  16.1 us
  transfers between devices with their start and end apart: 64, of which 22 were waited for; matrix products, arithmetic and copies ran while one was open for 28% of the time, Pallas kernels for 15%

profile of v3, /device:TPU:9, one launch (start us, length us, event | category | flops | bytes accessed | tf_op | source)
XLA Modules:
  0.0 753.4 jit_solution(13345039338524659193)
XLA Ops:
  16.6 12.1 %collective-permute-done.3 = bf16[128,2048]{1,0:T(8,128)(2,1)S(1)} collective-permute-done((bf16[128,2048]{1,0:T(8,128)(2,1)S(1)}, bf16[128,2048]{1,0:T(8,128)(2,1)S(1)}, u32[]{:S(2)}, u32[]{:S(2)}) %collective-permute-start.3) | collective-permute-done | bytes 524320 | tf_op jit(solution)/shard_map/ppermute | solution.py:397
  36.7 108.9 %all-gather.3.cloned.1.call-done = bf16[2048,2176]{1,0:T(8,128)(2,1)} async-done(((bf16[256,2176]{1,0:T(8,128)(2,1)}), bf16[2048,2176]{1,0:T(8,128)(2,1)}) %all-gather.3.cloned.1.call-update) | async-done | bytes 8912912 | tf_op jit(solution)/shard_map/all_gather | solution.py:656
  157.9 6.4 all-reduce.4
  197.5 12.4 %collective-permute-done.6 = bf16[128,2048]{1,0:T(8,128)(2,1)S(1)} collective-permute-done((bf16[128,2048]{1,0:T(8,128)(2,1)S(1)}, bf16[128,2048]{1,0:T(8,128)(2,1)S(1)}, u32[]{:S(2)}, u32[]{:S(2)}) %collective-permute-start.6) | collective-permute-done | bytes 524320 | tf_op jit(solution)/shard_map/ppermute | solution.py:397
  214.7 31.8 %collective-permute-done.7 = bf16[128,2048]{1,0:T(8,128)(2,1)S(1)} collective-permute-done((bf16[128,2048]{1,0:T(8,128)(2,1)S(1)}, bf16[128,2048]{1,0:T(8,128)(2,1)S(1)}, u32[]{:S(2)}, u32[]{:S(2)}) %collective-permute-start.7) | collective-permute-done | bytes 524320 | tf_op jit(solution)/shard_map/ppermute | solution.py:397
  250.8 12.0 %collective-permute-done.10 = bf16[128,2048]{1,0:T(8,128)(2,1)S(1)} collective-permute-done((bf16[128,2048]{1,0:T(8,128)(2,1)S(1)}, bf16[128,2048]{1,0:T(8,128)(2,1)S(1)}, u32[]{:S(2)}, u32[]{:S(2)}) %collective-permute-start.10) | collective-permute-done | bytes 524320 | tf_op jit(solution)/shard_map/ppermute | solution.py:397
  264.8 22.5 %collective-permute-done.9 = bf16[128,2048]{1,0:T(8,128)(2,1)} collective-permute-done((bf16[128,2048]{1,0:T(8,128)(2,1)S(1)}, bf16[128,2048]{1,0:T(8,128)(2,1)}, u32[]{:S(2)}, u32[]{:S(2)}) %collective-permute-start.9) | collective-permute-done | bytes 524320 | tf_op jit(solution)/shard_map/ppermute | solution.py:397
  295.2 28.6 %expert_rows.4 = (bf16[256,2048]{1,0:T(8,128)(2,1)S(1)}, bf16[256,2048]{1,0:T(8,128)(2,1)S(1)}, bf16[2048,1024]{1,0:T(8,128)(2,1)}, bf16[2048,2048]{1,0:T(8,128)...) custom-call(s32[4]{0:T(128)S(1)} %get-tuple-element.483.blocks_ref, ...), custom_call_target="tpu_custom_call" | custom-call | flops 1024 | bytes 1024 | tf_op jit(solution)/shard_map/expert_rows/pallas_call | solution.py:562
  327.8 29.6 %expert_rows.5 = (bf16[256,2048]{1,0:T(8,128)(2,1)S(1)}, bf16[256,2048]{1,0:T(8,128)(2,1)S(1)}, bf16[2048,1024]{1,0:T(8,128)(2,1)}, bf16[2048,2048]{1,0:T(8,128)...) custom-call(s32[4]{0:T(128)S(1)} %get-tuple-element.482.blocks_ref, ...), custom_call_target="tpu_custom_call", output_to_operand_aliasing={{2}: (15, {}), {3}: (16, {}), {5}: (17, {}), {6}: (18, {})} | custom-call | flops 1024 | bytes 1024 | tf_op jit(solution)/shard_map/expert_rows/pallas_call | solution.py:562
  360.5 28.7 %expert_rows.6 = (bf16[256,2048]{1,0:T(8,128)(2,1)S(1)}, bf16[256,2048]{1,0:T(8,128)(2,1)S(1)}, bf16[2048,1024]{1,0:T(8,128)(2,1)}, bf16[2048,2048]{1,0:T(8,128)...) custom-call(s32[4]{0:T(128)S(1)} %get-tuple-element.481.blocks_ref, ...), custom_call_target="tpu_custom_call", output_to_operand_aliasing={{2}: (15, {}), {3}: (16, {}), {5}: (17, {}), {6}: (18, {})} | custom-call | flops 1024 | bytes 1024 | tf_op jit(solution)/shard_map/expert_rows/pallas_call | solution.py:562
  393.6 29.0 %expert_rows.7 = (bf16[256,2048]{1,0:T(8,128)(2,1)S(1)}, bf16[256,2048]{1,0:T(8,128)(2,1)S(1)}, bf16[2048,1024]{1,0:T(8,128)(2,1)}, bf16[2048,2048]{1,0:T(8,128)...) custom-call(s32[4]{0:T(128)S(1)} %get-tuple-element.423.blocks_ref, ...), custom_call_target="tpu_custom_call", output_to_operand_aliasing={{2}: (15, {}), {3}: (16, {}), {5}: (17, {}), {6}: (18, {})} | custom-call | flops 1024 | bytes 1024 | tf_op jit(solution)/shard_map/expert_rows/pallas_call | solution.py:562
  429.4 10.5 %collective-permute-done.29 = f32[4,16,256]{2,1,0:T(8,128)S(1)} collective-permute-done((f32[4,16,256]{2,1,0:T(8,128)S(1)}, f32[4,16,256]{2,1,0:T(8,128)S(1)}, u32[]{:S(2)}, u32[]{:S(2)}) %collective-permute-start.29) | collective-permute-done | bytes 65568 | tf_op jit(solution)/shard_map/ppermute | solution.py:397
  447.9 10.8 %convolution_convert_fusion.1 = bf16[2048,2048]{1,0:T(8,128)(2,1)} fusion(bf16[2048,1024]{1,0:T(8,128)(2,1)S(1)} %copy-done.8, bf16[1024,2048]{1,0:T(8,128)(2,1)S(1)} %pad_maximum_fusion.1), kind=kOutput, calls=%fused_computation.2 | convolution fusion | flops 8594128896 | bytes 16777216 | tf_op jit(solution)/shard_map/dot_general | solution.py:847
  538.4 7.7 %multiply_reduce_fusion = (bf16[2048]{0:T(1024)(128)(2,1)S(1)}, bf16[512,2048]{1,0:T(8,128)(2,1)}) fusion(f32[512,2048]{1,0:T(8,128)S(1)} %bitcast.188, f32[512]{0:T(512)S(1)} %bitcast.210, bf16[2048,2176]{1,0:T(8,128)(2,1)} %all-gather.3.cloned.1.call-done, bf16[512,512]{1,0:T(8,128)(2,1)S(1)} %copy-done.59, bf16[512,512]{1,0:T(8,128)(2,1)S(1)} %get-tuple-element.438, ...), kind=kOutput, calls=%fused_computation.11 | convolution fusion | flops 3230136320 | bytes 14161920 | tf_op jit(solution)/shard_map/dot_general | solution.py:931
  546.3 5.9 convolution_convert_fusion
  552.2 6.9 pad_maximum_fusion
  564.8 10.7 %fusion.9 = f32[512,2048]{1,0:T(8,128)} fusion(bf16[2048,2048]{1,0:T(8,128)(2,1)} %get-tuple-element.330, bf16[2048,1024]{1,0:T(8,128)(2,1)S(1)} %copy-done.9), kind=kOutput, calls=%fused_computation.32 | convolution fusion | flops 4294967296 | bytes 14680064 | tf_op jit(solution)/shard_map/dot_general | solution.py:417
  584.7 6.8 collective-permute-done.41
  591.5 19.6 %collective-permute-done.42 = bf16[256,2048]{1,0:T(8,128)(2,1)S(1)} collective-permute-done((bf16[256,2048]{1,0:T(8,128)(2,1)S(1)}, bf16[256,2048]{1,0:T(8,128)(2,1)S(1)}, u32[]{:S(2)}, u32[]{:S(2)}) %collective-permute-start.42) | collective-permute-done | bytes 1048608 | tf_op jit(solution)/shard_map/ppermute | solution.py:397
  611.2 14.3 %collective-permute-done.43 = bf16[256,2048]{1,0:T(8,128)(2,1)S(1)} collective-permute-done((bf16[256,2048]{1,0:T(8,128)(2,1)S(1)}, bf16[256,2048]{1,0:T(8,128)(2,1)S(1)}, u32[]{:S(2)}, u32[]{:S(2)}) %collective-permute-start.43) | collective-permute-done | bytes 1048608 | tf_op jit(solution)/shard_map/ppermute | solution.py:397
  653.9 6.2 collective-permute-done.46
  671.5 7.0 fusion.6
  685.9 7.8 %convolution_add_fusion = f32[512,2048]{1,0:T(8,128)} fusion(f32[512,2048]{1,0:T(8,128)} %collective-permute-done.53, bf16[2048,2048]{1,0:T(8,128)(2,1)S(1)} %bitcast.176, bf16[2048,1024]{1,0:T(8,128)(2,1)S(1)} %copy-done.10), kind=kOutput, calls=%fused_computation.19 | convolution fusion | flops 4296015872 | bytes 18874368 | tf_op jit(solution)/shard_map/dot_general | solution.py:417
  696.0 40.0 %reduce-scatter.3.cloned.1.call-done = bf16[256,1664]{0,1:T(8,128)(2,1)} async-done(((bf16[2048,1664]{0,1:T(8,128)(2,1)}), bf16[256,1664]{0,1:T(8,128)(2,1)}) %reduce-scatter.3.cloned.1.call-update) | async-done | bytes 851984 | tf_op jit(solution)/shard_map/reduce_scatter | solution.py:948
  (455 shorter events, 261.7 us)
Async XLA Ops:
  7.2 138.4 %all-gather.3.cloned.1.call-start = ((), (), s32[]{:S(2)}) async-start(), calls=%async_computation.2 | async-start | bytes 10027008 | tf_op jit(solution)/shard_map/all_gather | solution.py:656
  15.3 277.4 %all-gather.5.cloned.1.call-start = ((), (), s32[]{:S(2)}) async-start(), calls=%async_computation.3 | async-start | bytes 9469952 | tf_op jit(solution)/shard_map/all_gather | solution.py:671
  145.6 506.2 %reduce-scatter.5.cloned.1.call-start = ((), (), s32[]{:S(2)}) async-start(), calls=%async_computation.5 | async-start | bytes 2359296 | tf_op jit(solution)/shard_map/reduce_scatter | solution.py:900
  210.4 36.1 %collective-permute-start.7 = (bf16[128,2048]{1,0:T(8,128)(2,1)S(1)}, bf16[128,2048]{1,0:T(8,128)(2,1)S(1)}, u32[]{:S(2)}, u32[]{:S(2)}) collective-permute-start(bf16[128,2048]{1,0:T(8,128)(2,1)S(1)} %multiply_convert_fusion.4), channel_id=1, source_target_pairs={{0,8},{1,9},{2,10},{3,11},{4,12},{5,13},{6,14},{7,15},{8,16},{9,17... | collective-permute-start | bytes 1572872 | tf_op jit(solution)/shard_map/ppermute | solution.py:397
  213.0 33.5 %collective-permute-start.8 = (bf16[128,2048]{1,0:T(8,128)(2,1)S(1)}, bf16[128,2048]{1,0:T(8,128)(2,1)S(1)}, u32[]{:S(2)}, u32[]{:S(2)}) collective-permute-start(bf16[128,2048]{1,0:T(8,128)(2,1)S(1)} %multiply_convert_fusion.4), channel_id=1, source_target_pairs={{0,4},{1,3},{2,6},{3,1},{4,0},{5,7},{6,2},{7,5},{8,12},{9,11},{10,... | collective-permute-start | bytes 1572872 | tf_op jit(solution)/shard_map/ppermute | solution.py:397
  213.7 75.8 %collective-permute-start.15 = (bf16[2,2048,256]{2,1,0:T(8,128)(2,1)S(1)}, bf16[2,2048,256]{2,1,0:T(8,128)(2,1)}, u32[]{:S(2)}, u32[]{:S(2)}) collective-permute-start(bf16[2,2048,256]{2,1,0:T(8,128)(2,1)S(1)} %copy-done.2), channel_id=1, source_target_pairs={{0,1},{1,0},{2,3},{3,2},{4,5},{5,4},{6,7},{7,6},{8,9},{9,8},{10,11... | collective-permute-start | bytes 6291464 | tf_op jit(solution)/shard_map/ppermute | solution.py:397
  248.5 38.8 %collective-permute-start.11 = (bf16[256,2048]{1,0:T(8,128)(2,1)S(1)}, bf16[256,2048]{1,0:T(8,128)(2,1)S(1)}, u32[]{:S(2)}, u32[]{:S(2)}) collective-permute-start(bf16[256,2048]{1,0:T(8,128)(2,1)S(1)} %pad_maximum_fusion.8.near_ref), channel_id=1, source_target_pairs={{0,2},{1,5},{2,0},{3,7},{4,6},{5,1},{6,4},{7,3},{8,10},{9,13},{10,... | collective-permute-start | bytes 3145736 | tf_op jit(solution)/shard_map/ppermute | solution.py:397
  249.5 43.2 %collective-permute-start.16 = (bf16[2,2048,256]{2,1,0:T(8,128)(2,1)}, bf16[2,2048,256]{2,1,0:T(8,128)(2,1)}, u32[]{:S(2)}, u32[]{:S(2)}) collective-permute-start(bf16[2,2048,256]{2,1,0:T(8,128)(2,1)} %refs_7_.7), channel_id=1, source_target_pairs={{0,1},{1,0},{2,3},{3,2},{4,5},{5,4},{6,7},{7,6},{8,9},{9,8},{10,11... | collective-permute-start | bytes 6291464 | tf_op jit(solution)/shard_map/ppermute | solution.py:397
  250.8 41.9 %collective-permute-start.17 = (bf16[2,256,2048]{2,1,0:T(8,128)(2,1)}, bf16[2,256,2048]{2,1,0:T(8,128)(2,1)}, u32[]{:S(2)}, u32[]{:S(2)}) collective-permute-start(bf16[2,256,2048]{2,1,0:T(8,128)(2,1)} %refs_8_.7), channel_id=1, source_target_pairs={{0,1},{1,0},{2,3},{3,2},{4,5},{5,4},{6,7},{7,6},{8,9},{9,8},{10,11... | collective-permute-start | bytes 6291464 | tf_op jit(solution)/shard_map/ppermute | solution.py:397
  289.1 34.6 %collective-permute-start.14 = (bf16[256,2048]{1,0:T(8,128)(2,1)}, bf16[256,2048]{1,0:T(8,128)(2,1)}, u32[]{:S(2)}, u32[]{:S(2)}) collective-permute-start(bf16[256,2048]{1,0:T(8,128)(2,1)} %constant_dynamic-update-slice_fusion.near_ref), channel_id=1, source_target_pairs={{0,2},{1,5},{2,0},{3,7},{4,6},{5,1},{6,4},{7,3},{8,10},{9,13},{10,... | collective-permute-start | bytes 3145736 | tf_op jit(solution)/shard_map/ppermute | solution.py:397
  289.2 34.5 %collective-permute-start.12 = (bf16[128,2048]{1,0:T(8,128)(2,1)}, bf16[128,2048]{1,0:T(8,128)(2,1)}, u32[]{:S(2)}, u32[]{:S(2)}) collective-permute-start(bf16[128,2048]{1,0:T(8,128)(2,1)} %collective-permute-done.9), channel_id=1, source_target_pairs={{0,8},{1,9},{2,10},{3,11},{4,12},{5,13},{6,14},{7,15},{8,16},{9,17... | collective-permute-start | bytes 1572872 | tf_op jit(solution)/shard_map/ppermute | solution.py:397
  289.5 34.3 %collective-permute-start.13 = (bf16[128,2048]{1,0:T(8,128)(2,1)}, bf16[128,2048]{1,0:T(8,128)(2,1)}, u32[]{:S(2)}, u32[]{:S(2)}) collective-permute-start(bf16[128,2048]{1,0:T(8,128)(2,1)} %collective-permute-done.9), channel_id=1, source_target_pairs={{0,4},{1,3},{2,6},{3,1},{4,0},{5,7},{6,2},{7,5},{8,12},{9,11},{10,... | collective-permute-start | bytes 1572872 | tf_op jit(solution)/shard_map/ppermute | solution.py:397
  324.9 33.7 %collective-permute-start.19 = (bf16[256,2048]{1,0:T(8,128)(2,1)S(1)}, bf16[256,2048]{1,0:T(8,128)(2,1)S(1)}, u32[]{:S(2)}, u32[]{:S(2)}) collective-permute-start(bf16[256,2048]{1,0:T(8,128)(2,1)S(1)} %constant_dynamic-update-slice_fusion.2.near_ref), channel_id=1, source_target_pairs={{0,2},{1,5},{2,0},{3,7},{4,6},{5,1},{6,4},{7,3},{8,10},{9,13},{10,... | collective-permute-start | bytes 3145736 | tf_op jit(solution)/shard_map/ppermute | solution.py:397
  389.5 33.1 %collective-permute-start.24 = (bf16[256,2048]{1,0:T(8,128)(2,1)S(1)}, bf16[256,2048]{1,0:T(8,128)(2,1)S(1)}, u32[]{:S(2)}, u32[]{:S(2)}) collective-permute-start(bf16[256,2048]{1,0:T(8,128)(2,1)S(1)} %get-tuple-element.241), channel_id=1, source_target_pairs={{0,2},{1,5},{2,0},{3,7},{4,6},{5,1},{6,4},{7,3},{8,10},{9,13},{10,... | collective-permute-start | bytes 3145736 | tf_op jit(solution)/shard_map/ppermute | solution.py:397
  498.3 77.2 %collective-permute-start.44 = (f32[2048,256]{1,0:T(8,128)}, f32[2048,256]{1,0:T(8,128)}, u32[]{:S(2)}, u32[]{:S(2)}) collective-permute-start(f32[2048,256]{1,0:T(8,128)} %fusion.44), channel_id=1, source_target_pairs={{0,1},{1,0},{2,3},{3,2},{4,5},{5,4},{6,7},{7,6},{8,9},{9,8},{10,11... | collective-permute-start | bytes 6291464 | tf_op jit(solution)/shard_map/ppermute | solution.py:397
  498.5 126.9 %collective-permute-start.45 = (f32[2048,256]{1,0:T(8,128)}, f32[2048,256]{1,0:T(8,128)}, u32[]{:S(2)}, u32[]{:S(2)}) collective-permute-start(f32[2048,256]{1,0:T(8,128)} %fusion.42), channel_id=1, source_target_pairs={{0,1},{1,0},{2,3},{3,2},{4,5},{5,4},{6,7},{7,6},{8,9},{9,8},{10,11... | collective-permute-start | bytes 6291464 | tf_op jit(solution)/shard_map/ppermute | solution.py:397
  518.8 217.1 %reduce-scatter.3.cloned.1.call-start = ((), (), s32[]{:S(2)}) async-start(), calls=%async_computation.4 | async-start | bytes 7667712 | tf_op jit(solution)/shard_map/reduce_scatter | solution.py:948
  575.5 35.7 %collective-permute-start.42 = (bf16[256,2048]{1,0:T(8,128)(2,1)S(1)}, bf16[256,2048]{1,0:T(8,128)(2,1)S(1)}, u32[]{:S(2)}, u32[]{:S(2)}) collective-permute-start(bf16[256,2048]{1,0:T(8,128)(2,1)S(1)} %copy-done.45), channel_id=1, source_target_pairs={{0,2},{1,5},{2,0},{3,7},{4,6},{5,1},{6,4},{7,3},{8,10},{9,13},{10,... | collective-permute-start | bytes 3145736 | tf_op jit(solution)/shard_map/ppermute | solution.py:397
  575.6 49.8 %collective-permute-start.43 = (bf16[256,2048]{1,0:T(8,128)(2,1)S(1)}, bf16[256,2048]{1,0:T(8,128)(2,1)S(1)}, u32[]{:S(2)}, u32[]{:S(2)}) collective-permute-start(bf16[256,2048]{1,0:T(8,128)(2,1)S(1)} %copy-done.44), channel_id=1, source_target_pairs={{0,2},{1,5},{2,0},{3,7},{4,6},{5,1},{6,4},{7,3},{8,10},{9,13},{10,... | collective-permute-start | bytes 3145736 | tf_op jit(solution)/shard_map/ppermute | solution.py:397
  625.5 34.6 %collective-permute-start.53 = (f32[512,2048]{1,0:T(8,128)}, f32[512,2048]{1,0:T(8,128)}, u32[]{:S(2)}, u32[]{:S(2)}) collective-permute-start(f32[512,2048]{1,0:T(8,128)} %fusion.9), channel_id=1, source_target_pairs={{0,1},{1,0},{2,3},{3,2},{4,5},{5,4},{6,7},{7,6},{8,9},{9,8},{10,11... | collective-permute-start | bytes 12582920 | tf_op jit(solution)/shard_map/ppermute | solution.py:397
  627.4 32.7 %collective-permute-start.51 = (f32[2048,256]{1,0:T(8,128)}, f32[2048,256]{1,0:T(8,128)}, u32[]{:S(2)}, u32[]{:S(2)}) collective-permute-start(f32[2048,256]{1,0:T(8,128)} %fusion.40), channel_id=1, source_target_pairs={{0,1},{1,0},{2,3},{3,2},{4,5},{5,4},{6,7},{7,6},{8,9},{9,8},{10,11... | collective-permute-start | bytes 6291464 | tf_op jit(solution)/shard_map/ppermute | solution.py:397
  662.5 75.5 %collective-permute-start.54 = (bf16[128,2048]{1,0:T(8,128)(2,1)}, bf16[128,2048]{1,0:T(8,128)(2,1)}, u32[]{:S(2)}, u32[]{:S(2)}) collective-permute-start(bf16[128,2048]{1,0:T(8,128)(2,1)} %add_convert_fusion.3), channel_id=1, source_target_pairs={{0,24},{1,25},{2,26},{3,27},{4,28},{5,29},{6,30},{7,31},{8,0},{9,1... | collective-permute-start | bytes 1572872 | tf_op jit(solution)/shard_map/ppermute | solution.py:397
  667.9 71.3 %collective-permute-start.55 = (bf16[128,2048]{1,0:T(8,128)(2,1)}, bf16[128,2048]{1,0:T(8,128)(2,1)}, u32[]{:S(2)}, u32[]{:S(2)}) collective-permute-start(bf16[128,2048]{1,0:T(8,128)(2,1)} %add_convert_fusion.2), channel_id=1, source_target_pairs={{0,16},{1,17},{2,18},{3,19},{4,20},{5,21},{6,22},{7,23},{8,24},{9,... | collective-permute-start | bytes 1572872 | tf_op jit(solution)/shard_map/ppermute | solution.py:397
  668.9 70.2 %collective-permute-start.56 = (bf16[128,2048]{1,0:T(8,128)(2,1)}, bf16[128,2048]{1,0:T(8,128)(2,1)}, u32[]{:S(2)}, u32[]{:S(2)}) collective-permute-start(bf16[128,2048]{1,0:T(8,128)(2,1)} %add_convert_fusion.1), channel_id=1, source_target_pairs={{0,8},{1,9},{2,10},{3,11},{4,12},{5,13},{6,14},{7,15},{8,16},{9,17... | collective-permute-start | bytes 1572872 | tf_op jit(solution)/shard_map/ppermute | solution.py:397
  (134 other events, 1909.7 us)
Sparse Core Ops, SparseCore 0:
  15.5 130.0 all-gather.2
  148.4 142.5 all-gather.4
  518.9 66.4 reduce-scatter.4
  588.9 146.9 reduce-scatter.2

commit v4 on v3

--- a/solution.py
+++ b/solution.py
@@ -449,79 +449,118 @@
     return (away, wide_sum(at(mine, side), at(back, side)))
 
 
-def expert_kernel(blocks_ref, near_ref, far_ref, *refs, n_experts):
-    grad_block_refs, (router_ref, place_ref), own, other = refs[:4], refs[4:6], refs[6:9], refs[9:12]
-    outputs, (gates_ref, dots_sum_ref, route_ref) = refs[-10:-3], refs[-3:]
-    near_route_ref, far_route_ref, active_ref, hidden_ref, dots_ref, grads_ref, rows_ref = outputs
-    _, width, units = own[0].shape
-    exp_local = place_ref.shape[0]
+def expert_kernel(
+    blocks_ref,
+    near_ref,
+    far_ref,
+    grads0_ref,
+    grads1_ref,
+    grads2_ref,
+    grads3_ref,
+    router_ref,
+    place_ref,
+    *refs,
+    n_experts,
+    at,
+    n_before,
+):
+    weight_refs, refs = refs[:6], refs[6 + n_before :]
+    near_route_ref, far_route_ref, active_ref, hidden_ref, dots_ref, grads_ref, rows_ref = refs[:7]
+    gate_buf, up_buf, down_buf, active_buf, hidden_buf, rows_buf, grads_buf, in_sems, out_sems = refs[7:]
+    exp_local, width = place_ref.shape[0], near_ref.shape[1]
+    units = gate_buf.shape[2]
     half = near_ref.shape[0]
-    step = pl.program_id(0)
-
-    @pl.when(step == 0)
-    def _():
-        rows_ref[:half] = near_ref[...]
-        rows_ref[half:] = far_ref[...]
-        quarter = half // 2
-        for at, ref in enumerate(grad_block_refs):
-            grads_ref[at * quarter : (at + 1) * quarter] = ref[:, :width]
-        named = jnp.concatenate([ref[:, width:] for ref in grad_block_refs], axis=0)
-        lane = lax.broadcasted_iota(jnp.int32, (1, LANES), 1)
-        logits = jnp.dot(rows_ref[...], router_ref[...], preferred_element_type=jnp.float32)
-        logits = jnp.where(lane < n_experts, logits, NEG_FILL)
-        powered = jnp.exp(logits - jnp.max(logits, axis=-1, keepdims=True))
-        total = jnp.sum(powered, axis=-1, keepdims=True)
-        gates_ref[...] = powered / total * named.astype(jnp.float32)
-        dots_sum_ref[...] = jnp.zeros_like(dots_sum_ref)
-        route_ref[...] = jnp.zeros_like(route_ref)
-
-    def expert(place, gate_ref, up_ref, down_ref):
-        rows = rows_ref[...]
-        gate = jnp.sum(gates_ref[...] * place, axis=-1, keepdims=True)
-        gate_pre = jnp.dot(rows, gate_ref[0], preferred_element_type=jnp.float32)
-        up_pre = jnp.dot(rows, up_ref[0], preferred_element_type=jnp.float32)
+    count = 2 * half
+    buffers = (gate_buf, up_buf, down_buf)
+
+    def fetch(slot, kind):
+        group, expert = slot // exp_local, slot % exp_local
+        return pltpu.make_async_copy(
+            weight_refs[3 * group + kind].at[expert], buffers[kind].at[slot], in_sems.at[slot, kind]
+        )
+
+    slots = 2 * exp_local
+    for slot in range(slots):
+        for kind in range(3):
+            fetch(slot, kind).start()
+    rows_buf[:half] = near_ref[...]
+    rows_buf[half:] = far_ref[...]
+    quarter = half // 2
+    grad_refs = (grads0_ref, grads1_ref, grads2_ref, grads3_ref)
+    for block, ref in enumerate(grad_refs):
+        grads_buf[block * quarter : (block + 1) * quarter] = ref[:, :width]
+
+    def round_rows(ref):
+        return ref.at[pl.ds(at * count, count)]
+
+    stores = [
+        pltpu.make_async_copy(rows_buf, round_rows(rows_ref), out_sems.at[0]),
+        pltpu.make_async_copy(grads_buf, round_rows(grads_ref), out_sems.at[1]),
+    ]
+    for store in stores:
+        store.start()
+    named = jnp.concatenate([ref[:, width:] for ref in grad_refs], axis=0)
+    rows = rows_buf[...]
+    grads = grads_buf[...]
+    lane = lax.broadcasted_iota(jnp.int32, (1, LANES), 1)
+    logits = jnp.dot(rows, router_ref[...], preferred_element_type=jnp.float32)
+    logits = jnp.where(lane < n_experts, logits, NEG_FILL)
+    powered = jnp.exp(logits - jnp.max(logits, axis=-1, keepdims=True))
+    gates = powered / jnp.sum(powered, axis=-1, keepdims=True) * named.astype(jnp.float32)
+    route = None
+    dots = jnp.zeros(logits.shape, jnp.float32)
+    for slot in range(slots):
+        expert = slot % exp_local
+        place = place_ref[expert : expert + 1, :]
+        gate = jnp.sum(gates * place, axis=-1, keepdims=True)
+        for kind in range(3):
+            fetch(slot, kind).wait()
+        gate_pre = jnp.dot(rows, gate_buf[slot], preferred_element_type=jnp.float32)
+        up_pre = jnp.dot(rows, up_buf[slot], preferred_element_type=jnp.float32)
         y_down = lax.dot_general(
-            grads_ref[...], down_ref[0], CONTRACT_LAST, preferred_element_type=jnp.float32
+            grads, down_buf[slot], CONTRACT_LAST, preferred_element_type=jnp.float32
         )
         sigmoid = 1.0 / (1.0 + jnp.exp(-gate_pre))
         silu = gate_pre * sigmoid
         active = silu * up_pre
-        dots_sum_ref[...] += jnp.sum(active * y_down, axis=-1, keepdims=True) * place
-        active_ref[...] = (active * gate).astype(jnp.bfloat16)
+        dots = dots + jnp.sum(active * y_down, axis=-1, keepdims=True) * place
+        active_buf[slot] = (active * gate).astype(jnp.bfloat16)
         active_grad = y_down * gate
         gate_grad = (active_grad * up_pre * sigmoid * (1.0 + gate_pre * (1.0 - sigmoid))).astype(
             jnp.bfloat16
         )
         up_grad = (active_grad * silu).astype(jnp.bfloat16)
-        hidden_ref[:, :units] = gate_grad
-        hidden_ref[:, units:] = up_grad
-        route_ref[...] += lax.dot_general(
-            gate_grad, gate_ref[0], CONTRACT_LAST, preferred_element_type=jnp.float32
+        hidden_buf[slot, :, :units] = gate_grad
+        hidden_buf[slot, :, units:] = up_grad
+        for buf, ref, columns, sem in (
+            (active_buf, active_ref, units, 2 + 2 * slot),
+            (hidden_buf, hidden_ref, 2 * units, 3 + 2 * slot),
+        ):
+            store = pltpu.make_async_copy(
+                buf.at[slot],
+                ref.at[pl.ds(at * count, count), pl.ds(slot * columns, columns)],
+                out_sems.at[sem],
+            )
+            store.start()
+            stores.append(store)
+        part = lax.dot_general(
+            gate_grad, gate_buf[slot], CONTRACT_LAST, preferred_element_type=jnp.float32
         ) + lax.dot_general(
-            up_grad, up_ref[0], CONTRACT_LAST, preferred_element_type=jnp.float32
-        )
-
-    place = place_ref[pl.ds(step % exp_local, 1), :]
-
-    @pl.when(step < exp_local)
-    def _():
-        expert(place, *own)
-
-    @pl.when(step >= exp_local)
-    def _():
-        expert(place, *other)
-
-    @pl.when(step == 2 * exp_local - 1)
-    def _():
-        near_route_ref[...] = route_ref[:half].astype(jnp.bfloat16)
-        far_route_ref[...] = route_ref[half:].astype(jnp.bfloat16)
-        dots_ref[...] = jnp.transpose(dots_sum_ref[...])[:n_experts]
+            up_grad, up_buf[slot], CONTRACT_LAST, preferred_element_type=jnp.float32
+        )
+        route = part if route is None else route + part
+    near_route_ref[...] = route[:half].astype(jnp.bfloat16)
+    far_route_ref[...] = route[half:].astype(jnp.bfloat16)
+    dots_ref[...] = jnp.transpose(dots)[:n_experts]
+    for store in stores:
+        store.wait()
 
 
 def expert_rows(at, before, blocks, near, far, all_grads, router, place, own, other, n_experts):
     half, width = near.shape
     count = 2 * half
     exp_local, _, units = own[0].shape
+    slots = 2 * exp_local
     wide = all_grads.shape[1]
 
     def whole(array):
@@ -534,68 +573,57 @@
             (count // 4, wide), lambda step, blocks: (blocks[row], 0), pipeline_mode=pl.Buffered(1)
         )
 
-    def own_expert(array):
-        return pl.BlockSpec(
-            (1, *array.shape[1:]), lambda step, blocks: (jnp.minimum(step, exp_local - 1), 0, 0)
-        )
-
-    def other_expert(array):
-        return pl.BlockSpec(
-            (1, *array.shape[1:]), lambda step, blocks: (jnp.maximum(step - exp_local, 0), 0, 0)
-        )
-
     def first_block(shape):
         return pl.BlockSpec(shape, lambda step, blocks: (0, 0))
 
-    def step_block(columns):
-        return pl.BlockSpec((count, columns), lambda step, blocks: (at, step))
-
-    def round_block(columns):
-        return pl.BlockSpec((count, columns), lambda step, blocks: (at, 0))
-
     def rounds(columns):
         return jax.ShapeDtypeStruct((GRID[0] * count, columns), jnp.bfloat16)
 
+    anywhere = pl.BlockSpec(memory_space=pl.ANY)
     inputs = (blocks, near, far, *(all_grads for _ in range(4)), router, place, *own, *other, *before)
     order = (2, 3, 5, 6)
     route = jax.ShapeDtypeStruct((half, width), jnp.bfloat16)
     return pl.pallas_call(
-        functools.partial(expert_kernel, n_experts=n_experts),
+        functools.partial(expert_kernel, n_experts=n_experts, at=at, n_before=len(before)),
         out_shape=[
             route,
             route,
-            rounds(2 * exp_local * units),
-            rounds(4 * exp_local * units),
+            rounds(slots * units),
+            rounds(2 * slots * units),
             jax.ShapeDtypeStruct((n_experts, count), jnp.float32),
             rounds(width),
             rounds(width),
         ],
         grid_spec=pltpu.PrefetchScalarGridSpec(
             num_scalar_prefetch=1,
-            grid=(2 * exp_local,),
+            grid=(1,),
             in_specs=[
                 whole(near),
                 whole(far),
                 *(picked(row) for row in range(4)),
                 whole(router),
                 whole(place),
-                *(own_expert(array) for array in own),
-                *(other_expert(array) for array in other),
-                *(pl.BlockSpec(memory_space=pl.ANY) for _ in before),
+                *(anywhere for _ in range(6 + len(before))),
             ],
             out_specs=[
                 first_block((half, width)),
                 first_block((half, width)),
-                step_block(units),
-                step_block(2 * units),
+                anywhere,
+                anywhere,
                 first_block((n_experts, count)),
-                round_block(width),
-                round_block(width),
+                anywhere,
+                anywhere,
             ],
             scratch_shapes=[
-                pltpu.VMEM((count, LANES), jnp.float32),
-                pltpu.VMEM((count, LANES), jnp.float32),
-                pltpu.VMEM((count, width), jnp.float32),
+                pltpu.VMEM((slots, width, units), jnp.bfloat16),
+                pltpu.VMEM((slots, width, units), jnp.bfloat16),
+                pltpu.VMEM((slots, units, width), jnp.bfloat16),
+                pltpu.VMEM((slots, count, units), jnp.bfloat16),
+                pltpu.VMEM((slots, count, 2 * units), jnp.bfloat16),
+                pltpu.VMEM((count, width), jnp.bfloat16),
+                pltpu.VMEM((count, width), jnp.bfloat16),
+                pltpu.SemaphoreType.DMA((slots, 3)),
+                pltpu.SemaphoreType.DMA((2 + 2 * slots,)),
             ],
         ),
         input_output_aliases={
@@ -607,6 +635,148 @@
         ),
         name="expert_rows",
     )(*inputs)
+
+
+def turned(values, cosine, sine):
+    return values * cosine + pltpu.roll(values, HD // 2, 1) * sine
+
+
+def allowed_pairs(segment_col_ref, segment_row_ref, padding_ref):
+    count = segment_col_ref.shape[0]
+    row = lax.broadcasted_iota(jnp.int32, (count, count), 0)
+    col = lax.broadcasted_iota(jnp.int32, (count, count), 1)
+    usable = (padding_ref[...] == 1) | (col == row)
+    return (segment_col_ref[...] == segment_row_ref[...]) & (col <= row) & usable
+
+
+def attend_kernel(
+    projected_ref,
+    scale_q_ref,
+    scale_k_ref,
+    gain_q_ref,
+    gain_k_ref,
+    cosine_ref,
+    sine_ref,
+    segment_col_ref,
+    segment_row_ref,
+    padding_ref,
+    mixed_ref,
+    queries_ref,
+    keys_ref,
+    values_ref,
+    log_sum_ref,
+):
+    width = mixed_ref.shape[1]
+    allowed = allowed_pairs(segment_col_ref, segment_row_ref, padding_ref)
+    cosine, sine = cosine_ref[...], sine_ref[...]
+    scale_q, scale_k = scale_q_ref[...], scale_k_ref[...]
+    for head in range(width // HD):
+        at = slice(head * HD, (head + 1) * HD)
+        raw_q = projected_ref[:, head * HD : (head + 1) * HD]
+        raw_k = projected_ref[:, width + head * HD : width + (head + 1) * HD]
+        raw_v = projected_ref[:, 2 * width + head * HD : 2 * width + (head + 1) * HD]
+        queries = turned(raw_q * scale_q * gain_q_ref[:, at], cosine, sine).astype(jnp.bfloat16)
+        keys = turned(raw_k * scale_k * gain_k_ref[:, at], cosine, sine).astype(jnp.bfloat16)
+        values = raw_v.astype(jnp.bfloat16)
+        scores = (
+            lax.dot_general(queries, keys, CONTRACT_LAST, preferred_element_type=jnp.float32)
+            * HD ** (-0.5)
+        )
+        scores = jnp.where(allowed, scores, NEG_FILL)
+        peak = jnp.max(scores, axis=-1, keepdims=True)
+        powered = jnp.exp(scores - peak)
+        total = jnp.sum(powered, axis=-1, keepdims=True)
+        probs_low = (powered / total).astype(jnp.bfloat16)
+        mixed_ref[:, at] = jnp.dot(
+            probs_low, values, preferred_element_type=jnp.float32
+        ).astype(jnp.bfloat16)
+        queries_ref[:, at] = queries
+        keys_ref[:, at] = keys
+        values_ref[:, at] = values
+        log_sum_ref[:, head : head + 1] = peak + jnp.log(total)
+
+
+def attend_back_kernel(
+    hidden_ref,
+    out_ref,
+    queries_ref,
+    keys_ref,
+    values_ref,
+    log_sum_ref,
+    projected_ref,
+    scale_q_ref,
+    scale_k_ref,
+    gain_q_ref,
+    gain_k_ref,
+    cosine_ref,
+    sine_ref,
+    segment_col_ref,
+    segment_row_ref,
+    padding_ref,
+    scaled_q_ref,
+    scaled_k_ref,
+    value_grad_ref,
+    inner_ref,
+    gain_grad_ref,
+):
+    width = queries_ref.shape[1]
+    allowed = allowed_pairs(segment_col_ref, segment_row_ref, padding_ref)
+    cosine, sine = cosine_ref[...], sine_ref[...]
+    mixed_grad_all = jnp.dot(
+        hidden_ref[...], out_ref[...], preferred_element_type=jnp.float32
+    ).astype(jnp.bfloat16)
+    contract_rows = (((0,), (0,)), ((), ()))
+    inner_q = jnp.zeros((queries_ref.shape[0], 1), jnp.float32)
+    inner_k = jnp.zeros((queries_ref.shape[0], 1), jnp.float32)
+    for head in range(width // HD):
+        at = slice(head * HD, (head + 1) * HD)
+        queries, keys, values = queries_ref[:, at], keys_ref[:, at], values_ref[:, at]
+        mixed_grad = mixed_grad_all[:, at]
+        scores = (
+            lax.dot_general(queries, keys, CONTRACT_LAST, preferred_element_type=jnp.float32)
+            * HD ** (-0.5)
+        )
+        powered = jnp.exp(jnp.where(allowed, scores, NEG_FILL) - log_sum_ref[:, head : head + 1])
+        probs = jnp.where(allowed, powered, 0.0)
+        prob_grad = lax.dot_general(
+            mixed_grad, values, CONTRACT_LAST, preferred_element_type=jnp.float32
+        )
+        delta = jnp.sum(probs * prob_grad, axis=-1, keepdims=True)
+        score_grad = (probs * (prob_grad - delta)).astype(jnp.bfloat16)
+        query_grad = jnp.dot(score_grad, keys, preferred_element_type=jnp.float32) * HD ** (-0.5)
+        key_grad = lax.dot_general(
+            score_grad, queries, contract_rows, preferred_element_type=jnp.float32
+        ) * HD ** (-0.5)
+        value_grad_ref[:, at] = lax.dot_general(
+            probs.astype(jnp.bfloat16),
+            mixed_grad,
+            contract_rows,
+            preferred_element_type=jnp.float32,
+        ).astype(jnp.bfloat16)
+        query_grad = turned(query_grad, cosine, -sine)
+        key_grad = turned(key_grad, cosine, -sine)
+        unit_q = projected_ref[:, head * HD : (head + 1) * HD] * scale_q_ref[...]
+        unit_k = projected_ref[:, width + head * HD : width + (head + 1) * HD] * scale_k_ref[...]
+        gain_grad_ref[0:1, at] = jnp.sum(query_grad * unit_q, axis=0, keepdims=True)
+        gain_grad_ref[1:2, at] = jnp.sum(key_grad * unit_k, axis=0, keepdims=True)
+        scaled_q = query_grad * gain_q_ref[:, at]
+        scaled_k = key_grad * gain_k_ref[:, at]
+        scaled_q_ref[:, at] = scaled_q
+        scaled_k_ref[:, at] = scaled_k
+        inner_q += jnp.sum(scaled_q * unit_q, axis=-1, keepdims=True)
+        inner_k += jnp.sum(scaled_k * unit_k, axis=-1, keepdims=True)
+    inner_ref[:, 0:1] = inner_q
+    inner_ref[:, 1:2] = inner_k
+
+
+def small_call(kernel, shapes, name):
+    return pl.pallas_call(
+        kernel,
+        out_shape=[jax.ShapeDtypeStruct(shape, dtype) for shape, dtype in shapes],
+        cost_estimate=pl.CostEstimate(flops=1024, bytes_accessed=1024, transcendentals=0),
+        compiler_params=pltpu.CompilerParams(vmem_limit_bytes=40 * 1024 * 1024),
+        name=name,
+    )
 
 
 def dense_shards(
@@ -631,8 +801,6 @@
     exp_local, _, ff_local = w_gate.shape
     n_experts = w_router.shape[1]
     head_cols = w_qkv.shape[2]
-    heads_local = head_cols // HD
-    score_scale = HD ** (-0.5)
     own_start = tp_rank * local_rows
     small_cols = norm_gains.shape[1]
     fsdp = FINE[:2]
@@ -651,9 +819,19 @@
     smalls, tokens_own = fence([send(small, swap) for swap in tp_swaps], tokens)
     small = small + smalls[0] + smalls[1] + smalls[2]
     weights_own = jnp.concatenate(
-        [w_qkv.transpose(1, 0, 2).reshape(w_qkv.shape[1], -1), w_out.T, small], axis=1
+        [w_qkv.transpose(1, 0, 2).reshape(w_qkv.shape[1], -1), small], axis=1
     )
     weights_full = lax.all_gather(weights_own, fsdp, axis=0, tiled=True)
+    block = w_out.shape[1]
+    out_full = jnp.zeros((width, w_out.shape[0]), jnp.bfloat16)
+    out_column, tokens_own = fence(w_out.T, tokens_own)
+    for steps in range(GRID[0]):
+        out_beside = send(out_column, SWAP_X)
+        for piece_x, piece_values in ((x, out_column), (1 - x, out_beside)):
+            start = ((z - steps) % GRID[0] * GRID[1] + piece_x) * block
+            out_full = lax.dynamic_update_slice_in_dim(out_full, piece_values, start, 0)
+        if steps < GRID[0] - 1:
+            out_column = send(out_column, z_shifts[0])
     names = jnp.arange(n_experts, dtype=jnp.int32)
     own_ids = own_rows(expert_ids)
     named = (own_ids[:, :, None] == names[None, None, :]).any(axis=1)
@@ -665,19 +843,24 @@
     rows_x = four_rows(mine, theirs).astype(jnp.float32)
     scale1 = lax.rsqrt(jnp.mean(rows_x * rows_x, axis=-1, keepdims=True) + EPSILON)
     own_weights = (w_gate, w_up, w_down)
-    grads_own, weights_own, weights_full, scale1, rows_x = fence(
-        grads_own, own_weights, weights_full, scale1, rows_x
+    grads_own, weights_own, weights_full, scale1, rows_x, out_full = fence(
+        grads_own, own_weights, weights_full, scale1, rows_x, out_full
     )
     all_grads_abs = lax.all_gather(grads_own, FINE[:3], axis=0, tiled=True)
     other_weights = tuple(send(weight, SWAP_CORE) for weight in weights_own)
     qkv_full = weights_full[:, : 3 * head_cols]
-    out_full = weights_full[:, 3 * head_cols : 4 * head_cols]
-    router_wide = weights_full[:, 4 * head_cols :]
+    router_wide = weights_full[:, 3 * head_cols :]
     router_full = router_wide[:, :n_experts]
     gains_wide = router_wide[:, n_experts : n_experts + 4].T.astype(jnp.float32)
 
-    cosine, sine = rope_tables(seq_len, HD)
-    allowed = allowed_mask(seg_ids[0], pad_mask[0], 0, seq_len)
+    cosine, sine = (table[:, 0] for table in rope_tables(seq_len, HD))
+    turns = (
+        jnp.concatenate([cosine, cosine], axis=1),
+        jnp.concatenate([-sine, sine], axis=1),
+        seg_ids.T,
+        seg_ids,
+        pad_mask,
+    )
     x_own = tokens.astype(jnp.float32)
     col_start = tp_rank * head_cols
     gain_query = lax.dynamic_slice_in_dim(gains_wide[2], col_start, head_cols)
@@ -686,32 +869,17 @@
     projected = jnp.dot(rows1, qkv_full, preferred_element_type=jnp.float32)
     query_raw = projected[:, :head_cols]
     key_raw = projected[:, head_cols : 2 * head_cols]
-    values = projected[:, 2 * head_cols :].astype(jnp.bfloat16).reshape(seq_len, heads_local, HD)
     squares = side_totals(
         jnp.sum(query_raw * query_raw, axis=-1), jnp.sum(key_raw * key_raw, axis=-1)
     )
     scale_q = lax.rsqrt(squares[0] / width + EPSILON)[:, None]
     scale_k = lax.rsqrt(squares[1] / width + EPSILON)[:, None]
-    unit_q = query_raw * scale_q
-    unit_k = key_raw * scale_k
-    queries = rotate((unit_q * gain_query).reshape(seq_len, heads_local, HD), cosine, sine).astype(
-        jnp.bfloat16
-    )
-    keys = rotate((unit_k * gain_key).reshape(seq_len, heads_local, HD), cosine, sine).astype(
-        jnp.bfloat16
-    )
-    raw_scores = (
-        jnp.einsum("qhd,khd->hqk", queries, keys, preferred_element_type=jnp.float32) * score_scale
-    )
-    scores = jnp.where(allowed[None], raw_scores, NEG_FILL)
-    powered = jnp.exp(scores - jnp.max(scores, axis=-1, keepdims=True))
-    probs = powered / jnp.sum(powered, axis=-1, keepdims=True)
-    probs_low = probs.astype(jnp.bfloat16)
-    mixed = (
-        jnp.einsum("hqk,khd->qhd", probs_low, values, preferred_element_type=jnp.float32)
-        .reshape(seq_len, head_cols)
-        .astype(jnp.bfloat16)
-    )
+    low_heads = ((seq_len, head_cols), jnp.bfloat16)
+    wide_heads = ((seq_len, head_cols), jnp.float32)
+    norms = (scale_q, scale_k, gain_query[None], gain_key[None])
+    mixed, queries, keys, values, log_sums = small_call(
+        attend_kernel, [low_heads] * 4 + [((seq_len, LANES), jnp.float32)], "attend"
+    )(projected, *norms, *turns)
     away, mine = core_split(
         lax.dot_general(mixed, out_full, CONTRACT_LAST, preferred_element_type=jnp.float32)
     )
@@ -731,10 +899,10 @@
         return send(column, z_shifts[0])
 
     def experts(at):
-        plane = (z - at) % GRID[0] * (GRID[1] * GRID[2])
         beside = jnp.where(core == 0, (1 - x) * GRID[2] + y, x * GRID[2] + 1 - y)
         across = jnp.where(core == 0, x * GRID[2] + 1 - y, (1 - x) * GRID[2] + y)
         opposite = (1 - x) * GRID[2] + 1 - y
+        plane = (z - at) % GRID[0] * (GRID[1] * GRID[2])
         blocks = plane + jnp.stack([x * GRID[2] + y, beside, across, opposite])
         before = [results[at - 1][index] for index in (2, 3, 5, 6)] if at else []
         return expert_rows(
@@ -890,44 +1058,38 @@
     mine = side_pair(hidden_low, far)
     theirs, mine, outputs, all_hidden = fence(send(mine, SWAP_CORE), mine, outputs, all_hidden)
     hidden_rows = four_rows(mine, theirs)
-    mixed_grad = jnp.dot(hidden_rows, out_full, preferred_element_type=jnp.float32).astype(
-        jnp.bfloat16
-    )
-    mixed_grad, grad_out_full = fence(
-        mixed_grad, pair_dots(hidden_rows, mixed).astype(jnp.bfloat16)
+    grad_out_full, hidden_rows = fence(
+        pair_dots(hidden_rows, mixed).astype(jnp.bfloat16), hidden_rows
     )
     grad_out = (
         lax.psum_scatter(grad_out_full, fsdp, scatter_dimension=0, tiled=True)
         .astype(jnp.float32)
         .T
     )
-    mixed_grad = mixed_grad.reshape(seq_len, heads_local, HD)
-    prob_grad = jnp.einsum("qhd,khd->hqk", mixed_grad, values, preferred_element_type=jnp.float32)
-    delta = jnp.sum(probs * prob_grad, axis=-1, keepdims=True)
-    score_grad = (probs * (prob_grad - delta)).astype(jnp.bfloat16)
-    value_grad = jnp.einsum(
-        "hqk,qhd->khd", probs_low, mixed_grad, preferred_element_type=jnp.float32
-    )
-    query_grad = (
-        jnp.einsum("hqk,khd->qhd", score_grad, keys, preferred_element_type=jnp.float32)
-        * score_scale
-    )
-    key_grad = (
-        jnp.einsum("hqk,qhd->khd", score_grad, queries, preferred_element_type=jnp.float32)
-        * score_scale
-    )
-    query_norm_grad = rotate_back(query_grad, cosine, sine).reshape(seq_len, head_cols)
-    key_norm_grad = rotate_back(key_grad, cosine, sine).reshape(seq_len, head_cols)
-    gain_query_grad = jnp.sum(query_norm_grad * unit_q, axis=0)
-    gain_key_grad = jnp.sum(key_norm_grad * unit_k, axis=0)
-    scaled_q = query_norm_grad * gain_query
-    scaled_k = key_norm_grad * gain_key
-    inners = side_totals(jnp.sum(scaled_q * unit_q, axis=-1), jnp.sum(scaled_k * unit_k, axis=-1))
+    output_seconds, (scaled_q, scaled_k, value_grad, inners, gain_grads), outputs = fence(
+        [send(pair[1], SWAP_SECOND) for pair in outputs[:2]],
+        small_call(
+            attend_back_kernel,
+            [
+                wide_heads,
+                wide_heads,
+                low_heads,
+                ((seq_len, 2), jnp.float32),
+                ((2, head_cols), jnp.float32),
+            ],
+            "attend_back",
+        )(hidden_rows, out_full, queries, keys, values, log_sums, projected, *norms, *turns),
+        outputs,
+    )
+    gain_query_grad, gain_key_grad = gain_grads[0], gain_grads[1]
+    inners = side_totals(inners[:, 0], inners[:, 1])
+    unit_q = query_raw * scale_q
+    unit_k = key_raw * scale_k
     query_raw_grad = scale_q * (scaled_q - unit_q * (inners[0] / width)[:, None])
     key_raw_grad = scale_k * (scaled_k - unit_k * (inners[1] / width)[:, None])
     qkv_grad = jnp.concatenate(
-        [query_raw_grad, key_raw_grad, value_grad.reshape(seq_len, head_cols)], axis=1
-    ).astype(jnp.bfloat16)
+        [query_raw_grad.astype(jnp.bfloat16), key_raw_grad.astype(jnp.bfloat16), value_grad], axis=1
+    )
     normed1_part = lax.dot_general(
         qkv_grad, qkv_full, CONTRACT_LAST, preferred_element_type=jnp.float32
     )
@@ -953,15 +1115,16 @@
     away, mine, outputs, all_hidden, all_active, _ = fence(
         away, mine, outputs, all_hidden, all_active, grad_full
     )
-    back, mine, output_seconds, others, more, other_down, all_hidden = fence(
+    back, mine, output_rest, others, more, other_down, all_hidden = fence(
         send(away, SWAP_CORE),
         mine,
-        [send(pair[1], SWAP_SECOND) for pair in outputs],
+        [send(pair[1], SWAP_SECOND) for pair in outputs[2:]],
         [send(other, SWAP_CORE) for other in others],
         [pair_dots(all_rows, piece(pair_count + at)) for at in range(2, pair_count)],
         pair_dots(all_active[:, units:], all_grads),
         all_hidden,
     )
+    output_seconds = [*output_seconds, *output_rest]
     away, kept = side_split(mine, back)
     output_firsts = [
         send(first_part(pair[0], second), SWAP_FIRST)

time: 761 us -> 725 us (0.953)
  waiting for transfers between devices: 323 us -> 298 us
  Pallas kernels: 116 us -> 98.9 us
  local copies, waits for them, and re-layouts: 47.2 us -> 62.5 us
  matrix products: 117 us -> 103 us
  starting transfers between devices: 62.3 us -> 71.5 us
    all_gather x1, waiting for transfers between devices: 109 us -> 65.4 us  [dense_shards(): weights_full = lax.all_gather(weights_own, fsdp, axis=0, tiled=True)]
    reduce_scatter x1, waiting for transfers between devices: 40 us -> 66.9 us  [dense_shards(): lax.psum_scatter(grad_full, fsdp, scatter_dimension=0, tiled=True)]
    ppermute x60 -> x67, waiting for transfers between devices: 174 us -> 152 us  [send(): return lax.ppermute(values, FINE, pairs)]
    pallas_call x4 -> x6, Pallas kernels: 116 us -> 98.9 us  [the longest x4 83.1 us: expert_rows(): pl.pallas_call(functools.partial(expert_kernel, n_experts=n_experts, at=a...]
    unnamed x194 -> x175, local copies, waits for them, and re-layouts: 16.1 us -> 30.6 us
    all_gather x1, waiting for transfers between devices: 0.01 us -> 13.8 us  [dense_shards(): all_grads_abs = lax.all_gather(grads_own, FINE[:3], axis=0, tiled=True)]
    dot_general x6 -> x0, matrix products: 13.3 us -> none  [the longest x1 3.67 us: dense_shards(): jnp.dot(hidden_rows, out_full, preferred_element_type=jnp.float32)]
    ppermute x60 -> x67, starting transfers between devices: 61.9 us -> 71.1 us  [send(): return lax.ppermute(values, FINE, pairs)]
  transfers between devices with their start and end apart: 64 -> 71, of which waited for: 22 -> 26; matrix products, arithmetic and copies ran while one was open for 28% -> 26% of each run, Pallas kernels for 15% -> 14%
where the time goes in v4:
time: 725 us; the launch traced here: 716 us
  waiting for transfers between devices  298 us (41%)
  matrix products  103 us (14%)
  Pallas kernels  98.9 us (14%)
  starting transfers between devices  71.5 us (10%)
  local copies, waits for them, and re-layouts  62.5 us (9%)
  other arithmetic  54 us (7%)
  between operations  15.3 us (2%)
  blocking collectives  12.2 us (2%)
    ppermute x67, waiting for transfers between devices, send(): return lax.ppermute(values, FINE, pairs)  152 us
    pallas_call x4, Pallas kernels, expert_rows(): pl.pallas_call(functools.partial(expert_kernel, n_experts=n_experts, at=a...  83.1 us
    ppermute x67, starting transfers between devices, send(): return lax.ppermute(values, FINE, pairs)  71.1 us
    dot_general x13, matrix products, pair_dots(): lax.dot_general(left, right, (((0,), (0,)), ((), ())), preferred_element_...  69.6 us
    reduce_scatter x1, waiting for transfers between devices, dense_shards(): lax.psum_scatter(grad_full, fsdp, scatter_dimension=0, tiled=True)  66.9 us
    all_gather x1, waiting for transfers between devices, dense_shards(): weights_full = lax.all_gather(weights_own, fsdp, axis=0, tiled=True)  65.4 us
    unnamed x175, local copies, waits for them, and re-layouts  30.6 us
  transfers between devices with their start and end apart: 71, of which 26 were waited for; matrix products, arithmetic and copies ran while one was open for 26% of the time, Pallas kernels for 14%

profile of v4, /device:TPU:9, one launch (start us, length us, event | category | flops | bytes accessed | tf_op | source)
XLA Modules:
  0.0 715.7 jit_solution(4772071297497918836)
XLA Ops:
  49.2 6.7 collective-permute-done.10
  66.0 65.4 %all-gather.3.cloned.1.call-done = bf16[2048,1664]{0,1:T(8,128)(2,1)} async-done(((bf16[256,1664]{0,1:T(8,128)(2,1)}), bf16[2048,1664]{0,1:T(8,128)(2,1)}) %all-gather.3.cloned.1.call-update) | async-done | bytes 6815760 | tf_op jit(solution)/shard_map/all_gather | solution.py:824
  135.1 6.9 fusion.2.projected_ref
  172.5 13.5 %collective-permute-done.13 = bf16[128,2048]{1,0:T(8,128)(2,1)S(1)} collective-permute-done((bf16[128,2048]{1,0:T(8,128)(2,1)S(1)}, bf16[128,2048]{1,0:T(8,128)(2,1)S(1)}, u32[]{:S(2)}, u32[]{:S(2)}) %collective-permute-start.13) | collective-permute-done | bytes 524320 | tf_op jit(solution)/shard_map/ppermute | solution.py:397
  191.3 13.1 %collective-permute-done.14 = bf16[128,2048]{1,0:T(8,128)(2,1)S(1)} collective-permute-done((bf16[128,2048]{1,0:T(8,128)(2,1)S(1)}, bf16[128,2048]{1,0:T(8,128)(2,1)S(1)}, u32[]{:S(2)}, u32[]{:S(2)}) %collective-permute-start.14) | collective-permute-done | bytes 524320 | tf_op jit(solution)/shard_map/ppermute | solution.py:397
  211.7 29.2 %collective-permute-done.16 = bf16[128,2048]{1,0:T(8,128)(2,1)S(1)} collective-permute-done((bf16[128,2048]{1,0:T(8,128)(2,1)S(1)}, bf16[128,2048]{1,0:T(8,128)(2,1)S(1)}, u32[]{:S(2)}, u32[]{:S(2)}) %collective-permute-start.16) | collective-permute-done | bytes 524320 | tf_op jit(solution)/shard_map/ppermute | solution.py:397
  243.0 9.4 %collective-permute-done.17 = bf16[128,2048]{1,0:T(8,128)(2,1)S(1)} collective-permute-done((bf16[128,2048]{1,0:T(8,128)(2,1)S(1)}, bf16[128,2048]{1,0:T(8,128)(2,1)S(1)}, u32[]{:S(2)}, u32[]{:S(2)}) %collective-permute-start.17) | collective-permute-done | bytes 524320 | tf_op jit(solution)/shard_map/ppermute | solution.py:397
  263.1 13.8 %all-gather.5.cloned.1.call-done.grads0_ref.grads1_ref.grads2_ref.grads3_ref = bf16[2048,2176]{1,0:T(8,128)(2,1)} async-done(((bf16[128,2176]{1,0:T(8,128)(2,1)}), bf16[2048,2176]{1,0:T(8,128)(2,1)}) %all-gather.5.cloned.1.call-update) | async-done | bytes 8912912 | tf_op jit(solution)/shard_map/all_gather | solution.py:849
  280.4 20.6 %expert_rows.4 = (bf16[256,2048]{1,0:T(8,128)(2,1)S(1)}, bf16[256,2048]{1,0:T(8,128)(2,1)S(1)}, bf16[2048,1024]{1,0:T(8,128)(2,1)}, bf16[2048,2048]{1,0:T(8,128)...) custom-call(s32[4]{0:T(128)S(1)} %get-tuple-element.502.blocks_ref, ...), custom_call_target="tpu_custom_call" | custom-call | flops 1024 | bytes 1024 | tf_op jit(solution)/shard_map/expert_rows/pallas_call | solution.py:586
  305.8 21.1 %expert_rows.5 = (bf16[256,2048]{1,0:T(8,128)(2,1)S(1)}, bf16[256,2048]{1,0:T(8,128)(2,1)S(1)}, bf16[2048,1024]{1,0:T(8,128)(2,1)}, bf16[2048,2048]{1,0:T(8,128)...) custom-call(s32[4]{0:T(128)S(1)} %get-tuple-element.501.blocks_ref, ...), custom_call_target="tpu_custom_call", output_to_operand_aliasing={{2}: (15, {}), {3}: (16, {}), {5}: (17, {}), {6}: (18, {})} | custom-call | flops 1024 | bytes 1024 | tf_op jit(solution)/shard_map/expert_rows/pallas_call | solution.py:586
  328.0 7.1 collective-permute-done.27
  337.7 20.8 %expert_rows.6 = (bf16[256,2048]{1,0:T(8,128)(2,1)S(1)}, bf16[256,2048]{1,0:T(8,128)(2,1)S(1)}, bf16[2048,1024]{1,0:T(8,128)(2,1)}, bf16[2048,2048]{1,0:T(8,128)...) custom-call(s32[4]{0:T(128)S(1)} %get-tuple-element.500.blocks_ref, ...), custom_call_target="tpu_custom_call", output_to_operand_aliasing={{2}: (15, {}), {3}: (16, {}), {5}: (17, {}), {6}: (18, {})} | custom-call | flops 1024 | bytes 1024 | tf_op jit(solution)/shard_map/expert_rows/pallas_call | solution.py:586
  358.5 7.5 %collective-permute-done.29 = bf16[256,2048]{1,0:T(8,128)(2,1)S(1)} collective-permute-done((bf16[256,2048]{1,0:T(8,128)(2,1)S(1)}, bf16[256,2048]{1,0:T(8,128)(2,1)S(1)}, u32[]{:S(2)}, u32[]{:S(2)}) %collective-permute-start.29) | collective-permute-done | bytes 1048608 | tf_op jit(solution)/shard_map/ppermute | solution.py:397
  369.5 20.5 %expert_rows.7 = (bf16[256,2048]{1,0:T(8,128)(2,1)S(1)}, bf16[256,2048]{1,0:T(8,128)(2,1)S(1)}, bf16[2048,1024]{1,0:T(8,128)(2,1)}, bf16[2048,2048]{1,0:T(8,128)...) custom-call(s32[4]{0:T(128)S(1)} %get-tuple-element.460.blocks_ref, ...), custom_call_target="tpu_custom_call", output_to_operand_aliasing={{2}: (15, {}), {3}: (16, {}), {5}: (17, {}), {6}: (18, {})} | custom-call | flops 1024 | bytes 1024 | tf_op jit(solution)/shard_map/expert_rows/pallas_call | solution.py:586
  399.9 9.3 %collective-permute-done.36 = f32[4,16,256]{2,1,0:T(8,128)S(1)} collective-permute-done((f32[4,16,256]{2,1,0:T(8,128)S(1)}, f32[4,16,256]{2,1,0:T(8,128)S(1)}, u32[]{:S(2)}, u32[]{:S(2)}) %collective-permute-start.36) | collective-permute-done | bytes 65568 | tf_op jit(solution)/shard_map/ppermute | solution.py:397
  412.6 13.2 %convolution_convert_fusion.1 = bf16[2048,2048]{1,0:T(8,128)(2,1)} fusion(bf16[2048,1024]{1,0:T(8,128)(2,1)S(1)} %copy-done.35, bf16[1024,2048]{1,0:T(8,128)(2,1)} %pad_maximum_fusion.1), kind=kOutput, calls=%fused_computation.1 | convolution fusion | flops 8594128896 | bytes 16777216 | tf_op jit(solution)/shard_map/dot_general | solution.py:1015
  425.8 8.8 %collective-permute-done.38 = bf16[128,2048]{1,0:T(8,128)(2,1)S(1)} collective-permute-done((bf16[128,2048]{1,0:T(8,128)(2,1)S(1)}, bf16[128,2048]{1,0:T(8,128)(2,1)S(1)}, u32[]{:S(2)}, u32[]{:S(2)}) %collective-permute-start.38) | collective-permute-done | bytes 524320 | tf_op jit(solution)/shard_map/ppermute | solution.py:397
  490.6 10.4 %attend_back.1 = (f32[512,512]{1,0:T(8,128)S(1)}, f32[512,512]{1,0:T(8,128)S(1)}, bf16[512,512]{1,0:T(8,128)(2,1)S(1)}, f32[512,2]{1,0:T(8,128)S(1)}, f32[2,512]{1,0:T(2,128)S(1)}) custom-call(bf16[512,2048]{1,0:T(8,128)(2,1)S(1)} %bitcast.119, bf16[2048,512]{1,0:T(8,128)(2,1)} %constant_dynamic-update-slice_fusion.8.out_ref, ...), custom_call_target="tpu_custom_call" | custom-call | flops 1024 | bytes 1024 | tf_op jit(solution)/shard_map/attend_back/pallas_call | solution.py:1071
  525.2 6.9 pad_maximum_fusion
  534.9 10.5 %fusion.7 = f32[512,2048]{1,0:T(8,128)} fusion(bf16[2048,2048]{1,0:T(8,128)(2,1)} %get-tuple-element.375, bf16[2048,1024]{1,0:T(8,128)(2,1)S(1)} %copy-done.36), kind=kOutput, calls=%fused_computation.26 | convolution fusion | flops 4294967296 | bytes 14680064 | tf_op jit(solution)/shard_map/dot_general | solution.py:417
  553.1 8.8 %collective-permute-done.50 = bf16[256,2048]{1,0:T(8,128)(2,1)S(1)} collective-permute-done((bf16[256,2048]{1,0:T(8,128)(2,1)S(1)}, bf16[256,2048]{1,0:T(8,128)(2,1)S(1)}, u32[]{:S(2)}, u32[]{:S(2)}) %collective-permute-start.50) | collective-permute-done | bytes 1048608 | tf_op jit(solution)/shard_map/ppermute | solution.py:397
  606.1 7.3 %fusion.4 = f32[1,2048,256]{2,1,0:T(8,128)S(1)} fusion(f32[2048,256]{1,0:T(8,128)} %collective-permute-done.59, bf16[2048,2048]{1,0:T(8,128)(2,1)} %get-tuple-element.307, bf16[2048,2048]{1,0:T(8,128)(2,1)} %get-tuple-element.398), kind=kOutput, calls=%fused_computation.17 | convolution fusion | flops 2148007936 | bytes 13631488 | tf_op jit(solution)/shard_map/dot_general | solution.py:417
  621.0 7.8 %convolution_add_fusion = f32[512,2048]{1,0:T(8,128)} fusion(f32[512,2048]{1,0:T(8,128)} %collective-permute-done.60, bf16[2048,2048]{1,0:T(8,128)(2,1)S(1)} %bitcast.126, bf16[2048,1024]{1,0:T(8,128)(2,1)S(1)} %copy-done.37), kind=kOutput, calls=%fused_computation.13 | convolution fusion | flops 4296015872 | bytes 18874368 | tf_op jit(solution)/shard_map/dot_general | solution.py:417
  631.1 66.9 %reduce-scatter.3.cloned.1.call-done = bf16[256,1664]{0,1:T(8,128)(2,1)} async-done(((bf16[2048,1664]{0,1:T(8,128)(2,1)}), bf16[256,1664]{0,1:T(8,128)(2,1)}) %reduce-scatter.3.cloned.1.call-update) | async-done | bytes 851984 | tf_op jit(solution)/shard_map/reduce_scatter | solution.py:1110
  (446 shorter events, 294.7 us)
Async XLA Ops:
  7.2 124.2 %all-gather.3.cloned.1.call-start = ((), (), s32[]{:S(2)}) async-start(), calls=%async_computation.2 | async-start | bytes 7667712 | tf_op jit(solution)/shard_map/all_gather | solution.py:824
  16.5 260.3 %all-gather.5.cloned.1.call-start = ((), (), s32[]{:S(2)}) async-start(), calls=%async_computation.3 | async-start | bytes 9469952 | tf_op jit(solution)/shard_map/all_gather | solution.py:849
  31.5 31.3 %collective-permute-start.4 = (bf16[2,128,2048]{2,1,0:T(8,128)(2,1)}, bf16[2,128,2048]{2,1,0:T(8,128)(2,1)S(1)}, u32[]{:S(2)}, u32[]{:S(2)}) collective-permute-start(bf16[2,128,2048]{2,1,0:T(8,128)(2,1)} %pad_maximum_fusion.6), channel_id=1, source_target_pairs={{0,1},{1,0},{2,3},{3,2},{4,5},{5,4},{6,7},{7,6},{8,9},{9,8},{10,11... | collective-permute-start | bytes 3145736 | tf_op jit(solution)/shard_map/ppermute | solution.py:397
  131.4 459.2 %reduce-scatter.5.cloned.1.call-start = ((), (), s32[]{:S(2)}) async-start(), calls=%async_computation.5 | async-start | bytes 2359296 | tf_op jit(solution)/shard_map/reduce_scatter | solution.py:1065
  189.3 67.3 %collective-permute-start.22 = (bf16[2,2048,256]{2,1,0:T(8,128)(2,1)}, bf16[2,2048,256]{2,1,0:T(8,128)(2,1)}, u32[]{:S(2)}, u32[]{:S(2)}) collective-permute-start(bf16[2,2048,256]{2,1,0:T(8,128)(2,1)} %refs_0_.7), channel_id=1, source_target_pairs={{0,1},{1,0},{2,3},{3,2},{4,5},{5,4},{6,7},{7,6},{8,9},{9,8},{10,11... | collective-permute-start | bytes 6291464 | tf_op jit(solution)/shard_map/ppermute | solution.py:397
  204.4 36.5 %collective-permute-start.16 = (bf16[128,2048]{1,0:T(8,128)(2,1)S(1)}, bf16[128,2048]{1,0:T(8,128)(2,1)S(1)}, u32[]{:S(2)}, u32[]{:S(2)}) collective-permute-start(bf16[128,2048]{1,0:T(8,128)(2,1)S(1)} %collective-permute-done.14), channel_id=1, source_target_pairs={{0,8},{1,9},{2,10},{3,11},{4,12},{5,13},{6,14},{7,15},{8,16},{9,17... | collective-permute-start | bytes 1572872 | tf_op jit(solution)/shard_map/ppermute | solution.py:397
  207.5 44.9 %collective-permute-start.18 = (bf16[256,2048]{1,0:T(8,128)(2,1)S(1)}, bf16[256,2048]{1,0:T(8,128)(2,1)S(1)}, u32[]{:S(2)}, u32[]{:S(2)}) collective-permute-start(bf16[256,2048]{1,0:T(8,128)(2,1)S(1)} %pad_maximum_fusion.7.near_ref), channel_id=1, source_target_pairs={{0,2},{1,5},{2,0},{3,7},{4,6},{5,1},{6,4},{7,3},{8,10},{9,13},{10,... | collective-permute-start | bytes 3145736 | tf_op jit(solution)/shard_map/ppermute | solution.py:397
  208.6 54.5 %collective-permute-start.23 = (bf16[2,2048,256]{2,1,0:T(8,128)(2,1)}, bf16[2,2048,256]{2,1,0:T(8,128)(2,1)}, u32[]{:S(2)}, u32[]{:S(2)}) collective-permute-start(bf16[2,2048,256]{2,1,0:T(8,128)(2,1)} %refs_1_.7), channel_id=1, source_target_pairs={{0,1},{1,0},{2,3},{3,2},{4,5},{5,4},{6,7},{7,6},{8,9},{9,8},{10,11... | collective-permute-start | bytes 6291464 | tf_op jit(solution)/shard_map/ppermute | solution.py:397
  211.7 51.4 %collective-permute-start.24 = (bf16[2,256,2048]{2,1,0:T(8,128)(2,1)}, bf16[2,256,2048]{2,1,0:T(8,128)(2,1)}, u32[]{:S(2)}, u32[]{:S(2)}) collective-permute-start(bf16[2,256,2048]{2,1,0:T(8,128)(2,1)} %refs_2_.7), channel_id=1, source_target_pairs={{0,1},{1,0},{2,3},{3,2},{4,5},{5,4},{6,7},{7,6},{8,9},{9,8},{10,11... | collective-permute-start | bytes 6291464 | tf_op jit(solution)/shard_map/ppermute | solution.py:397
  254.3 46.8 %collective-permute-start.21 = (bf16[256,2048]{1,0:T(8,128)(2,1)}, bf16[256,2048]{1,0:T(8,128)(2,1)}, u32[]{:S(2)}, u32[]{:S(2)}) collective-permute-start(bf16[256,2048]{1,0:T(8,128)(2,1)} %constant_dynamic-update-slice_fusion.near_ref), channel_id=1, source_target_pairs={{0,2},{1,5},{2,0},{3,7},{4,6},{5,1},{6,4},{7,3},{8,10},{9,13},{10,... | collective-permute-start | bytes 3145736 | tf_op jit(solution)/shard_map/ppermute | solution.py:397
  255.3 45.8 %collective-permute-start.19 = (bf16[128,2048]{1,0:T(8,128)(2,1)}, bf16[128,2048]{1,0:T(8,128)(2,1)}, u32[]{:S(2)}, u32[]{:S(2)}) collective-permute-start(bf16[128,2048]{1,0:T(8,128)(2,1)} %copy-done.65), channel_id=1, source_target_pairs={{0,8},{1,9},{2,10},{3,11},{4,12},{5,13},{6,14},{7,15},{8,16},{9,17... | collective-permute-start | bytes 1572872 | tf_op jit(solution)/shard_map/ppermute | solution.py:397
  256.7 44.4 %collective-permute-start.20 = (bf16[128,2048]{1,0:T(8,128)(2,1)}, bf16[128,2048]{1,0:T(8,128)(2,1)}, u32[]{:S(2)}, u32[]{:S(2)}) collective-permute-start(bf16[128,2048]{1,0:T(8,128)(2,1)} %copy-done.65), channel_id=1, source_target_pairs={{0,4},{1,3},{2,6},{3,1},{4,0},{5,7},{6,2},{7,5},{8,12},{9,11},{10,... | collective-permute-start | bytes 1572872 | tf_op jit(solution)/shard_map/ppermute | solution.py:397
  305.8 29.3 %collective-permute-start.27 = (bf16[256,2048]{1,0:T(8,128)(2,1)S(1)}, bf16[256,2048]{1,0:T(8,128)(2,1)S(1)}, u32[]{:S(2)}, u32[]{:S(2)}) collective-permute-start(bf16[256,2048]{1,0:T(8,128)(2,1)S(1)} %get-tuple-element.238), channel_id=1, source_target_pairs={{0,2},{1,5},{2,0},{3,7},{4,6},{5,1},{6,4},{7,3},{8,10},{9,13},{10,... | collective-permute-start | bytes 3145736 | tf_op jit(solution)/shard_map/ppermute | solution.py:397
  336.7 29.3 %collective-permute-start.29 = (bf16[256,2048]{1,0:T(8,128)(2,1)S(1)}, bf16[256,2048]{1,0:T(8,128)(2,1)S(1)}, u32[]{:S(2)}, u32[]{:S(2)}) collective-permute-start(bf16[256,2048]{1,0:T(8,128)(2,1)S(1)} %get-tuple-element.253), channel_id=1, source_target_pairs={{0,2},{1,5},{2,0},{3,7},{4,6},{5,1},{6,4},{7,3},{8,10},{9,13},{10,... | collective-permute-start | bytes 3145736 | tf_op jit(solution)/shard_map/ppermute | solution.py:397
  471.9 31.1 %collective-permute-start.46 = (bf16[256,2048]{1,0:T(8,128)(2,1)}, bf16[256,2048]{1,0:T(8,128)(2,1)}, u32[]{:S(2)}, u32[]{:S(2)}) collective-permute-start(bf16[256,2048]{1,0:T(8,128)(2,1)} %get-tuple-element.333), channel_id=1, source_target_pairs={{0,2},{1,5},{2,0},{3,7},{4,6},{5,1},{6,4},{7,3},{8,10},{9,13},{10,... | collective-permute-start | bytes 3145736 | tf_op jit(solution)/shard_map/ppermute | solution.py:397
  472.1 30.9 %collective-permute-start.47 = (bf16[256,2048]{1,0:T(8,128)(2,1)}, bf16[256,2048]{1,0:T(8,128)(2,1)}, u32[]{:S(2)}, u32[]{:S(2)}) collective-permute-start(bf16[256,2048]{1,0:T(8,128)(2,1)} %get-tuple-element.334), channel_id=1, source_target_pairs={{0,2},{1,5},{2,0},{3,7},{4,6},{5,1},{6,4},{7,3},{8,10},{9,13},{10,... | collective-permute-start | bytes 3145736 | tf_op jit(solution)/shard_map/ppermute | solution.py:397
  478.5 219.5 %reduce-scatter.3.cloned.1.call-start = ((), (), s32[]{:S(2)}) async-start(), calls=%async_computation.4 | async-start | bytes 7667712 | tf_op jit(solution)/shard_map/reduce_scatter | solution.py:1110
  480.0 73.0 %collective-permute-start.51 = (f32[2048,256]{1,0:T(8,128)}, f32[2048,256]{1,0:T(8,128)}, u32[]{:S(2)}, u32[]{:S(2)}) collective-permute-start(f32[2048,256]{1,0:T(8,128)} %fusion.29), channel_id=1, source_target_pairs={{0,1},{1,0},{2,3},{3,2},{4,5},{5,4},{6,7},{7,6},{8,9},{9,8},{10,11... | collective-permute-start | bytes 6291464 | tf_op jit(solution)/shard_map/ppermute | solution.py:397
  481.0 72.0 %collective-permute-start.52 = (f32[2048,256]{1,0:T(8,128)}, f32[2048,256]{1,0:T(8,128)}, u32[]{:S(2)}, u32[]{:S(2)}) collective-permute-start(f32[2048,256]{1,0:T(8,128)} %fusion.27), channel_id=1, source_target_pairs={{0,1},{1,0},{2,3},{3,2},{4,5},{5,4},{6,7},{7,6},{8,9},{9,8},{10,11... | collective-permute-start | bytes 6291464 | tf_op jit(solution)/shard_map/ppermute | solution.py:397
  533.6 28.3 %collective-permute-start.50 = (bf16[256,2048]{1,0:T(8,128)(2,1)S(1)}, bf16[256,2048]{1,0:T(8,128)(2,1)S(1)}, u32[]{:S(2)}, u32[]{:S(2)}) collective-permute-start(bf16[256,2048]{1,0:T(8,128)(2,1)S(1)} %copy-done.57), channel_id=1, source_target_pairs={{0,2},{1,5},{2,0},{3,7},{4,6},{5,1},{6,4},{7,3},{8,10},{9,13},{10,... | collective-permute-start | bytes 3145736 | tf_op jit(solution)/shard_map/ppermute | solution.py:397
  561.9 32.6 %collective-permute-start.60 = (f32[512,2048]{1,0:T(8,128)}, f32[512,2048]{1,0:T(8,128)}, u32[]{:S(2)}, u32[]{:S(2)}) collective-permute-start(f32[512,2048]{1,0:T(8,128)} %fusion.7), channel_id=1, source_target_pairs={{0,1},{1,0},{2,3},{3,2},{4,5},{5,4},{6,7},{7,6},{8,9},{9,8},{10,11... | collective-permute-start | bytes 12582920 | tf_op jit(solution)/shard_map/ppermute | solution.py:397
  597.0 103.9 %collective-permute-start.61 = (bf16[128,2048]{1,0:T(8,128)(2,1)}, bf16[128,2048]{1,0:T(8,128)(2,1)}, u32[]{:S(2)}, u32[]{:S(2)}) collective-permute-start(bf16[128,2048]{1,0:T(8,128)(2,1)} %add_convert_fusion.3), channel_id=1, source_target_pairs={{0,24},{1,25},{2,26},{3,27},{4,28},{5,29},{6,30},{7,31},{8,0},{9,1... | collective-permute-start | bytes 1572872 | tf_op jit(solution)/shard_map/ppermute | solution.py:397
  602.5 98.9 %collective-permute-start.62 = (bf16[128,2048]{1,0:T(8,128)(2,1)}, bf16[128,2048]{1,0:T(8,128)(2,1)}, u32[]{:S(2)}, u32[]{:S(2)}) collective-permute-start(bf16[128,2048]{1,0:T(8,128)(2,1)} %add_convert_fusion.2), channel_id=1, source_target_pairs={{0,16},{1,17},{2,18},{3,19},{4,20},{5,21},{6,22},{7,23},{8,24},{9,... | collective-permute-start | bytes 1572872 | tf_op jit(solution)/shard_map/ppermute | solution.py:397
  603.5 97.9 %collective-permute-start.63 = (bf16[128,2048]{1,0:T(8,128)(2,1)}, bf16[128,2048]{1,0:T(8,128)(2,1)}, u32[]{:S(2)}, u32[]{:S(2)}) collective-permute-start(bf16[128,2048]{1,0:T(8,128)(2,1)} %add_convert_fusion.1), channel_id=1, source_target_pairs={{0,8},{1,9},{2,10},{3,11},{4,12},{5,13},{6,14},{7,15},{8,16},{9,17... | collective-permute-start | bytes 1572872 | tf_op jit(solution)/shard_map/ppermute | solution.py:397
  (132 other events, 1616.8 us)
Sparse Core Ops, SparseCore 0:
  16.7 114.6 all-gather.2
  134.3 142.5 all-gather.4
  478.6 64.8 reduce-scatter.4
  547.1 150.8 reduce-scatter.2

commit v5 on v4

--- a/solution.py
+++ b/solution.py
@@ -1023,8 +1023,9 @@
     firsts.append(first)
     homes.append(home)
     dots = dots[..., :part] + dots_back
-    home, dots_back, dots, outputs, all_hidden, others = fence(
+    home, output_early, dots_back, dots, outputs, all_hidden, others = fence(
         route_home(3),
+        send(outputs[0][1], SWAP_SECOND),
         [send(dots[at], shift_z(-at)) for at in range(1, GRID[0])],
         dots[0],
         outputs,
@@ -1067,7 +1068,7 @@
         .T
     )
     output_seconds, (scaled_q, scaled_k, value_grad, inners, gain_grads), outputs = fence(
-        [send(pair[1], SWAP_SECOND) for pair in outputs[:2]],
+        [send(pair[1], SWAP_SECOND) for pair in outputs[1:3]],
         small_call(
             attend_back_kernel,
             [
@@ -1118,13 +1119,13 @@
     back, mine, output_rest, others, more, other_down, all_hidden = fence(
         send(away, SWAP_CORE),
         mine,
-        [send(pair[1], SWAP_SECOND) for pair in outputs[2:]],
+        [send(pair[1], SWAP_SECOND) for pair in outputs[3:]],
         [send(other, SWAP_CORE) for other in others],
         [pair_dots(all_rows, piece(pair_count + at)) for at in range(2, pair_count)],
         pair_dots(all_active[:, units:], all_grads),
         all_hidden,
     )
-    output_seconds = [*output_seconds, *output_rest]
+    output_seconds = [output_early, *output_seconds, *output_rest]
     away, kept = side_split(mine, back)
     output_firsts = [
         send(first_part(pair[0], second), SWAP_FIRST)

time: 725 us -> 738 us (1.018)
  waiting for transfers between devices: 298 us -> 310 us
    reduce_scatter x1, waiting for transfers between devices: 66.9 us -> 80.2 us  [dense_shards(): lax.psum_scatter(grad_full, fsdp, scatter_dimension=0, tiled=True)]
    unnamed x175 -> x169, local copies, waits for them, and re-layouts: 30.6 us -> 31.5 us
  transfers between devices with their start and end apart: 71 -> 71, of which waited for: 26 -> 27; matrix products, arithmetic and copies ran while one was open for 26% -> 25% of each run, Pallas kernels for 14% -> 14%
where the time goes in v5:
time: 738 us; the launch traced here: 727 us
  waiting for transfers between devices  310 us (42%)
  matrix products  100 us (14%)
  Pallas kernels  98.7 us (13%)
  starting transfers between devices  71.9 us (10%)
  local copies, waits for them, and re-layouts  63 us (9%)
  other arithmetic  55.5 us (8%)
  between operations  15.3 us (2%)
  blocking collectives  12.2 us (2%)
    ppermute x67, waiting for transfers between devices, send(): return lax.ppermute(values, FINE, pairs)  151 us
    pallas_call x4, Pallas kernels, expert_rows(): pl.pallas_call(functools.partial(expert_kernel, n_experts=n_experts, at=a...  82.9 us
    reduce_scatter x1, waiting for transfers between devices, dense_shards(): lax.psum_scatter(grad_full, fsdp, scatter_dimension=0, tiled=True)  80.2 us
    ppermute x67, starting transfers between devices, send(): return lax.ppermute(values, FINE, pairs)  71.6 us
    dot_general x13, matrix products, pair_dots(): lax.dot_general(left, right, (((0,), (0,)), ((), ())), preferred_element_...  69.2 us
    all_gather x1, waiting for transfers between devices, dense_shards(): weights_full = lax.all_gather(weights_own, fsdp, axis=0, tiled=True)  65.4 us
    unnamed x169, local copies, waits for them, and re-layouts  31.5 us
  transfers between devices with their start and end apart: 71, of which 27 were waited for; matrix products, arithmetic and copies ran while one was open for 25% of the time, Pallas kernels for 14%

profile of v5, /device:TPU:9, one launch (start us, length us, event | category | flops | bytes accessed | tf_op | source)
XLA Modules:
  0.0 726.6 jit_solution(8243445161771712268)
XLA Ops:
  49.2 6.7 collective-permute-done.10
  66.0 65.4 %all-gather.3.cloned.1.call-done = bf16[2048,1664]{0,1:T(8,128)(2,1)} async-done(((bf16[256,1664]{0,1:T(8,128)(2,1)}), bf16[2048,1664]{0,1:T(8,128)(2,1)}) %all-gather.3.cloned.1.call-update) | async-done | bytes 6815760 | tf_op jit(solution)/shard_map/all_gather | solution.py:824
  135.1 6.9 fusion.2.projected_ref
  142.2 6.6 all-reduce.4
  172.8 13.1 %collective-permute-done.13 = bf16[128,2048]{1,0:T(8,128)(2,1)S(1)} collective-permute-done((bf16[128,2048]{1,0:T(8,128)(2,1)S(1)}, bf16[128,2048]{1,0:T(8,128)(2,1)S(1)}, u32[]{:S(2)}, u32[]{:S(2)}) %collective-permute-start.13) | collective-permute-done | bytes 524320 | tf_op jit(solution)/shard_map/ppermute | solution.py:397
  191.3 13.4 %collective-permute-done.14 = bf16[128,2048]{1,0:T(8,128)(2,1)S(1)} collective-permute-done((bf16[128,2048]{1,0:T(8,128)(2,1)S(1)}, bf16[128,2048]{1,0:T(8,128)(2,1)S(1)}, u32[]{:S(2)}, u32[]{:S(2)}) %collective-permute-start.14) | collective-permute-done | bytes 524320 | tf_op jit(solution)/shard_map/ppermute | solution.py:397
  212.0 28.9 %collective-permute-done.16 = bf16[128,2048]{1,0:T(8,128)(2,1)S(1)} collective-permute-done((bf16[128,2048]{1,0:T(8,128)(2,1)S(1)}, bf16[128,2048]{1,0:T(8,128)(2,1)S(1)}, u32[]{:S(2)}, u32[]{:S(2)}) %collective-permute-start.16) | collective-permute-done | bytes 524320 | tf_op jit(solution)/shard_map/ppermute | solution.py:397
  243.0 9.3 %collective-permute-done.17 = bf16[128,2048]{1,0:T(8,128)(2,1)S(1)} collective-permute-done((bf16[128,2048]{1,0:T(8,128)(2,1)S(1)}, bf16[128,2048]{1,0:T(8,128)(2,1)S(1)}, u32[]{:S(2)}, u32[]{:S(2)}) %collective-permute-start.17) | collective-permute-done | bytes 524320 | tf_op jit(solution)/shard_map/ppermute | solution.py:397
  262.8 13.3 %all-gather.5.cloned.1.call-done.grads0_ref.grads1_ref.grads2_ref.grads3_ref = bf16[2048,2176]{1,0:T(8,128)(2,1)} async-done(((bf16[128,2176]{1,0:T(8,128)(2,1)}), bf16[2048,2176]{1,0:T(8,128)(2,1)}) %all-gather.5.cloned.1.call-update) | async-done | bytes 8912912 | tf_op jit(solution)/shard_map/all_gather | solution.py:849
  279.6 20.4 %expert_rows.4 = (bf16[256,2048]{1,0:T(8,128)(2,1)S(1)}, bf16[256,2048]{1,0:T(8,128)(2,1)S(1)}, bf16[2048,1024]{1,0:T(8,128)(2,1)}, bf16[2048,2048]{1,0:T(8,128)...) custom-call(s32[4]{0:T(128)S(1)} %get-tuple-element.492.blocks_ref, ...), custom_call_target="tpu_custom_call" | custom-call | flops 1024 | bytes 1024 | tf_op jit(solution)/shard_map/expert_rows/pallas_call | solution.py:586
  305.0 21.3 %expert_rows.5 = (bf16[256,2048]{1,0:T(8,128)(2,1)S(1)}, bf16[256,2048]{1,0:T(8,128)(2,1)S(1)}, bf16[2048,1024]{1,0:T(8,128)(2,1)}, bf16[2048,2048]{1,0:T(8,128)...) custom-call(s32[4]{0:T(128)S(1)} %get-tuple-element.491.blocks_ref, ...), custom_call_target="tpu_custom_call", output_to_operand_aliasing={{2}: (15, {}), {3}: (16, {}), {5}: (17, {}), {6}: (18, {})} | custom-call | flops 1024 | bytes 1024 | tf_op jit(solution)/shard_map/expert_rows/pallas_call | solution.py:586
  327.4 6.8 collective-permute-done.27
  336.8 20.5 %expert_rows.6 = (bf16[256,2048]{1,0:T(8,128)(2,1)S(1)}, bf16[256,2048]{1,0:T(8,128)(2,1)S(1)}, bf16[2048,1024]{1,0:T(8,128)(2,1)}, bf16[2048,2048]{1,0:T(8,128)...) custom-call(s32[4]{0:T(128)S(1)} %get-tuple-element.490.blocks_ref, ...), custom_call_target="tpu_custom_call", output_to_operand_aliasing={{2}: (15, {}), {3}: (16, {}), {5}: (17, {}), {6}: (18, {})} | custom-call | flops 1024 | bytes 1024 | tf_op jit(solution)/shard_map/expert_rows/pallas_call | solution.py:586
  357.4 7.8 %collective-permute-done.29 = bf16[256,2048]{1,0:T(8,128)(2,1)S(1)} collective-permute-done((bf16[256,2048]{1,0:T(8,128)(2,1)S(1)}, bf16[256,2048]{1,0:T(8,128)(2,1)S(1)}, u32[]{:S(2)}, u32[]{:S(2)}) %collective-permute-start.29) | collective-permute-done | bytes 1048608 | tf_op jit(solution)/shard_map/ppermute | solution.py:397
  370.7 20.6 %expert_rows.7 = (bf16[256,2048]{1,0:T(8,128)(2,1)S(1)}, bf16[256,2048]{1,0:T(8,128)(2,1)S(1)}, bf16[2048,1024]{1,0:T(8,128)(2,1)}, bf16[2048,2048]{1,0:T(8,128)...) custom-call(s32[4]{0:T(128)S(1)} %get-tuple-element.450.blocks_ref, ...), custom_call_target="tpu_custom_call", output_to_operand_aliasing={{2}: (15, {}), {3}: (16, {}), {5}: (17, {}), {6}: (18, {})} | custom-call | flops 1024 | bytes 1024 | tf_op jit(solution)/shard_map/expert_rows/pallas_call | solution.py:586
  401.0 9.7 %collective-permute-done.36 = f32[4,16,256]{2,1,0:T(8,128)S(1)} collective-permute-done((f32[4,16,256]{2,1,0:T(8,128)S(1)}, f32[4,16,256]{2,1,0:T(8,128)S(1)}, u32[]{:S(2)}, u32[]{:S(2)}) %collective-permute-start.36) | collective-permute-done | bytes 65568 | tf_op jit(solution)/shard_map/ppermute | solution.py:397
  413.8 10.7 %convolution_convert_fusion.1 = bf16[2048,2048]{1,0:T(8,128)(2,1)S(1)} fusion(bf16[2048,1024]{1,0:T(8,128)(2,1)S(1)} %copy-done.35, bf16[1024,2048]{1,0:T(8,128)(2,1)} %pad_maximum_fusion.1), kind=kOutput, calls=%fused_computation.1 | convolution fusion | flops 8594128896 | bytes 16777216 | tf_op jit(solution)/shard_map/dot_general | solution.py:1015
  424.5 10.8 %collective-permute-done.38 = bf16[128,2048]{1,0:T(8,128)(2,1)S(1)} collective-permute-done((bf16[128,2048]{1,0:T(8,128)(2,1)S(1)}, bf16[128,2048]{1,0:T(8,128)(2,1)S(1)}, u32[]{:S(2)}, u32[]{:S(2)}) %collective-permute-start.38) | collective-permute-done | bytes 524320 | tf_op jit(solution)/shard_map/ppermute | solution.py:397
  496.0 10.4 %attend_back.1 = (f32[512,512]{1,0:T(8,128)S(1)}, f32[512,512]{1,0:T(8,128)S(1)}, bf16[512,512]{1,0:T(8,128)(2,1)S(1)}, f32[512,2]{1,0:T(8,128)S(1)}, f32[2,512]{1,0:T(2,128)S(1)}) custom-call(bf16[512,2048]{1,0:T(8,128)(2,1)S(1)} %bitcast.119, bf16[2048,512]{1,0:T(8,128)(2,1)} %constant_dynamic-update-slice_fusion.8.out_ref, ...), custom_call_target="tpu_custom_call" | custom-call | flops 1024 | bytes 1024 | tf_op jit(solution)/shard_map/attend_back/pallas_call | solution.py:1072
  530.3 6.9 pad_maximum_fusion
  540.0 10.7 %fusion.7 = f32[512,2048]{1,0:T(8,128)} fusion(bf16[2048,2048]{1,0:T(8,128)(2,1)} %get-tuple-element.365, bf16[2048,1024]{1,0:T(8,128)(2,1)S(1)} %copy-done.36), kind=kOutput, calls=%fused_computation.26 | convolution fusion | flops 4294967296 | bytes 14680064 | tf_op jit(solution)/shard_map/dot_general | solution.py:417
  603.7 7.3 %fusion.4 = f32[1,2048,256]{2,1,0:T(8,128)S(1)} fusion(f32[2048,256]{1,0:T(8,128)} %collective-permute-done.59, bf16[2048,2048]{1,0:T(8,128)(2,1)} %get-tuple-element.302, bf16[2048,2048]{1,0:T(8,128)(2,1)} %get-tuple-element.388), kind=kOutput, calls=%fused_computation.17 | convolution fusion | flops 2148007936 | bytes 13631488 | tf_op jit(solution)/shard_map/dot_general | solution.py:417
  618.6 7.8 %convolution_add_fusion = f32[512,2048]{1,0:T(8,128)} fusion(f32[512,2048]{1,0:T(8,128)} %collective-permute-done.60, bf16[2048,2048]{1,0:T(8,128)(2,1)S(1)} %bitcast.126, bf16[2048,1024]{1,0:T(8,128)(2,1)S(1)} %copy-done.37), kind=kOutput, calls=%fused_computation.13 | convolution fusion | flops 4296015872 | bytes 18874368 | tf_op jit(solution)/shard_map/dot_general | solution.py:417
  628.7 80.2 %reduce-scatter.3.cloned.1.call-done = bf16[256,1664]{0,1:T(8,128)(2,1)} async-done(((bf16[2048,1664]{0,1:T(8,128)(2,1)}), bf16[256,1664]{0,1:T(8,128)(2,1)}) %reduce-scatter.3.cloned.1.call-update) | async-done | bytes 851984 | tf_op jit(solution)/shard_map/reduce_scatter | solution.py:1111
  (439 shorter events, 295.8 us)
Async XLA Ops:
  7.2 124.2 %all-gather.3.cloned.1.call-start = ((), (), s32[]{:S(2)}) async-start(), calls=%async_computation.2 | async-start | bytes 7667712 | tf_op jit(solution)/shard_map/all_gather | solution.py:824
  16.5 259.5 %all-gather.5.cloned.1.call-start = ((), (), s32[]{:S(2)}) async-start(), calls=%async_computation.3 | async-start | bytes 9469952 | tf_op jit(solution)/shard_map/all_gather | solution.py:849
  31.5 31.3 %collective-permute-start.4 = (bf16[2,128,2048]{2,1,0:T(8,128)(2,1)}, bf16[2,128,2048]{2,1,0:T(8,128)(2,1)S(1)}, u32[]{:S(2)}, u32[]{:S(2)}) collective-permute-start(bf16[2,128,2048]{2,1,0:T(8,128)(2,1)} %pad_maximum_fusion.6), channel_id=1, source_target_pairs={{0,1},{1,0},{2,3},{3,2},{4,5},{5,4},{6,7},{7,6},{8,9},{9,8},{10,11... | collective-permute-start | bytes 3145736 | tf_op jit(solution)/shard_map/ppermute | solution.py:397
  131.4 455.5 %reduce-scatter.5.cloned.1.call-start = ((), (), s32[]{:S(2)}) async-start(), calls=%async_computation.5 | async-start | bytes 2359296 | tf_op jit(solution)/shard_map/reduce_scatter | solution.py:1066
  189.8 66.6 %collective-permute-start.22 = (bf16[2,2048,256]{2,1,0:T(8,128)(2,1)}, bf16[2,2048,256]{2,1,0:T(8,128)(2,1)}, u32[]{:S(2)}, u32[]{:S(2)}) collective-permute-start(bf16[2,2048,256]{2,1,0:T(8,128)(2,1)} %refs_0_.7), channel_id=1, source_target_pairs={{0,1},{1,0},{2,3},{3,2},{4,5},{5,4},{6,7},{7,6},{8,9},{9,8},{10,11... | collective-permute-start | bytes 6291464 | tf_op jit(solution)/shard_map/ppermute | solution.py:397
  204.7 36.2 %collective-permute-start.16 = (bf16[128,2048]{1,0:T(8,128)(2,1)S(1)}, bf16[128,2048]{1,0:T(8,128)(2,1)S(1)}, u32[]{:S(2)}, u32[]{:S(2)}) collective-permute-start(bf16[128,2048]{1,0:T(8,128)(2,1)S(1)} %collective-permute-done.14), channel_id=1, source_target_pairs={{0,8},{1,9},{2,10},{3,11},{4,12},{5,13},{6,14},{7,15},{8,16},{9,17... | collective-permute-start | bytes 1572872 | tf_op jit(solution)/shard_map/ppermute | solution.py:397
  207.8 44.5 %collective-permute-start.18 = (bf16[256,2048]{1,0:T(8,128)(2,1)S(1)}, bf16[256,2048]{1,0:T(8,128)(2,1)S(1)}, u32[]{:S(2)}, u32[]{:S(2)}) collective-permute-start(bf16[256,2048]{1,0:T(8,128)(2,1)S(1)} %pad_maximum_fusion.7.near_ref), channel_id=1, source_target_pairs={{0,2},{1,5},{2,0},{3,7},{4,6},{5,1},{6,4},{7,3},{8,10},{9,13},{10,... | collective-permute-start | bytes 3145736 | tf_op jit(solution)/shard_map/ppermute | solution.py:397
  208.9 53.9 %collective-permute-start.23 = (bf16[2,2048,256]{2,1,0:T(8,128)(2,1)}, bf16[2,2048,256]{2,1,0:T(8,128)(2,1)}, u32[]{:S(2)}, u32[]{:S(2)}) collective-permute-start(bf16[2,2048,256]{2,1,0:T(8,128)(2,1)} %refs_1_.7), channel_id=1, source_target_pairs={{0,1},{1,0},{2,3},{3,2},{4,5},{5,4},{6,7},{7,6},{8,9},{9,8},{10,11... | collective-permute-start | bytes 6291464 | tf_op jit(solution)/shard_map/ppermute | solution.py:397
  212.0 50.8 %collective-permute-start.24 = (bf16[2,256,2048]{2,1,0:T(8,128)(2,1)}, bf16[2,256,2048]{2,1,0:T(8,128)(2,1)}, u32[]{:S(2)}, u32[]{:S(2)}) collective-permute-start(bf16[2,256,2048]{2,1,0:T(8,128)(2,1)} %refs_2_.7), channel_id=1, source_target_pairs={{0,1},{1,0},{2,3},{3,2},{4,5},{5,4},{6,7},{7,6},{8,9},{9,8},{10,11... | collective-permute-start | bytes 6291464 | tf_op jit(solution)/shard_map/ppermute | solution.py:397
  254.1 45.9 %collective-permute-start.21 = (bf16[256,2048]{1,0:T(8,128)(2,1)}, bf16[256,2048]{1,0:T(8,128)(2,1)}, u32[]{:S(2)}, u32[]{:S(2)}) collective-permute-start(bf16[256,2048]{1,0:T(8,128)(2,1)} %constant_dynamic-update-slice_fusion.near_ref), channel_id=1, source_target_pairs={{0,2},{1,5},{2,0},{3,7},{4,6},{5,1},{6,4},{7,3},{8,10},{9,13},{10,... | collective-permute-start | bytes 3145736 | tf_op jit(solution)/shard_map/ppermute | solution.py:397
  255.0 45.0 %collective-permute-start.19 = (bf16[128,2048]{1,0:T(8,128)(2,1)}, bf16[128,2048]{1,0:T(8,128)(2,1)}, u32[]{:S(2)}, u32[]{:S(2)}) collective-permute-start(bf16[128,2048]{1,0:T(8,128)(2,1)} %copy-done.65), channel_id=1, source_target_pairs={{0,8},{1,9},{2,10},{3,11},{4,12},{5,13},{6,14},{7,15},{8,16},{9,17... | collective-permute-start | bytes 1572872 | tf_op jit(solution)/shard_map/ppermute | solution.py:397
  256.4 43.7 %collective-permute-start.20 = (bf16[128,2048]{1,0:T(8,128)(2,1)}, bf16[128,2048]{1,0:T(8,128)(2,1)}, u32[]{:S(2)}, u32[]{:S(2)}) collective-permute-start(bf16[128,2048]{1,0:T(8,128)(2,1)} %copy-done.65), channel_id=1, source_target_pairs={{0,4},{1,3},{2,6},{3,1},{4,0},{5,7},{6,2},{7,5},{8,12},{9,11},{10,... | collective-permute-start | bytes 1572872 | tf_op jit(solution)/shard_map/ppermute | solution.py:397
  304.9 29.3 %collective-permute-start.27 = (bf16[256,2048]{1,0:T(8,128)(2,1)S(1)}, bf16[256,2048]{1,0:T(8,128)(2,1)S(1)}, u32[]{:S(2)}, u32[]{:S(2)}) collective-permute-start(bf16[256,2048]{1,0:T(8,128)(2,1)S(1)} %get-tuple-element.233), channel_id=1, source_target_pairs={{0,2},{1,5},{2,0},{3,7},{4,6},{5,1},{6,4},{7,3},{8,10},{9,13},{10,... | collective-permute-start | bytes 3145736 | tf_op jit(solution)/shard_map/ppermute | solution.py:397
  335.8 29.3 %collective-permute-start.29 = (bf16[256,2048]{1,0:T(8,128)(2,1)S(1)}, bf16[256,2048]{1,0:T(8,128)(2,1)S(1)}, u32[]{:S(2)}, u32[]{:S(2)}) collective-permute-start(bf16[256,2048]{1,0:T(8,128)(2,1)S(1)} %get-tuple-element.248), channel_id=1, source_target_pairs={{0,2},{1,5},{2,0},{3,7},{4,6},{5,1},{6,4},{7,3},{8,10},{9,13},{10,... | collective-permute-start | bytes 3145736 | tf_op jit(solution)/shard_map/ppermute | solution.py:397
  477.4 31.0 %collective-permute-start.47 = (bf16[256,2048]{1,0:T(8,128)(2,1)}, bf16[256,2048]{1,0:T(8,128)(2,1)}, u32[]{:S(2)}, u32[]{:S(2)}) collective-permute-start(bf16[256,2048]{1,0:T(8,128)(2,1)} %get-tuple-element.326), channel_id=1, source_target_pairs={{0,2},{1,5},{2,0},{3,7},{4,6},{5,1},{6,4},{7,3},{8,10},{9,13},{10,... | collective-permute-start | bytes 3145736 | tf_op jit(solution)/shard_map/ppermute | solution.py:397
  478.7 29.7 %collective-permute-start.48 = (bf16[256,2048]{1,0:T(8,128)(2,1)}, bf16[256,2048]{1,0:T(8,128)(2,1)}, u32[]{:S(2)}, u32[]{:S(2)}) collective-permute-start(bf16[256,2048]{1,0:T(8,128)(2,1)} %get-tuple-element.327), channel_id=1, source_target_pairs={{0,2},{1,5},{2,0},{3,7},{4,6},{5,1},{6,4},{7,3},{8,10},{9,13},{10,... | collective-permute-start | bytes 3145736 | tf_op jit(solution)/shard_map/ppermute | solution.py:397
  484.0 224.9 %reduce-scatter.3.cloned.1.call-start = ((), (), s32[]{:S(2)}) async-start(), calls=%async_computation.4 | async-start | bytes 7667712 | tf_op jit(solution)/shard_map/reduce_scatter | solution.py:1111
  485.5 72.9 %collective-permute-start.51 = (f32[2048,256]{1,0:T(8,128)}, f32[2048,256]{1,0:T(8,128)}, u32[]{:S(2)}, u32[]{:S(2)}) collective-permute-start(f32[2048,256]{1,0:T(8,128)} %fusion.29), channel_id=1, source_target_pairs={{0,1},{1,0},{2,3},{3,2},{4,5},{5,4},{6,7},{7,6},{8,9},{9,8},{10,11... | collective-permute-start | bytes 6291464 | tf_op jit(solution)/shard_map/ppermute | solution.py:397
  486.5 71.9 %collective-permute-start.52 = (f32[2048,256]{1,0:T(8,128)}, f32[2048,256]{1,0:T(8,128)}, u32[]{:S(2)}, u32[]{:S(2)}) collective-permute-start(f32[2048,256]{1,0:T(8,128)} %fusion.27), channel_id=1, source_target_pairs={{0,1},{1,0},{2,3},{3,2},{4,5},{5,4},{6,7},{7,6},{8,9},{9,8},{10,11... | collective-permute-start | bytes 6291464 | tf_op jit(solution)/shard_map/ppermute | solution.py:397
  558.4 33.1 %collective-permute-start.60 = (f32[512,2048]{1,0:T(8,128)}, f32[512,2048]{1,0:T(8,128)}, u32[]{:S(2)}, u32[]{:S(2)}) collective-permute-start(f32[512,2048]{1,0:T(8,128)} %fusion.7), channel_id=1, source_target_pairs={{0,1},{1,0},{2,3},{3,2},{4,5},{5,4},{6,7},{7,6},{8,9},{9,8},{10,11... | collective-permute-start | bytes 12582920 | tf_op jit(solution)/shard_map/ppermute | solution.py:397
  563.5 28.0 %collective-permute-start.58 = (f32[2048,256]{1,0:T(8,128)}, f32[2048,256]{1,0:T(8,128)}, u32[]{:S(2)}, u32[]{:S(2)}) collective-permute-start(f32[2048,256]{1,0:T(8,128)} %fusion.25), channel_id=1, source_target_pairs={{0,1},{1,0},{2,3},{3,2},{4,5},{5,4},{6,7},{7,6},{8,9},{9,8},{10,11... | collective-permute-start | bytes 6291464 | tf_op jit(solution)/shard_map/ppermute | solution.py:397
  594.0 117.8 %collective-permute-start.61 = (bf16[128,2048]{1,0:T(8,128)(2,1)}, bf16[128,2048]{1,0:T(8,128)(2,1)}, u32[]{:S(2)}, u32[]{:S(2)}) collective-permute-start(bf16[128,2048]{1,0:T(8,128)(2,1)} %add_convert_fusion.3), channel_id=1, source_target_pairs={{0,24},{1,25},{2,26},{3,27},{4,28},{5,29},{6,30},{7,31},{8,0},{9,1... | collective-permute-start | bytes 1572872 | tf_op jit(solution)/shard_map/ppermute | solution.py:397
  598.2 114.1 %collective-permute-start.62 = (bf16[128,2048]{1,0:T(8,128)(2,1)}, bf16[128,2048]{1,0:T(8,128)(2,1)}, u32[]{:S(2)}, u32[]{:S(2)}) collective-permute-start(bf16[128,2048]{1,0:T(8,128)(2,1)} %add_convert_fusion.2), channel_id=1, source_target_pairs={{0,16},{1,17},{2,18},{3,19},{4,20},{5,21},{6,22},{7,23},{8,24},{9,... | collective-permute-start | bytes 1572872 | tf_op jit(solution)/shard_map/ppermute | solution.py:397
  600.5 111.8 %collective-permute-start.63 = (bf16[128,2048]{1,0:T(8,128)(2,1)}, bf16[128,2048]{1,0:T(8,128)(2,1)}, u32[]{:S(2)}, u32[]{:S(2)}) collective-permute-start(bf16[128,2048]{1,0:T(8,128)(2,1)} %add_convert_fusion.1), channel_id=1, source_target_pairs={{0,8},{1,9},{2,10},{3,11},{4,12},{5,13},{6,14},{7,15},{8,16},{9,17... | collective-permute-start | bytes 1572872 | tf_op jit(solution)/shard_map/ppermute | solution.py:397
  (129 other events, 1542.3 us)
Sparse Core Ops, SparseCore 0:
  16.7 114.6 all-gather.2
  134.3 141.7 all-gather.4
  484.1 66.1 reduce-scatter.4
  553.9 154.9 reduce-scatter.2

commit v6 on v4

--- a/solution.py
+++ b/solution.py
@@ -843,11 +843,15 @@
     rows_x = four_rows(mine, theirs).astype(jnp.float32)
     scale1 = lax.rsqrt(jnp.mean(rows_x * rows_x, axis=-1, keepdims=True) + EPSILON)
     own_weights = (w_gate, w_up, w_down)
-    grads_own, weights_own, weights_full, scale1, rows_x, out_full = fence(
-        grads_own, own_weights, weights_full, scale1, rows_x, out_full
+    weights_own, out_full, _ = fence(own_weights, out_full, theirs)
+    other_weights = tuple(send(weight, SWAP_CORE) for weight in weights_own)
+    down_rows = jnp.concatenate(
+        [weights[2].reshape(-1, width) for weights in (own_weights, other_weights)]
+    )
+    grads_own, other_weights, down_rows, weights_full, scale1, rows_x, out_full = fence(
+        grads_own, other_weights, down_rows, weights_full, scale1, rows_x, out_full
     )
     all_grads_abs = lax.all_gather(grads_own, FINE[:3], axis=0, tiled=True)
-    other_weights = tuple(send(weight, SWAP_CORE) for weight in weights_own)
     qkv_full = weights_full[:, : 3 * head_cols]
     router_wide = weights_full[:, 3 * head_cols :]
     router_full = router_wide[:, :n_experts]
@@ -984,17 +988,13 @@
     dots = jnp.stack([result[4] for result in results])
     part = dots.shape[-1] // 4
     all_active, all_hidden, all_grads, all_rows = (results[-1][index] for index in (2, 3, 5, 6))
-    down_rows = jnp.concatenate(
-        [weights[2].reshape(-1, width) for weights in (own_weights, other_weights)]
-    )
-    back, first, home, dots_back, dots, all_active, down_rows, all_hidden = fence(
+    back, first, home, dots_back, dots, all_active, all_hidden = fence(
         send(results[3][1], SWAP_SECOND),
         route_first(2),
         route_home(1),
         send(dots[..., 2 * part :], SWAP_SECOND),
         dots,
         all_active,
-        down_rows,
         all_hidden,
     )
     seconds.append(back)

time: 725 us -> 726 us (level)
  starting transfers between devices: 71.5 us -> 82.8 us
    all_gather x1, waiting for transfers between devices: 65.4 us -> 54 us  [dense_shards(): weights_full = lax.all_gather(weights_own, fsdp, axis=0, tiled=True)]
    ppermute x67, starting transfers between devices: 71.1 us -> 82.3 us  [send(): return lax.ppermute(values, FINE, pairs)]
    all_gather x1, waiting for transfers between devices: 13.8 us -> 21.5 us  [dense_shards(): all_grads_abs = lax.all_gather(grads_own, FINE[:3], axis=0, tiled=True)]
    unnamed x175 -> x181, local copies, waits for them, and re-layouts: 30.6 us -> 32.7 us
  transfers between devices with their start and end apart: 71 -> 71, of which waited for: 26 -> 27; matrix products, arithmetic and copies ran while one was open for 26% -> 26% of each run, Pallas kernels for 14% -> 13%
where the time goes in v6:
time: 726 us; the launch traced here: 715 us
  waiting for transfers between devices  291 us (40%)
  matrix products  101 us (14%)
  Pallas kernels  92.9 us (13%)
  starting transfers between devices  82.8 us (11%)
  local copies, waits for them, and re-layouts  64.9 us (9%)
  other arithmetic  55.5 us (8%)
  between operations  15.6 us (2%)
  blocking collectives  12.1 us (2%)
    ppermute x67, waiting for transfers between devices, send(): return lax.ppermute(values, FINE, pairs)  151 us
    ppermute x67, starting transfers between devices, send(): return lax.ppermute(values, FINE, pairs)  82.3 us
    pallas_call x4, Pallas kernels, expert_rows(): pl.pallas_call(functools.partial(expert_kernel, n_experts=n_experts, at=a...  77.1 us
    dot_general x13, matrix products, pair_dots(): lax.dot_general(left, right, (((0,), (0,)), ((), ())), preferred_element_...  69.9 us
    reduce_scatter x1, waiting for transfers between devices, dense_shards(): lax.psum_scatter(grad_full, fsdp, scatter_dimension=0, tiled=True)  64.5 us
    all_gather x1, waiting for transfers between devices, dense_shards(): weights_full = lax.all_gather(weights_own, fsdp, axis=0, tiled=True)  54 us
    unnamed x181, local copies, waits for them, and re-layouts  32.7 us
    all_gather x1, waiting for transfers between devices, dense_shards(): all_grads_abs = lax.all_gather(grads_own, FINE[:3], axis=0, tiled=True)  21.5 us
  transfers between devices with their start and end apart: 71, of which 27 were waited for; matrix products, arithmetic and copies ran while one was open for 26% of the time, Pallas kernels for 13%

profile of v6, /device:TPU:9, one launch (start us, length us, event | category | flops | bytes accessed | tf_op | source)
XLA Modules:
  0.0 715.5 jit_solution(15570690628426785589)
XLA Ops:
  49.2 6.8 collective-permute-done.8
  77.4 54.0 %all-gather.3.cloned.1.call-done = bf16[2048,1664]{0,1:T(8,128)(2,1)} async-done(((bf16[256,1664]{0,1:T(8,128)(2,1)}), bf16[2048,1664]{0,1:T(8,128)(2,1)}) %all-gather.3.cloned.1.call-update) | async-done | bytes 6815760 | tf_op jit(solution)/shard_map/all_gather | solution.py:824
  135.1 6.9 fusion.2.projected_ref
  172.6 13.4 %collective-permute-done.16 = bf16[128,2048]{1,0:T(8,128)(2,1)S(1)} collective-permute-done((bf16[128,2048]{1,0:T(8,128)(2,1)S(1)}, bf16[128,2048]{1,0:T(8,128)(2,1)S(1)}, u32[]{:S(2)}, u32[]{:S(2)}) %collective-permute-start.16) | collective-permute-done | bytes 524320 | tf_op jit(solution)/shard_map/ppermute | solution.py:397
  189.4 15.1 %collective-permute-done.17 = bf16[128,2048]{1,0:T(8,128)(2,1)S(1)} collective-permute-done((bf16[128,2048]{1,0:T(8,128)(2,1)S(1)}, bf16[128,2048]{1,0:T(8,128)(2,1)S(1)}, u32[]{:S(2)}, u32[]{:S(2)}) %collective-permute-start.17) | collective-permute-done | bytes 524320 | tf_op jit(solution)/shard_map/ppermute | solution.py:397
  210.7 27.8 %collective-permute-done.19 = bf16[128,2048]{1,0:T(8,128)(2,1)S(1)} collective-permute-done((bf16[128,2048]{1,0:T(8,128)(2,1)S(1)}, bf16[128,2048]{1,0:T(8,128)(2,1)S(1)}, u32[]{:S(2)}, u32[]{:S(2)}) %collective-permute-start.19) | collective-permute-done | bytes 524320 | tf_op jit(solution)/shard_map/ppermute | solution.py:397
  238.5 8.3 %collective-permute-done.21.far_ref = bf16[256,2048]{1,0:T(8,128)(2,1)S(1)} collective-permute-done((bf16[256,2048]{1,0:T(8,128)(2,1)S(1)}, bf16[256,2048]{1,0:T(8,128)(2,1)S(1)}, u32[]{:S(2)}, u32[]{:S(2)}) %collective-permute-start.21) | collective-permute-done | bytes 1048608 | tf_op jit(solution)/shard_map/ppermute | solution.py:397
  258.8 21.5 %all-gather.5.cloned.1.call-done.grads0_ref.grads1_ref.grads2_ref.grads3_ref = bf16[2048,2176]{1,0:T(8,128)(2,1)} async-done(((bf16[128,2176]{1,0:T(8,128)(2,1)}), bf16[2048,2176]{1,0:T(8,128)(2,1)}) %all-gather.5.cloned.1.call-update) | async-done | bytes 8912912 | tf_op jit(solution)/shard_map/all_gather | solution.py:854
  285.4 19.4 %expert_rows.4 = (bf16[256,2048]{1,0:T(8,128)(2,1)S(1)}, bf16[256,2048]{1,0:T(8,128)(2,1)S(1)}, bf16[2048,1024]{1,0:T(8,128)(2,1)}, bf16[2048,2048]{1,0:T(8,128)...) custom-call(s32[4]{0:T(128)S(1)} %get-tuple-element.510.blocks_ref, ...), custom_call_target="tpu_custom_call" | custom-call | flops 1024 | bytes 1024 | tf_op jit(solution)/shard_map/expert_rows/pallas_call | solution.py:586
  308.9 19.6 %expert_rows.5 = (bf16[256,2048]{1,0:T(8,128)(2,1)S(1)}, bf16[256,2048]{1,0:T(8,128)(2,1)S(1)}, bf16[2048,1024]{1,0:T(8,128)(2,1)}, bf16[2048,2048]{1,0:T(8,128)...) custom-call(s32[4]{0:T(128)S(1)} %get-tuple-element.509.blocks_ref, ...), custom_call_target="tpu_custom_call", output_to_operand_aliasing={{2}: (15, {}), {3}: (16, {}), {5}: (17, {}), {6}: (18, {})} | custom-call | flops 1024 | bytes 1024 | tf_op jit(solution)/shard_map/expert_rows/pallas_call | solution.py:586
  329.6 7.2 collective-permute-done.27
  340.2 19.0 %expert_rows.6 = (bf16[256,2048]{1,0:T(8,128)(2,1)S(1)}, bf16[256,2048]{1,0:T(8,128)(2,1)S(1)}, bf16[2048,1024]{1,0:T(8,128)(2,1)}, bf16[2048,2048]{1,0:T(8,128)...) custom-call(s32[4]{0:T(128)S(1)} %get-tuple-element.508.blocks_ref, ...), custom_call_target="tpu_custom_call", output_to_operand_aliasing={{2}: (15, {}), {3}: (16, {}), {5}: (17, {}), {6}: (18, {})} | custom-call | flops 1024 | bytes 1024 | tf_op jit(solution)/shard_map/expert_rows/pallas_call | solution.py:586
  359.3 8.4 %collective-permute-done.29 = bf16[256,2048]{1,0:T(8,128)(2,1)S(1)} collective-permute-done((bf16[256,2048]{1,0:T(8,128)(2,1)S(1)}, bf16[256,2048]{1,0:T(8,128)(2,1)S(1)}, u32[]{:S(2)}, u32[]{:S(2)}) %collective-permute-start.29) | collective-permute-done | bytes 1048608 | tf_op jit(solution)/shard_map/ppermute | solution.py:397
  371.4 19.0 %expert_rows.7 = (bf16[256,2048]{1,0:T(8,128)(2,1)S(1)}, bf16[256,2048]{1,0:T(8,128)(2,1)S(1)}, bf16[2048,1024]{1,0:T(8,128)(2,1)}, bf16[2048,2048]{1,0:T(8,128)...) custom-call(s32[4]{0:T(128)S(1)} %get-tuple-element.468.blocks_ref, ...), custom_call_target="tpu_custom_call", output_to_operand_aliasing={{2}: (15, {}), {3}: (16, {}), {5}: (17, {}), {6}: (18, {})} | custom-call | flops 1024 | bytes 1024 | tf_op jit(solution)/shard_map/expert_rows/pallas_call | solution.py:586
  399.4 7.8 %collective-permute-done.36 = f32[4,16,256]{2,1,0:T(8,128)S(1)} collective-permute-done((f32[4,16,256]{2,1,0:T(8,128)S(1)}, f32[4,16,256]{2,1,0:T(8,128)S(1)}, u32[]{:S(2)}, u32[]{:S(2)}) %collective-permute-start.36) | collective-permute-done | bytes 65568 | tf_op jit(solution)/shard_map/ppermute | solution.py:397
  412.4 11.0 %convolution_convert_fusion.1 = bf16[2048,2048]{1,0:T(8,128)(2,1)} fusion(bf16[2048,1024]{1,0:T(8,128)(2,1)S(1)} %copy-done.37, bf16[1024,2048]{1,0:T(8,128)(2,1)S(1)} %copy-done.54), kind=kOutput, calls=%fused_computation.1 | convolution fusion | flops 8594128896 | bytes 16777216 | tf_op jit(solution)/shard_map/dot_general | solution.py:1015
  429.5 7.8 %collective-permute-start.41 = (f32[16,128]{1,0:T(8,128)S(1)}, f32[16,128]{1,0:T(8,128)S(1)}, u32[]{:S(2)}, u32[]{:S(2)}) collective-permute-start(f32[16,128]{1,0:T(8,128)S(1)} %get-tuple-element.503), channel_id=1, source_target_pairs={{0,24},{1,25},{2,26},{3,27},{4,28},{5,29},{6,30},{7,31},{8,0},{9,1... | collective-permute-start | bytes 24584 | tf_op jit(solution)/shard_map/ppermute | solution.py:397
  489.7 10.4 %attend_back.1 = (f32[512,512]{1,0:T(8,128)S(1)}, f32[512,512]{1,0:T(8,128)S(1)}, bf16[512,512]{1,0:T(8,128)(2,1)S(1)}, f32[512,2]{1,0:T(8,128)S(1)}, f32[2,512]{1,0:T(2,128)S(1)}) custom-call(bf16[512,2048]{1,0:T(8,128)(2,1)S(1)} %bitcast.119, bf16[2048,512]{1,0:T(8,128)(2,1)} %constant_dynamic-update-slice_fusion.8.out_ref, ...), custom_call_target="tpu_custom_call" | custom-call | flops 1024 | bytes 1024 | tf_op jit(solution)/shard_map/attend_back/pallas_call | solution.py:1071
  524.1 6.9 pad_maximum_fusion
  535.0 10.5 %fusion.7 = f32[512,2048]{1,0:T(8,128)} fusion(bf16[2048,2048]{1,0:T(8,128)(2,1)} %get-tuple-element.383, bf16[2048,1024]{1,0:T(8,128)(2,1)S(1)} %copy-done.38), kind=kOutput, calls=%fused_computation.26 | convolution fusion | flops 4294967296 | bytes 14680064 | tf_op jit(solution)/shard_map/dot_general | solution.py:417
  553.3 7.7 %collective-permute-done.50 = bf16[256,2048]{1,0:T(8,128)(2,1)S(1)} collective-permute-done((bf16[256,2048]{1,0:T(8,128)(2,1)S(1)}, bf16[256,2048]{1,0:T(8,128)(2,1)S(1)}, u32[]{:S(2)}, u32[]{:S(2)}) %collective-permute-start.50) | collective-permute-done | bytes 1048608 | tf_op jit(solution)/shard_map/ppermute | solution.py:397
  608.1 7.3 %fusion.4 = f32[1,2048,256]{2,1,0:T(8,128)S(1)} fusion(f32[2048,256]{1,0:T(8,128)} %collective-permute-done.59, bf16[2048,2048]{1,0:T(8,128)(2,1)} %get-tuple-element.315, bf16[2048,2048]{1,0:T(8,128)(2,1)} %get-tuple-element.406), kind=kOutput, calls=%fused_computation.17 | convolution fusion | flops 2148007936 | bytes 13631488 | tf_op jit(solution)/shard_map/dot_general | solution.py:417
  623.0 7.8 %convolution_add_fusion = f32[512,2048]{1,0:T(8,128)} fusion(f32[512,2048]{1,0:T(8,128)} %collective-permute-done.60, bf16[2048,2048]{1,0:T(8,128)(2,1)S(1)} %bitcast.126, bf16[2048,1024]{1,0:T(8,128)(2,1)S(1)} %copy-done.39), kind=kOutput, calls=%fused_computation.13 | convolution fusion | flops 4296015872 | bytes 18874368 | tf_op jit(solution)/shard_map/dot_general | solution.py:417
  633.1 64.5 %reduce-scatter.3.cloned.1.call-done = bf16[256,1664]{0,1:T(8,128)(2,1)} async-done(((bf16[2048,1664]{0,1:T(8,128)(2,1)}), bf16[256,1664]{0,1:T(8,128)(2,1)}) %reduce-scatter.3.cloned.1.call-update) | async-done | bytes 851984 | tf_op jit(solution)/shard_map/reduce_scatter | solution.py:1110
  (452 shorter events, 311.9 us)
Async XLA Ops:
  7.2 124.2 %all-gather.3.cloned.1.call-start = ((), (), s32[]{:S(2)}) async-start(), calls=%async_computation.2 | async-start | bytes 7667712 | tf_op jit(solution)/shard_map/all_gather | solution.py:824
  16.5 263.8 %all-gather.5.cloned.1.call-start = ((), (), s32[]{:S(2)}) async-start(), calls=%async_computation.3 | async-start | bytes 9469952 | tf_op jit(solution)/shard_map/all_gather | solution.py:854
  31.5 31.4 %collective-permute-start.11 = (bf16[2,128,2048]{2,1,0:T(8,128)(2,1)}, bf16[2,128,2048]{2,1,0:T(8,128)(2,1)}, u32[]{:S(2)}, u32[]{:S(2)}) collective-permute-start(bf16[2,128,2048]{2,1,0:T(8,128)(2,1)} %pad_maximum_fusion.6), channel_id=1, source_target_pairs={{0,1},{1,0},{2,3},{3,2},{4,5},{5,4},{6,7},{7,6},{8,9},{9,8},{10,11... | collective-permute-start | bytes 3145736 | tf_op jit(solution)/shard_map/ppermute | solution.py:397
  131.4 457.5 %reduce-scatter.5.cloned.1.call-start = ((), (), s32[]{:S(2)}) async-start(), calls=%async_computation.5 | async-start | bytes 2359296 | tf_op jit(solution)/shard_map/reduce_scatter | solution.py:1065
  204.6 42.2 %collective-permute-start.21 = (bf16[256,2048]{1,0:T(8,128)(2,1)S(1)}, bf16[256,2048]{1,0:T(8,128)(2,1)S(1)}, u32[]{:S(2)}, u32[]{:S(2)}) collective-permute-start(bf16[256,2048]{1,0:T(8,128)(2,1)S(1)} %pad_maximum_fusion.7.near_ref), channel_id=1, source_target_pairs={{0,2},{1,5},{2,0},{3,7},{4,6},{5,1},{6,4},{7,3},{8,10},{9,13},{10,... | collective-permute-start | bytes 3145736 | tf_op jit(solution)/shard_map/ppermute | solution.py:397
  205.7 32.8 %collective-permute-start.19 = (bf16[128,2048]{1,0:T(8,128)(2,1)S(1)}, bf16[128,2048]{1,0:T(8,128)(2,1)S(1)}, u32[]{:S(2)}, u32[]{:S(2)}) collective-permute-start(bf16[128,2048]{1,0:T(8,128)(2,1)S(1)} %collective-permute-done.17), channel_id=1, source_target_pairs={{0,8},{1,9},{2,10},{3,11},{4,12},{5,13},{6,14},{7,15},{8,16},{9,17... | collective-permute-start | bytes 1572872 | tf_op jit(solution)/shard_map/ppermute | solution.py:397
  208.6 29.9 %collective-permute-start.20 = (bf16[128,2048]{1,0:T(8,128)(2,1)S(1)}, bf16[128,2048]{1,0:T(8,128)(2,1)S(1)}, u32[]{:S(2)}, u32[]{:S(2)}) collective-permute-start(bf16[128,2048]{1,0:T(8,128)(2,1)S(1)} %collective-permute-done.17), channel_id=1, source_target_pairs={{0,4},{1,3},{2,6},{3,1},{4,0},{5,7},{6,2},{7,5},{8,12},{9,11},{10,... | collective-permute-start | bytes 1572872 | tf_op jit(solution)/shard_map/ppermute | solution.py:397
  248.6 56.2 %collective-permute-start.24 = (bf16[256,2048]{1,0:T(8,128)(2,1)}, bf16[256,2048]{1,0:T(8,128)(2,1)}, u32[]{:S(2)}, u32[]{:S(2)}) collective-permute-start(bf16[256,2048]{1,0:T(8,128)(2,1)} %constant_dynamic-update-slice_fusion.near_ref), channel_id=1, source_target_pairs={{0,2},{1,5},{2,0},{3,7},{4,6},{5,1},{6,4},{7,3},{8,10},{9,13},{10,... | collective-permute-start | bytes 3145736 | tf_op jit(solution)/shard_map/ppermute | solution.py:397
  248.7 56.1 %collective-permute-start.22 = (bf16[128,2048]{1,0:T(8,128)(2,1)}, bf16[128,2048]{1,0:T(8,128)(2,1)}, u32[]{:S(2)}, u32[]{:S(2)}) collective-permute-start(bf16[128,2048]{1,0:T(8,128)(2,1)} %copy-done.68), channel_id=1, source_target_pairs={{0,8},{1,9},{2,10},{3,11},{4,12},{5,13},{6,14},{7,15},{8,16},{9,17... | collective-permute-start | bytes 1572872 | tf_op jit(solution)/shard_map/ppermute | solution.py:397
  251.7 53.1 %collective-permute-start.23 = (bf16[128,2048]{1,0:T(8,128)(2,1)}, bf16[128,2048]{1,0:T(8,128)(2,1)}, u32[]{:S(2)}, u32[]{:S(2)}) collective-permute-start(bf16[128,2048]{1,0:T(8,128)(2,1)} %copy-done.68), channel_id=1, source_target_pairs={{0,4},{1,3},{2,6},{3,1},{4,0},{5,7},{6,2},{7,5},{8,12},{9,11},{10,... | collective-permute-start | bytes 1572872 | tf_op jit(solution)/shard_map/ppermute | solution.py:397
  307.5 29.3 %collective-permute-start.27 = (bf16[256,2048]{1,0:T(8,128)(2,1)S(1)}, bf16[256,2048]{1,0:T(8,128)(2,1)S(1)}, u32[]{:S(2)}, u32[]{:S(2)}) collective-permute-start(bf16[256,2048]{1,0:T(8,128)(2,1)S(1)} %get-tuple-element.246), channel_id=1, source_target_pairs={{0,2},{1,5},{2,0},{3,7},{4,6},{5,1},{6,4},{7,3},{8,10},{9,13},{10,... | collective-permute-start | bytes 3145736 | tf_op jit(solution)/shard_map/ppermute | solution.py:397
  338.4 29.3 %collective-permute-start.29 = (bf16[256,2048]{1,0:T(8,128)(2,1)S(1)}, bf16[256,2048]{1,0:T(8,128)(2,1)S(1)}, u32[]{:S(2)}, u32[]{:S(2)}) collective-permute-start(bf16[256,2048]{1,0:T(8,128)(2,1)S(1)} %get-tuple-element.261), channel_id=1, source_target_pairs={{0,2},{1,5},{2,0},{3,7},{4,6},{5,1},{6,4},{7,3},{8,10},{9,13},{10,... | collective-permute-start | bytes 3145736 | tf_op jit(solution)/shard_map/ppermute | solution.py:397
  470.8 31.3 %collective-permute-start.46 = (bf16[256,2048]{1,0:T(8,128)(2,1)}, bf16[256,2048]{1,0:T(8,128)(2,1)}, u32[]{:S(2)}, u32[]{:S(2)}) collective-permute-start(bf16[256,2048]{1,0:T(8,128)(2,1)} %get-tuple-element.341), channel_id=1, source_target_pairs={{0,2},{1,5},{2,0},{3,7},{4,6},{5,1},{6,4},{7,3},{8,10},{9,13},{10,... | collective-permute-start | bytes 3145736 | tf_op jit(solution)/shard_map/ppermute | solution.py:397
  472.2 29.8 %collective-permute-start.47 = (bf16[256,2048]{1,0:T(8,128)(2,1)}, bf16[256,2048]{1,0:T(8,128)(2,1)}, u32[]{:S(2)}, u32[]{:S(2)}) collective-permute-start(bf16[256,2048]{1,0:T(8,128)(2,1)} %get-tuple-element.342), channel_id=1, source_target_pairs={{0,2},{1,5},{2,0},{3,7},{4,6},{5,1},{6,4},{7,3},{8,10},{9,13},{10,... | collective-permute-start | bytes 3145736 | tf_op jit(solution)/shard_map/ppermute | solution.py:397
  477.4 220.1 %reduce-scatter.3.cloned.1.call-start = ((), (), s32[]{:S(2)}) async-start(), calls=%async_computation.4 | async-start | bytes 7667712 | tf_op jit(solution)/shard_map/reduce_scatter | solution.py:1110
  479.1 74.2 %collective-permute-start.51 = (f32[2048,256]{1,0:T(8,128)}, f32[2048,256]{1,0:T(8,128)}, u32[]{:S(2)}, u32[]{:S(2)}) collective-permute-start(f32[2048,256]{1,0:T(8,128)} %fusion.29), channel_id=1, source_target_pairs={{0,1},{1,0},{2,3},{3,2},{4,5},{5,4},{6,7},{7,6},{8,9},{9,8},{10,11... | collective-permute-start | bytes 6291464 | tf_op jit(solution)/shard_map/ppermute | solution.py:397
  480.1 73.2 %collective-permute-start.52 = (f32[2048,256]{1,0:T(8,128)}, f32[2048,256]{1,0:T(8,128)}, u32[]{:S(2)}, u32[]{:S(2)}) collective-permute-start(f32[2048,256]{1,0:T(8,128)} %fusion.27), channel_id=1, source_target_pairs={{0,1},{1,0},{2,3},{3,2},{4,5},{5,4},{6,7},{7,6},{8,9},{9,8},{10,11... | collective-permute-start | bytes 6291464 | tf_op jit(solution)/shard_map/ppermute | solution.py:397
  533.6 27.4 %collective-permute-start.50 = (bf16[256,2048]{1,0:T(8,128)(2,1)S(1)}, bf16[256,2048]{1,0:T(8,128)(2,1)S(1)}, u32[]{:S(2)}, u32[]{:S(2)}) collective-permute-start(bf16[256,2048]{1,0:T(8,128)(2,1)S(1)} %copy-done.61), channel_id=1, source_target_pairs={{0,2},{1,5},{2,0},{3,7},{4,6},{5,1},{6,4},{7,3},{8,10},{9,13},{10,... | collective-permute-start | bytes 3145736 | tf_op jit(solution)/shard_map/ppermute | solution.py:397
  561.0 32.5 %collective-permute-start.60 = (f32[512,2048]{1,0:T(8,128)}, f32[512,2048]{1,0:T(8,128)}, u32[]{:S(2)}, u32[]{:S(2)}) collective-permute-start(f32[512,2048]{1,0:T(8,128)} %fusion.7), channel_id=1, source_target_pairs={{0,1},{1,0},{2,3},{3,2},{4,5},{5,4},{6,7},{7,6},{8,9},{9,8},{10,11... | collective-permute-start | bytes 12582920 | tf_op jit(solution)/shard_map/ppermute | solution.py:397
  565.3 28.2 %collective-permute-start.58 = (f32[2048,256]{1,0:T(8,128)}, f32[2048,256]{1,0:T(8,128)}, u32[]{:S(2)}, u32[]{:S(2)}) collective-permute-start(f32[2048,256]{1,0:T(8,128)} %fusion.25), channel_id=1, source_target_pairs={{0,1},{1,0},{2,3},{3,2},{4,5},{5,4},{6,7},{7,6},{8,9},{9,8},{10,11... | collective-permute-start | bytes 6291464 | tf_op jit(solution)/shard_map/ppermute | solution.py:397
  566.0 27.5 %collective-permute-start.59 = (f32[2048,256]{1,0:T(8,128)}, f32[2048,256]{1,0:T(8,128)}, u32[]{:S(2)}, u32[]{:S(2)}) collective-permute-start(f32[2048,256]{1,0:T(8,128)} %fusion.23), channel_id=1, source_target_pairs={{0,1},{1,0},{2,3},{3,2},{4,5},{5,4},{6,7},{7,6},{8,9},{9,8},{10,11... | collective-permute-start | bytes 6291464 | tf_op jit(solution)/shard_map/ppermute | solution.py:397
  595.9 104.5 %collective-permute-start.61 = (bf16[128,2048]{1,0:T(8,128)(2,1)}, bf16[128,2048]{1,0:T(8,128)(2,1)}, u32[]{:S(2)}, u32[]{:S(2)}) collective-permute-start(bf16[128,2048]{1,0:T(8,128)(2,1)} %add_convert_fusion.3), channel_id=1, source_target_pairs={{0,24},{1,25},{2,26},{3,27},{4,28},{5,29},{6,30},{7,31},{8,0},{9,1... | collective-permute-start | bytes 1572872 | tf_op jit(solution)/shard_map/ppermute | solution.py:397
  604.5 96.5 %collective-permute-start.62 = (bf16[128,2048]{1,0:T(8,128)(2,1)}, bf16[128,2048]{1,0:T(8,128)(2,1)}, u32[]{:S(2)}, u32[]{:S(2)}) collective-permute-start(bf16[128,2048]{1,0:T(8,128)(2,1)} %add_convert_fusion.2), channel_id=1, source_target_pairs={{0,16},{1,17},{2,18},{3,19},{4,20},{5,21},{6,22},{7,23},{8,24},{9,... | collective-permute-start | bytes 1572872 | tf_op jit(solution)/shard_map/ppermute | solution.py:397
  605.5 95.4 %collective-permute-start.63 = (bf16[128,2048]{1,0:T(8,128)(2,1)}, bf16[128,2048]{1,0:T(8,128)(2,1)}, u32[]{:S(2)}, u32[]{:S(2)}) collective-permute-start(bf16[128,2048]{1,0:T(8,128)(2,1)} %add_convert_fusion.1), channel_id=1, source_target_pairs={{0,8},{1,9},{2,10},{3,11},{4,12},{5,13},{6,14},{7,15},{8,16},{9,17... | collective-permute-start | bytes 1572872 | tf_op jit(solution)/shard_map/ppermute | solution.py:397
  (135 other events, 1630.1 us)
Sparse Core Ops, SparseCore 0:
  16.7 114.6 all-gather.2
  134.3 146.0 all-gather.4
  477.5 66.0 reduce-scatter.4
  547.1 150.4 reduce-scatter.2
